TPU v7x, 32 devices: a whole 2x2x4 slice. The times are simulated.
32 devices in a mesh: dp: 2 (over core), expert: 4 (over y, x), seg: 4 (over z).
Axes of the slice: x: 2, y: 2, z: 4, core: 2. Of those that a mesh axis runs over, the one named last changes fastest.
Arguments:
- tokens: bfloat16 [512, 3072], P(('dp', 'expert'), 'seg'), parts along dimension 0, may hold values from -6 to 6
- expert_ids: int32 [512, 4], P(('dp', 'expert')), parts along dimension 0, may hold values from 0 to 15, as said below
- route_weight: float32 [512, 4], P(('dp', 'expert')), parts along dimension 0, may hold values from 0.1 to 1
- w_up: bfloat16 [16, 3072, 6144], P('expert', None, 'seg'), may hold values from -0.109375 to 0.109375
- w_down: bfloat16 [16, 6144, 3072], P('expert', 'seg'), may hold values from -0.078125 to 0.078125
Outputs:
- mixed: bfloat16 [512, 3072], P(('dp', 'expert'), 'seg'), parts along dimension 0
There are 2 independent parts, one for each index of `dp`. A program takes and returns all parts, laid end to end along the dimension named above; an argument that names none is the same for every part. Nothing has to cross between parts.
Inputs may be any that keep to these rules, and one draw needn't show every extreme that they name: `expert_ids`: each row names 4 different experts. Within each aligned block of 64 rows (the rows of one device), no expert is named by more than 21 rows, and one expert is named by exactly 21 rows in every block.
All inputs are finite; a program needn't handle non-finite values.
Results may differ from a plain program's by a relative error of at most 0.0049.
Values may be sent and summed in bfloat16 or wider, within the bound.
No kernel may reach another device: no remote copies, remote signals or barrier semaphores. Data moves between devices by JAX's collectives and lax.ppermute only.
A program may use at most 128 MiB of HBM per device.

v0:
```python
import jax
import jax.numpy as jnp
from jax import lax
from jax.sharding import PartitionSpec as P

D = 3072
EXPERTS = 16
SEND_CAP = 21


def route_slots(expert_ids):
    flat_route = expert_ids.reshape(-1)
    onehot = (flat_route[:, None] == jnp.arange(EXPERTS, dtype=jnp.int32)[None, :]).astype(
        jnp.int32
    )
    before = jnp.cumsum(onehot, axis=0) - onehot
    return flat_route * SEND_CAP + jnp.sum(before * onehot, axis=1)


def pack_rows(rows, target, topk):
    repeated = jnp.repeat(rows, topk, axis=0)
    buffer = jnp.zeros((EXPERTS * SEND_CAP, rows.shape[1]), rows.dtype)
    return buffer.at[target].set(repeated)


def shards(tokens, expert_ids, route_weight, w_up, w_down):
    expert_count = lax.axis_size("expert")
    exp_local = w_up.shape[0]
    topk = expert_ids.shape[1]
    tok_rows = tokens.shape[0]
    width_seg = tokens.shape[1]
    target = route_slots(expert_ids)
    norm_weight = route_weight / jnp.sum(route_weight, axis=1, keepdims=True)
    flat_weight = norm_weight.reshape(-1)
    packed = pack_rows(tokens, target, topk).reshape(expert_count, exp_local * SEND_CAP, width_seg)
    arrived = lax.all_to_all(packed, "expert", split_axis=0, concat_axis=0, tiled=True)
    piece = lax.all_gather(arrived, "seg", axis=2, tiled=True)
    block = piece.reshape(piece.shape[0], exp_local, SEND_CAP, piece.shape[2])
    up_sum = jnp.einsum("sekd,edf->eskf", block, w_up, preferred_element_type=jnp.float32)
    hidden = jax.nn.silu(up_sum).astype(jnp.bfloat16)
    source_count = hidden.shape[1]
    partial_out = jnp.einsum("eskf,efd->sekd", hidden, w_down, preferred_element_type=jnp.float32)
    partial_out = partial_out.reshape(source_count, exp_local * SEND_CAP, D)
    returned = lax.all_to_all(partial_out, "expert", split_axis=0, concat_axis=0, tiled=True)
    picked = returned.reshape(EXPERTS * SEND_CAP, D)[target]
    weighted = (picked * flat_weight[:, None]).reshape(tok_rows, topk, D).sum(axis=1)
    summed_tokens = lax.psum_scatter(weighted, "seg", scatter_dimension=1, tiled=True)
    return summed_tokens.astype(jnp.bfloat16)


def solution(mesh):
    placed = (
        P(("dp", "expert"), "seg"),
        P(("dp", "expert"), None),
        P(("dp", "expert"), None),
        P("expert", None, "seg"),
        P("expert", "seg", None),
    )
    return jax.shard_map(
        shards, mesh=mesh, in_specs=placed, out_specs=P(("dp", "expert"), "seg"), check_vma=False
    )
```

profile of v0, /device:TPU:0, one launch (start us, length us, event | category | flops | bytes accessed | tf_op | source)
XLA Modules:
  0.0 214.7 jit_solution(16818171967153989624)
XLA Ops:
  6.5 0.0 all-gather.2.cloned.1.call-start
  6.5 0.8 copy.17
  7.3 0.1 eq.29
  7.4 0.1 eq.25
  7.5 0.7 broadcast_multiply_fusion
  8.2 0.6 reduce-window.6
  8.8 0.2 slice_reduce_fusion
  9.0 0.1 copy.16
  9.1 0.1 mul.34
  9.2 1.0 broadcast_in_dim.5
  10.2 0.1 reshape.88
  10.3 0.1 fusion.21
  10.4 1.8 scatter_custom_fusion
  12.2 0.1 reshape.72
  12.3 14.1 %all_to_all.10 = bf16[4,84,768]{2,1,0:T(8,128)(2,1)} all-to-all(bf16[4,84,768]{2,1,0:T(8,128)(2,1)S(1)} %reshape.72), channel_id=1, replica_groups=mesh['dp'=2,'expert'=4,'seg'=4] {'expert'}, dimensions={0} | all-to-all | bytes 1032192 | tf_op jit(solution)/shard_map/all_to_all | solution.py:36
  26.4 0.0 all-gather.2.cloned.1.call-update
  26.4 46.3 %all-gather.2.cloned.1.call-done = bf16[4,84,3072]{2,1,0:T(8,128)(2,1)} async-done(((bf16[4,84,768]{2,1,0:T(8,128)(2,1)}), bf16[4,84,3072]{2,1,0:T(8,128)(2,1)}) %all-gather.2.cloned.1.call-update) | async-done | bytes 2064400 | tf_op jit(solution)/shard_map/all_gather | solution.py:37
  72.7 3.2 %copy.20 = bf16[4,84,3072]{2,0,1:T(4,128)(2,1)S(1)} copy(bf16[4,84,3072]{2,1,0:T(8,128)(2,1)} %all-gather.2.cloned.1.call-done) | data formatting | bytes 4128768 | tf_op jit(solution)/shard_map/all_gather | solution.py:37
  76.0 28.4 %fusion.4 = f32[4,4,21,3072]{3,2,0,1:T(8,128)} fusion(bf16[4,1536,3072]{2,1,0:T(8,128)(2,1)} %param.9, bf16[4,3072,1536]{2,1,0:T(8,128)(2,1)} %param.8, bf16[4,4,21,3072]{3,0,2,1:T(4,128)(2,1)S(1)} %bitcast.42), kind=kOutput, calls=%fused_computation.6 | convolution fusion | flops 6344368128 | bytes 81690624 | tf_op jit(solution)/shard_map/eskf,efd->sekd/dot_general | solution.py:42
  104.4 5.0 %copy.22 = f32[4,4,21,3072]{3,0,2,1:T(4,128)S(1)} copy(f32[4,4,21,3072]{3,2,0,1:T(8,128)} %fusion.4) | data formatting | bytes 8257536 | tf_op jit(solution)/shard_map/eskf,efd->sekd/transpose | solution.py:42
  109.4 4.4 %copy.23 = f32[4,84,3072]{2,1,0:T(8,128)} copy(f32[4,84,3072]{2,0,1:T(4,128)S(1)} %bitcast.41) | data formatting | bytes 8257536 | tf_op jit(solution)/shard_map/reshape | solution.py:43
  113.8 0.0 copy-start
  113.8 5.0 %all-to-all-start.1 = ((f32[4,84,3072]{2,1,0:T(8,128)}), f32[4,84,3072]{2,1,0:T(8,128)}, u32[]{:S(2)}, u32[]{:S(2)}) async-start(f32[4,84,3072]{2,1,0:T(8,128)} %copy.23), calls=%async_computation.1 | async-start | bytes 8650752 | tf_op jit(solution)/shard_map/all_to_all | solution.py:44
  118.8 0.3 reduce-scatter.2.cloned.1.call-start
  119.0 0.0 copy-done
  119.1 0.1 copy.24
  119.2 48.5 %all-to-all-done.1 = f32[4,84,3072]{2,1,0:T(8,128)} async-done(((f32[4,84,3072]{2,1,0:T(8,128)}), f32[4,84,3072]{2,1,0:T(8,128)}, u32[]{:S(2)}, u32[]{:S(2)}) %all-to-all-start.1) | async-done | bytes 4128800 | tf_op jit(solution)/shard_map/all_to_all | solution.py:44
  167.7 3.8 %reshape.75 = f32[336,3072]{1,0:T(8,128)} reshape(f32[4,84,3072]{2,1,0:T(8,128)} %all-to-all-done.1) | data formatting | bytes 8257536 | tf_op jit(solution)/shard_map/reshape | solution.py:45
  171.5 6.8 %gather_fusion = f32[256,3072]{1,0:T(8,128)} fusion(f32[336,3072]{1,0:T(8,128)} %reshape.75, s32[1024]{0:T(1024)S(1)} %pad_clamp_fusion), kind=kCustom, calls=%fused_computation | custom fusion | bytes 6292480 | tf_op jit(solution)/shard_map/gather | solution.py:45
  178.4 3.1 %gather.6 = f32[64,4,3072]{2,1,0:T(4,128)S(1)} reshape(f32[256,3072]{1,0:T(8,128)} %gather_fusion) | data formatting | bytes 6291456 | tf_op jit(solution)/shard_map/gather | solution.py:45
  181.5 3.1 %multiply_reduce_fusion = f32[64,3072]{1,0:T(8,128)} fusion(f32[64,4,3072]{2,1,0:T(4,128)S(1)} %gather.6, f32[64,4]{1,0:T(8,128)S(1)} %copy.24), kind=kLoop, calls=%fused_computation.7 | loop fusion | flops 1376256 | bytes 3933184 | tf_op jit(solution)/shard_map/reduce_sum | solution.py:46
  184.6 0.0 reduce-scatter.2.cloned.1.call-update
  184.6 21.7 %reduce-scatter.2.cloned.1.call-done = f32[64,768]{1,0:T(8,128)} async-done(((f32[64,3072]{1,0:T(8,128)}), f32[64,768]{1,0:T(8,128)}) %reduce-scatter.2.cloned.1.call-update) | async-done | bytes 196624 | tf_op jit(solution)/shard_map/reduce_scatter | solution.py:47
  206.3 1.6 convert_element_type.16
  (7 shorter events, 0.1 us)
Async XLA Ops:
  6.5 66.2 %all-gather.2.cloned.1.call-start = ((), (), s32[]{:S(2)}) async-start(), calls=%async_computation.3 | async-start | bytes 2703360 | tf_op jit(solution)/shard_map/all_gather | solution.py:37
  113.8 5.3 %copy-start = (f32[64,4]{0,1:T(4,128)S(1)}, f32[64,4]{0,1:T(4,128)}, u32[]{:S(2)}) copy-start(f32[64,4]{0,1:T(4,128)} %param.7) | copy-start | bytes 3076
  113.8 54.0 %all-to-all-start.1 = ((f32[4,84,3072]{2,1,0:T(8,128)}), f32[4,84,3072]{2,1,0:T(8,128)}, u32[]{:S(2)}, u32[]{:S(2)}) async-start(f32[4,84,3072]{2,1,0:T(8,128)} %copy.23), calls=%async_computation.1 | async-start | bytes 8650752 | tf_op jit(solution)/shard_map/all_to_all | solution.py:44
  118.8 87.5 %reduce-scatter.2.cloned.1.call-start = ((), (), s32[]{:S(2)}) async-start(), calls=%async_computation.4 | async-start | bytes 983040 | tf_op jit(solution)/shard_map/reduce_scatter | solution.py:47
Sparse Core Ops, SparseCore 0:
  26.6 46.1 all-gather.1
  184.8 21.4 reduce-scatter.1
where the time goes:
time: 215 us
  waiting for transfers between devices  117 us (54%)
  local copies, waits for them, and re-layouts  30.8 us (14%)
  matrix products  28.4 us (13%)
  blocking collectives  14.1 us (7%)
  between operations  13.5 us (6%)
  other arithmetic  6.14 us (3%)
  starting transfers between devices  5.27 us (2%)
    all_to_all x1, waiting for transfers between devices, shards(): lax.all_to_all(partial_out, 'expert', split_axis=0, concat_axis=0, tiled=...  48.5 us
    all_gather x1, waiting for transfers between devices, shards(): piece = lax.all_gather(arrived, 'seg', axis=2, tiled=True)  46.3 us
    dot_general x1, matrix products, shards(): jnp.einsum('eskf,efd->sekd', hidden, w_down, preferred_element_type=jnp.f...  28.4 us
    reduce_scatter x1, waiting for transfers between devices, shards(): lax.psum_scatter(weighted, 'seg', scatter_dimension=1, tiled=True)  21.7 us
    all_to_all x1, blocking collectives, shards(): lax.all_to_all(packed, 'expert', split_axis=0, concat_axis=0, tiled=True)  14.1 us
    gather x2, local copies, waits for them, and re-layouts, shards(): picked = returned.reshape(EXPERTS * SEND_CAP, D)[target]  9.95 us
    all_to_all x1, starting transfers between devices, shards(): lax.all_to_all(partial_out, 'expert', split_axis=0, concat_axis=0, tiled=...  5 us
    transpose x1, local copies, waits for them, and re-layouts, shards(): jnp.einsum('eskf,efd->sekd', hidden, w_down, preferred_element_type=jnp.f...  4.99 us
  transfers between devices with their start and end apart: 3, of which 3 were waited for; matrix products, arithmetic and copies ran while one was open for 0% of the time, Pallas kernels for 0%

commit v1 on v0

v1 whole, which is shorter than its diff:
```python
import functools

import jax
import jax.numpy as jnp
from jax import lax
from jax.experimental import pallas as pl
from jax.experimental.pallas import tpu as pltpu
from jax.sharding import PartitionSpec as P

SEND_CAP = 21
LANES = 128


def hop(value, axis, k):
    n = lax.axis_size(axis)
    return lax.ppermute(value, axis, [(i, i ^ k) for i in range(n)])


def up_to(value, multiple):
    return -(-value // multiple) * multiple


def expert_kernel(
    sizes, place, *refs
):
    (n_exp, n_seg, n_loc, rows, tok, col_a, col_b, tile_f, tile_d, topk) = sizes
    xa = refs[:n_exp]
    xb = refs[n_exp:n_exp + n_seg]
    meta, w_up, w_down = refs[n_exp + n_seg:n_exp + n_seg + 3]
    outs = refs[n_exp + n_seg + 3:]
    ca = outs[:n_exp]
    cb = outs[n_exp:n_exp + n_seg]
    packed, hidden, pick, pick_t, row_w = outs[n_exp + n_seg:]
    step = pl.program_id(0)
    seg_at = place[0]
    first_expert = place[1] * n_loc
    tokens = n_exp * tok
    ff = w_up.shape[2] * (hidden.shape[1] // w_up.shape[2])
    per_expert = ff // tile_f
    n_up = n_loc * per_expert
    slice_d = col_a + col_b
    tiles_a = col_a // tile_d
    tiles_b = col_b // tile_d
    n_a = n_seg * tiles_a

    @pl.when(step == 0)
    def _():
        info = meta[...].astype(jnp.float32)
        ids = info[:topk]
        weights = info[topk:2 * topk] + info[2 * topk:3 * topk]
        masks = []
        gains = []
        for e in range(n_loc):
            here = (ids == (first_expert + e).astype(jnp.float32)).astype(jnp.float32)
            masks.append(jnp.sum(here, axis=0, keepdims=True))
            gains.append(jnp.sum(here * weights, axis=0, keepdims=True))
        earlier = (
            lax.broadcasted_iota(jnp.int32, (tokens, tokens), 0)
            < lax.broadcasted_iota(jnp.int32, (tokens, tokens), 1)
        ).astype(jnp.float32).astype(jnp.bfloat16)
        slot_of_row = lax.broadcasted_iota(jnp.int32, (rows, tokens), 0).astype(jnp.float32)
        for e in range(n_loc):
            mask = jnp.broadcast_to(masks[e], (16, tokens))
            before = jnp.dot(mask.astype(jnp.bfloat16), earlier, preferred_element_type=jnp.float32)
            chosen = jnp.where(
                (slot_of_row == before[:1]) & (masks[e] > 0.5), 1.0, 0.0
            )
            pick[e * rows:(e + 1) * rows, :] = chosen.astype(jnp.bfloat16)
            row_w[e * rows:(e + 1) * rows, :] = jnp.sum(chosen * gains[e], axis=1, keepdims=True)
        pick_t[...] = jnp.transpose(pick[...].astype(jnp.float32)).astype(jnp.bfloat16)
        for j in range(n_seg):
            at = pl.multiple_of((seg_at ^ j) * slice_d, LANES)
            part = None
            for k in range(n_exp):
                piece = jnp.dot(
                    pick[:, k * tok:(k + 1) * tok], xa[k][:, j * col_a:(j + 1) * col_a],
                    preferred_element_type=jnp.float32,
                )
                part = piece if part is None else part + piece
            packed[:, pl.ds(at, col_a)] = part.astype(jnp.bfloat16)
            part = jnp.dot(pick[...], xb[j][...], preferred_element_type=jnp.float32)
            packed[:, pl.ds(pl.multiple_of(at + col_a, LANES), col_b)] = part.astype(jnp.bfloat16)

    for e in range(n_loc):
        for f in range(per_expert):
            @pl.when(step == e * per_expert + f)
            def _(e=e, f=f):
                up = jnp.dot(
                    packed[e * rows:(e + 1) * rows, :], w_up[0], preferred_element_type=jnp.float32
                )
                act = up / (1.0 + jnp.exp(-up))
                hidden[e * rows:(e + 1) * rows, f * tile_f:(f + 1) * tile_f] = act.astype(jnp.bfloat16)

    def down():
        total = None
        for e in range(n_loc):
            at = slice(e * rows, (e + 1) * rows)
            result = jnp.dot(hidden[at, :], w_down[e], preferred_element_type=jnp.float32)
            result = result * row_w[at, :]
            high = result.astype(jnp.bfloat16)
            low = (result - high.astype(jnp.float32)).astype(jnp.bfloat16)
            back = pick_t[:, at]
            part = jnp.dot(back, high, preferred_element_type=jnp.float32)
            part = part + jnp.dot(back, low, preferred_element_type=jnp.float32)
            total = part if total is None else total + part
        return total

    @pl.when((step >= n_up) & (step < n_up + n_a))
    def _():
        total = down()
        for k in range(n_exp):
            ca[k][...] = total[k * tok:(k + 1) * tok].astype(jnp.bfloat16)

    for j in range(n_seg):
        for b in range(tiles_b):
            @pl.when(step == n_up + n_a + j * tiles_b + b)
            def _(j=j, b=b):
                cb[j][:, b * tile_d:(b + 1) * tile_d] = down().astype(jnp.bfloat16)


def experts(place, xa, xb, meta, w_up, w_down, topk):
    n_exp, n_seg = len(xa), len(xb)
    n_loc, width, ff = w_up.shape
    tok = xa[0].shape[0]
    col_a = xa[0].shape[1] // n_seg
    col_b = xb[0].shape[1]
    tokens = n_exp * tok
    rows = up_to(SEND_CAP * n_exp, 16)
    tile_f = ff // 2
    tile_d = col_b
    slice_d = col_a + col_b
    per_expert = ff // tile_f
    n_up = n_loc * per_expert
    tiles_a = col_a // tile_d
    tiles_b = col_b // tile_d
    n_a = n_seg * tiles_a
    n_b = n_seg * tiles_b
    per_slice = slice_d // tile_d

    def up_at(i, place):
        i = jnp.minimum(i, n_up - 1)
        return i // per_expert, 0, i % per_expert

    def down_at(i, place):
        i = jnp.maximum(i - n_up, 0)
        j_a = jnp.minimum(i // tiles_a, n_seg - 1)
        at_a = (place[0] ^ j_a) * per_slice + i % tiles_a
        late = jnp.maximum(i - n_a, 0)
        j_b = late // tiles_b
        at_b = (place[0] ^ j_b) * per_slice + tiles_a + late % tiles_b
        return 0, 0, jnp.where(i < n_a, at_a, at_b)

    def a_at(i, place):
        return 0, jnp.clip(i - n_up, 0, n_a - 1)

    whole = lambda i, place: (0, 0)
    sizes = (n_exp, n_seg, n_loc, rows, tok, col_a, col_b, tile_f, tile_d, topk)
    grid_spec = pltpu.PrefetchScalarGridSpec(
        num_scalar_prefetch=1,
        grid=(n_up + n_a + n_b,),
        in_specs=[pl.BlockSpec(x.shape, whole) for x in xa]
        + [pl.BlockSpec(x.shape, whole) for x in xb]
        + [
            pl.BlockSpec(meta.shape, whole),
            pl.BlockSpec((1, width, tile_f), up_at),
            pl.BlockSpec((n_loc, ff, tile_d), down_at),
        ],
        out_specs=[pl.BlockSpec((tok, tile_d), a_at) for _ in xa]
        + [pl.BlockSpec((tokens, col_b), whole) for _ in xb],
        scratch_shapes=[
            pltpu.VMEM((n_loc * rows, width), jnp.bfloat16),
            pltpu.VMEM((n_loc * rows, ff), jnp.bfloat16),
            pltpu.VMEM((n_loc * rows, tokens), jnp.bfloat16),
            pltpu.VMEM((tokens, n_loc * rows), jnp.bfloat16),
            pltpu.VMEM((n_loc * rows, 1), jnp.float32),
        ],
    )
    outs = pl.pallas_call(
        functools.partial(expert_kernel, sizes),
        grid_spec=grid_spec,
        out_shape=[jax.ShapeDtypeStruct(x.shape, jnp.bfloat16) for x in xa]
        + [jax.ShapeDtypeStruct(x.shape, jnp.bfloat16) for x in xb],
        compiler_params=pltpu.CompilerParams(vmem_limit_bytes=48 << 20),
    )(place, *xa, *xb, meta, w_up, w_down)
    return outs[:n_exp], outs[n_exp:]


def total_of(parts):
    total = parts[0].astype(jnp.float32)
    for part in parts[1:]:
        total = total + part.astype(jnp.float32)
    return total


def shards(tokens, expert_ids, route_weight, w_up, w_down):
    n_exp = lax.axis_size("expert")
    n_seg = lax.axis_size("seg")
    tok, slice_d = tokens.shape
    topk = expert_ids.shape[1]
    if slice_d % (3 * LANES):
        return plain(tokens, expert_ids, route_weight, w_up, w_down)
    col_b = slice_d // 3
    col_a = slice_d - col_b
    place = jnp.stack([lax.axis_index("seg"), lax.axis_index("expert")]).astype(jnp.int32)

    norm = route_weight / jnp.sum(route_weight, axis=1, keepdims=True)
    high = lax.reduce_precision(norm, 8, 7)
    low = norm - high
    info = jnp.concatenate([expert_ids.astype(jnp.float32), high, low], axis=1).T
    info = jnp.pad(info.astype(jnp.bfloat16), ((0, up_to(3 * topk, 16) - 3 * topk), (0, col_b - tok)))

    first_a = tokens[:, :col_a]
    first_b = jnp.concatenate([tokens[:, col_a:], info], axis=0)
    got_a = {k: hop(first_a, "seg", k) for k in reversed(range(1, n_seg))}
    got_b = {k: hop(first_b, "expert", k) for k in reversed(range(1, n_exp))}
    mine_a = jnp.concatenate([first_a] + [got_a[k] for k in range(1, n_seg)], axis=1)
    all_b = [first_b] + [got_b[k] for k in range(1, n_exp)]
    mine_b = jnp.concatenate([b[:tok] for b in all_b], axis=0)
    meta = jnp.concatenate([b[tok:, :tok] for b in all_b], axis=1)
    xa = {k: hop(mine_a, "expert", k) for k in reversed(range(1, n_exp))}
    xb = {k: hop(mine_b, "seg", k) for k in reversed(range(1, n_seg))}
    xa[0], xb[0] = mine_a, mine_b

    ca, cb = experts(
        place, [xa[k] for k in range(n_exp)], [xb[k] for k in range(n_seg)], meta, w_up, w_down, topk
    )

    ra = {k: hop(ca[k], "expert", k) for k in reversed(range(1, n_exp))}
    rb = {k: hop(cb[k], "seg", k) for k in reversed(range(1, n_seg))}
    sum_a = total_of([ca[0]] + [ra[k] for k in range(1, n_exp)])
    sum_b = total_of([cb[0]] + [rb[k] for k in range(1, n_seg)])
    part_a = [sum_a[:, j * col_a:(j + 1) * col_a] for j in range(n_seg)]
    part_b = [sum_b[k * tok:(k + 1) * tok] for k in range(n_exp)]
    fa = {j: hop(part_a[j].astype(jnp.bfloat16), "seg", j) for j in reversed(range(1, n_seg))}
    fb = {k: hop(part_b[k].astype(jnp.bfloat16), "expert", k) for k in reversed(range(1, n_exp))}
    out_a = total_of([part_a[0]] + [fa[j] for j in range(1, n_seg)])
    out_b = total_of([part_b[0]] + [fb[k] for k in range(1, n_exp)])
    return jnp.concatenate([out_a, out_b], axis=1).astype(jnp.bfloat16)


def plain(tokens, expert_ids, route_weight, w_up, w_down):
    n_exp = lax.axis_size("expert")
    exp_local, width = w_up.shape[:2]
    n_experts = n_exp * exp_local
    topk = expert_ids.shape[1]
    tok_rows, width_seg = tokens.shape
    flat = expert_ids.reshape(-1)
    onehot = (flat[:, None] == jnp.arange(n_experts, dtype=jnp.int32)[None, :]).astype(jnp.int32)
    before = jnp.cumsum(onehot, axis=0) - onehot
    target = flat * SEND_CAP + jnp.sum(before * onehot, axis=1)
    norm_weight = route_weight / jnp.sum(route_weight, axis=1, keepdims=True)
    buffer = jnp.zeros((n_experts * SEND_CAP, width_seg), tokens.dtype)
    packed = buffer.at[target].set(jnp.repeat(tokens, topk, axis=0))
    packed = packed.reshape(n_exp, exp_local * SEND_CAP, width_seg)
    arrived = lax.all_to_all(packed, "expert", split_axis=0, concat_axis=0, tiled=True)
    piece = lax.all_gather(arrived, "seg", axis=2, tiled=True)
    block = piece.reshape(n_exp, exp_local, SEND_CAP, width)
    up_sum = jnp.einsum("sekd,edf->eskf", block, w_up, preferred_element_type=jnp.float32)
    hidden = jax.nn.silu(up_sum).astype(jnp.bfloat16)
    partial_out = jnp.einsum("eskf,efd->sekd", hidden, w_down, preferred_element_type=jnp.float32)
    partial_out = partial_out.reshape(n_exp, exp_local * SEND_CAP, width)
    returned = lax.all_to_all(partial_out, "expert", split_axis=0, concat_axis=0, tiled=True)
    picked = returned.reshape(n_experts * SEND_CAP, width)[target]
    weighted = (picked * norm_weight.reshape(-1)[:, None]).reshape(tok_rows, topk, width).sum(axis=1)
    return lax.psum_scatter(weighted, "seg", scatter_dimension=1, tiled=True).astype(jnp.bfloat16)


def solution(mesh):
    placed = (
        P(("dp", "expert"), "seg"),
        P(("dp", "expert"), None),
        P(("dp", "expert"), None),
        P("expert", None, "seg"),
        P("expert", "seg", None),
    )
    return jax.shard_map(
        shards, mesh=mesh, in_specs=placed, out_specs=P(("dp", "expert"), "seg"), check_vma=False
    )
```

time: 215 us -> 98.3 us (0.46)
  waiting for transfers between devices: 117 us -> 17 us
  Pallas kernels: 0 us -> 39.7 us
  starting transfers between devices: 5.27 us -> 35.8 us
  local copies, waits for them, and re-layouts: 30.8 us -> 1.66 us
  matrix products: 28.4 us -> 0 us
  blocking collectives: 14.1 us -> 0 us
  between operations: 13.5 us -> 0.13 us
  other arithmetic: 6.14 us -> 3.18 us
    all_to_all x1 -> x0, waiting for transfers between devices: 48.5 us -> none  [shards(): lax.all_to_all(partial_out, 'expert', split_axis=0, concat_axis=0, tiled=...]
    all_gather x1 -> x0, waiting for transfers between devices: 46.3 us -> none  [shards(): piece = lax.all_gather(arrived, 'seg', axis=2, tiled=True)]
    pallas_call x0 -> x1, Pallas kernels: none -> 39.7 us  [experts(): pl.pallas_call(functools.partial(expert_kernel, sizes), grid_spec=grid_sp...]
    ppermute x0 -> x24, starting transfers between devices: none -> 35.8 us  [hop(): return lax.ppermute(value, axis, [(i, i ^ k) for i in range(n)])]
    dot_general x1 -> x0, matrix products: 28.4 us -> none  [shards(): jnp.einsum('eskf,efd->sekd', hidden, w_down, preferred_element_type=jnp.f...]
    reduce_scatter x1 -> x0, waiting for transfers between devices: 21.7 us -> none  [shards(): lax.psum_scatter(weighted, 'seg', scatter_dimension=1, tiled=True)]
    ppermute x0 -> x24, waiting for transfers between devices: none -> 17 us  [hop(): return lax.ppermute(value, axis, [(i, i ^ k) for i in range(n)])]
    all_to_all x1 -> x0, blocking collectives: 14.1 us -> none  [shards(): lax.all_to_all(packed, 'expert', split_axis=0, concat_axis=0, tiled=True)]
  transfers between devices with their start and end apart: 3 -> 24, of which waited for: 3 -> 8; matrix products, arithmetic and copies ran while one was open for 0% -> 1% of each run, Pallas kernels for 0% -> 0%
where the time goes in v1:
time: 98.3 us; the launch traced here: 97.6 us
  Pallas kernels  39.7 us (40%)
  starting transfers between devices  35.8 us (36%)
  waiting for transfers between devices  17 us (17%)
  other arithmetic  3.18 us (3%)
  local copies, waits for them, and re-layouts  1.66 us (2%)
    pallas_call x1, Pallas kernels, experts(): pl.pallas_call(functools.partial(expert_kernel, sizes), grid_spec=grid_sp...  39.7 us
    ppermute x24, starting transfers between devices, hop(): return lax.ppermute(value, axis, [(i, i ^ k) for i in range(n)])  35.8 us
    ppermute x24, waiting for transfers between devices, hop(): return lax.ppermute(value, axis, [(i, i ^ k) for i in range(n)])  17 us
  transfers between devices with their start and end apart: 24, of which 8 were waited for; matrix products, arithmetic and copies ran while one was open for 1% of the time, Pallas kernels for 0%

profile of v1, /device:TPU:0, one launch (start us, length us, event | category | flops | bytes accessed | tf_op | source)
XLA Modules:
  0.0 97.6 jit_solution(16875710911440579646)
XLA Ops:
  0.0 0.7 convert_convert_fusion
  0.7 0.7 reduce_sum.9
  1.4 0.7 reduce-precision_convert_fusion
  2.1 0.8 slice.58
  2.9 4.0 %collective-permute-start.8 = (bf16[80,256]{1,0:T(8,128)(2,1)S(1)}, bf16[80,256]{1,0:T(8,128)(2,1)S(1)}, u32[]{:S(2)}, u32[]{:S(2)}) collective-permute-start(bf16[80,256]{1,0:T(8,128)(2,1)S(1)} %pad_maximum_fusion.3), channel_id=1, source_target_pairs={{0,12},{4,8},{8,4},{12,0},{1,13},{5,9},{9,5},{13,1},{2,14},{6,10},... | collective-permute-start | bytes 122888 | tf_op jit(solution)/shard_map/ppermute | solution.py:16
  6.9 0.5 collective-permute-start.7
  7.4 0.1 collective-permute-start.6
  7.5 0.8 slice.57
  8.4 4.0 %collective-permute-start.2 = (bf16[64,512]{1,0:T(8,128)(2,1)S(1)}, bf16[64,512]{1,0:T(8,128)(2,1)S(1)}, u32[]{:S(2)}, u32[]{:S(2)}) collective-permute-start(bf16[64,512]{1,0:T(8,128)(2,1)S(1)} %slice.57), channel_id=1, source_target_pairs={{0,3},{1,2},{2,1},{3,0},{4,7},{5,6},{6,5},{7,4},{8,11},{9,10},{10,... | collective-permute-start | bytes 196616 | tf_op jit(solution)/shard_map/ppermute | solution.py:16
  12.4 0.6 collective-permute-start
  12.9 0.0 collective-permute-done.7
  12.9 0.0 collective-permute-done.6
  13.0 3.9 %collective-permute-start.11 = (bf16[256,256]{1,0:T(8,128)(2,1)S(1)}, bf16[256,256]{1,0:T(8,128)(2,1)S(1)}, u32[]{:S(2)}, u32[]{:S(2)}) collective-permute-start(bf16[256,256]{1,0:T(8,128)(2,1)S(1)} %pad_maximum_fusion.1.refs_4_), channel_id=1, source_target_pairs={{0,3},{1,2},{2,1},{3,0},{4,7},{5,6},{6,5},{7,4},{8,11},{9,10},{10,... | collective-permute-start | bytes 393224 | tf_op jit(solution)/shard_map/ppermute | solution.py:16
  16.9 0.0 collective-permute-done.2
  16.9 4.4 %collective-permute-done.1 = bf16[64,512]{1,0:T(8,128)(2,1)S(1)} collective-permute-done((bf16[64,512]{1,0:T(8,128)(2,1)S(1)}, bf16[64,512]{1,0:T(8,128)(2,1)S(1)}, u32[]{:S(2)}, u32[]{:S(2)}) %collective-permute-start.1) | collective-permute-done | bytes 65568 | tf_op jit(solution)/shard_map/ppermute | solution.py:16
  21.2 0.0 collective-permute-done
  21.2 2.5 %collective-permute-start.5 = (bf16[64,2048]{1,0:T(8,128)(2,1)S(1)}, bf16[64,2048]{1,0:T(8,128)(2,1)S(1)}, u32[]{:S(2)}, u32[]{:S(2)}) collective-permute-start(bf16[64,2048]{1,0:T(8,128)(2,1)S(1)} %pad_maximum_fusion.refs_0_), channel_id=1, source_target_pairs={{0,12},{4,8},{8,4},{12,0},{1,13},{5,9},{9,5},{13,1},{2,14},{6,10},... | collective-permute-start | bytes 786440 | tf_op jit(solution)/shard_map/ppermute | solution.py:16
  23.8 0.5 collective-permute-start.4
  24.3 0.5 collective-permute-start.3
  24.8 0.0 collective-permute-start.10
  24.8 3.3 %collective-permute-start.9 = (bf16[256,256]{1,0:T(8,128)(2,1)S(1)}, bf16[256,256]{1,0:T(8,128)(2,1)S(1)}, u32[]{:S(2)}, u32[]{:S(2)}) collective-permute-start(bf16[256,256]{1,0:T(8,128)(2,1)S(1)} %pad_maximum_fusion.1.refs_4_), channel_id=1, source_target_pairs={{0,1},{1,0},{2,3},{3,2},{4,5},{5,4},{6,7},{7,6},{8,9},{9,8},{10,11... | collective-permute-start | bytes 393224 | tf_op jit(solution)/shard_map/ppermute | solution.py:16
  28.1 0.1 pad_add_fusion.place
  28.2 0.1 pad_maximum_fusion.4.refs_8_
  28.3 3.7 %collective-permute-done.10.refs_6_ = bf16[256,256]{1,0:T(8,128)(2,1)S(1)} collective-permute-done((bf16[256,256]{1,0:T(8,128)(2,1)S(1)}, bf16[256,256]{1,0:T(8,128)(2,1)S(1)}, u32[]{:S(2)}, u32[]{:S(2)}) %collective-permute-start.10) | collective-permute-done | bytes 131104 | tf_op jit(solution)/shard_map/ppermute | solution.py:16
  32.0 0.4 collective-permute-done.9.refs_5_
  32.4 0.0 collective-permute-done.5.refs_3_
  32.4 0.0 collective-permute-done.4.refs_2_
  32.4 39.7 %shard_map.55 = (bf16[64,2048]{1,0:T(8,128)(2,1)S(1)}, bf16[64,2048]{1,0:T(8,128)(2,1)S(1)}, bf16[64,2048]{1,0:T(8,128)(2,1)S(1)}, bf16[64,2048]{1,0:T(8,128)(2,...) custom-call(s32[2]{0:T(128)S(1)} %pad_add_fusion.place, ...), custom_call_target="tpu_custom_call" | custom-call | tf_op jit(solution)/shard_map/pallas_call | solution.py:178
  72.1 0.7 collective-permute-start.18
  72.9 1.7 %collective-permute-start.19 = (bf16[256,256]{1,0:T(8,128)(2,1)S(1)}, bf16[256,256]{1,0:T(8,128)(2,1)S(1)}, u32[]{:S(2)}, u32[]{:S(2)}) collective-permute-start(bf16[256,256]{1,0:T(8,128)(2,1)S(1)} %get-tuple-element.19), channel_id=1, source_target_pairs={{0,2},{1,3},{2,0},{3,1},{4,6},{5,7},{6,4},{7,5},{8,10},{9,11},{10,... | collective-permute-start | bytes 393224 | tf_op jit(solution)/shard_map/ppermute | solution.py:16
  74.6 2.0 %collective-permute-start.20 = (bf16[256,256]{1,0:T(8,128)(2,1)S(1)}, bf16[256,256]{1,0:T(8,128)(2,1)S(1)}, u32[]{:S(2)}, u32[]{:S(2)}) collective-permute-start(bf16[256,256]{1,0:T(8,128)(2,1)S(1)} %get-tuple-element.20), channel_id=1, source_target_pairs={{0,3},{1,2},{2,1},{3,0},{4,7},{5,6},{6,5},{7,4},{8,11},{9,10},{10,... | collective-permute-start | bytes 393224 | tf_op jit(solution)/shard_map/ppermute | solution.py:16
  76.6 1.5 %collective-permute-start.12 = (bf16[64,2048]{1,0:T(8,128)(2,1)S(1)}, bf16[64,2048]{1,0:T(8,128)(2,1)S(1)}, u32[]{:S(2)}, u32[]{:S(2)}) collective-permute-start(bf16[64,2048]{1,0:T(8,128)(2,1)S(1)} %get-tuple-element.14), channel_id=1, source_target_pairs={{0,4},{4,0},{8,12},{12,8},{1,5},{5,1},{9,13},{13,9},{2,6},{6,2},{1... | collective-permute-start | bytes 786440 | tf_op jit(solution)/shard_map/ppermute | solution.py:16
  78.1 1.5 %collective-permute-start.13 = (bf16[64,2048]{1,0:T(8,128)(2,1)S(1)}, bf16[64,2048]{1,0:T(8,128)(2,1)S(1)}, u32[]{:S(2)}, u32[]{:S(2)}) collective-permute-start(bf16[64,2048]{1,0:T(8,128)(2,1)S(1)} %get-tuple-element.15), channel_id=1, source_target_pairs={{0,8},{4,12},{8,0},{12,4},{1,9},{5,13},{9,1},{13,5},{2,10},{6,14},... | collective-permute-start | bytes 786440 | tf_op jit(solution)/shard_map/ppermute | solution.py:16
  79.6 1.3 %collective-permute-start.14 = (bf16[64,2048]{1,0:T(8,128)(2,1)S(1)}, bf16[64,2048]{1,0:T(8,128)(2,1)S(1)}, u32[]{:S(2)}, u32[]{:S(2)}) collective-permute-start(bf16[64,2048]{1,0:T(8,128)(2,1)S(1)} %get-tuple-element.16), channel_id=1, source_target_pairs={{0,12},{4,8},{8,4},{12,0},{1,13},{5,9},{9,5},{13,1},{2,14},{6,10},... | collective-permute-start | bytes 786440 | tf_op jit(solution)/shard_map/ppermute | solution.py:16
  80.9 1.6 %collective-permute-done.19 = bf16[256,256]{1,0:T(8,128)(2,1)S(1)} collective-permute-done((bf16[256,256]{1,0:T(8,128)(2,1)S(1)}, bf16[256,256]{1,0:T(8,128)(2,1)S(1)}, u32[]{:S(2)}, u32[]{:S(2)}) %collective-permute-start.19) | collective-permute-done | bytes 131104 | tf_op jit(solution)/shard_map/ppermute | solution.py:16
  82.5 0.1 fusion.8
  82.6 2.0 %collective-permute-start.21 = (bf16[64,256]{1,0:T(8,128)(2,1)S(1)}, bf16[64,256]{1,0:T(8,128)(2,1)S(1)}, u32[]{:S(2)}, u32[]{:S(2)}) collective-permute-start(bf16[64,256]{1,0:T(8,128)(2,1)S(1)} %get-tuple-element.28), channel_id=1, source_target_pairs={{0,4},{4,0},{8,12},{12,8},{1,5},{5,1},{9,13},{13,9},{2,6},{6,2},{1... | collective-permute-start | bytes 98312 | tf_op jit(solution)/shard_map/ppermute | solution.py:16
  84.6 1.5 %collective-permute-start.23 = (bf16[64,256]{1,0:T(8,128)(2,1)S(1)}, bf16[64,256]{1,0:T(8,128)(2,1)S(1)}, u32[]{:S(2)}, u32[]{:S(2)}) collective-permute-start(bf16[64,256]{1,0:T(8,128)(2,1)S(1)} %get-tuple-element.29), channel_id=1, source_target_pairs={{0,12},{4,8},{8,4},{12,0},{1,13},{5,9},{9,5},{13,1},{2,14},{6,10},... | collective-permute-start | bytes 98312 | tf_op jit(solution)/shard_map/ppermute | solution.py:16
  86.2 0.0 collective-permute-start.22
  86.2 1.8 %collective-permute-done.13 = bf16[64,2048]{1,0:T(8,128)(2,1)S(1)} collective-permute-done((bf16[64,2048]{1,0:T(8,128)(2,1)S(1)}, bf16[64,2048]{1,0:T(8,128)(2,1)S(1)}, u32[]{:S(2)}, u32[]{:S(2)}) %collective-permute-start.13) | collective-permute-done | bytes 262176 | tf_op jit(solution)/shard_map/ppermute | solution.py:16
  88.0 0.1 fusion.7
  88.1 0.3 collective-permute-start.15
  88.4 2.5 %collective-permute-start.17 = (bf16[64,512]{1,0:T(8,128)(2,1)S(1)}, bf16[64,512]{1,0:T(8,128)(2,1)S(1)}, u32[]{:S(2)}, u32[]{:S(2)}) collective-permute-start(bf16[64,512]{1,0:T(8,128)(2,1)S(1)} %get-tuple-element.26), channel_id=1, source_target_pairs={{0,3},{1,2},{2,1},{3,0},{4,7},{5,6},{6,5},{7,4},{8,11},{9,10},{10,... | collective-permute-start | bytes 196616 | tf_op jit(solution)/shard_map/ppermute | solution.py:16
  90.9 0.8 collective-permute-start.16
  91.7 1.3 %collective-permute-done.15 = bf16[64,512]{1,0:T(8,128)(2,1)S(1)} collective-permute-done((bf16[64,512]{1,0:T(8,128)(2,1)S(1)}, bf16[64,512]{1,0:T(8,128)(2,1)S(1)}, u32[]{:S(2)}, u32[]{:S(2)}) %collective-permute-start.15) | collective-permute-done | bytes 65568 | tf_op jit(solution)/shard_map/ppermute | solution.py:16
  93.0 1.6 %collective-permute-done.17 = bf16[64,512]{1,0:T(8,128)(2,1)S(1)} collective-permute-done((bf16[64,512]{1,0:T(8,128)(2,1)S(1)}, bf16[64,512]{1,0:T(8,128)(2,1)S(1)}, u32[]{:S(2)}, u32[]{:S(2)}) %collective-permute-start.17) | collective-permute-done | bytes 65568 | tf_op jit(solution)/shard_map/ppermute | solution.py:16
  94.6 2.3 %collective-permute-done.16 = bf16[64,512]{1,0:T(8,128)(2,1)S(1)} collective-permute-done((bf16[64,512]{1,0:T(8,128)(2,1)S(1)}, bf16[64,512]{1,0:T(8,128)(2,1)S(1)}, u32[]{:S(2)}, u32[]{:S(2)}) %collective-permute-start.16) | collective-permute-done | bytes 65568 | tf_op jit(solution)/shard_map/ppermute | solution.py:16
  96.9 0.6 pad_maximum_fusion.2
  (27 shorter events, 0.2 us)
Async XLA Ops:
  2.9 9.5 %collective-permute-start.8 = (bf16[80,256]{1,0:T(8,128)(2,1)S(1)}, bf16[80,256]{1,0:T(8,128)(2,1)S(1)}, u32[]{:S(2)}, u32[]{:S(2)}) collective-permute-start(bf16[80,256]{1,0:T(8,128)(2,1)S(1)} %pad_maximum_fusion.3), channel_id=1, source_target_pairs={{0,12},{4,8},{8,4},{12,0},{1,13},{5,9},{9,5},{13,1},{2,14},{6,10},... | collective-permute-start | bytes 122888 | tf_op jit(solution)/shard_map/ppermute | solution.py:16
  6.9 6.1 %collective-permute-start.7 = (bf16[80,256]{1,0:T(8,128)(2,1)S(1)}, bf16[80,256]{1,0:T(8,128)(2,1)S(1)}, u32[]{:S(2)}, u32[]{:S(2)}) collective-permute-start(bf16[80,256]{1,0:T(8,128)(2,1)S(1)} %pad_maximum_fusion.3), channel_id=1, source_target_pairs={{0,8},{4,12},{8,0},{12,4},{1,9},{5,13},{9,1},{13,5},{2,10},{6,14},... | collective-permute-start | bytes 122888 | tf_op jit(solution)/shard_map/ppermute | solution.py:16
  7.4 5.6 %collective-permute-start.6 = (bf16[80,256]{1,0:T(8,128)(2,1)S(1)}, bf16[80,256]{1,0:T(8,128)(2,1)S(1)}, u32[]{:S(2)}, u32[]{:S(2)}) collective-permute-start(bf16[80,256]{1,0:T(8,128)(2,1)S(1)} %pad_maximum_fusion.3), channel_id=1, source_target_pairs={{0,4},{4,0},{8,12},{12,8},{1,5},{5,1},{9,13},{13,9},{2,6},{6,2},{1... | collective-permute-start | bytes 122888 | tf_op jit(solution)/shard_map/ppermute | solution.py:16
  8.4 8.5 %collective-permute-start.2 = (bf16[64,512]{1,0:T(8,128)(2,1)S(1)}, bf16[64,512]{1,0:T(8,128)(2,1)S(1)}, u32[]{:S(2)}, u32[]{:S(2)}) collective-permute-start(bf16[64,512]{1,0:T(8,128)(2,1)S(1)} %slice.57), channel_id=1, source_target_pairs={{0,3},{1,2},{2,1},{3,0},{4,7},{5,6},{6,5},{7,4},{8,11},{9,10},{10,... | collective-permute-start | bytes 196616 | tf_op jit(solution)/shard_map/ppermute | solution.py:16
  12.4 8.9 %collective-permute-start.1 = (bf16[64,512]{1,0:T(8,128)(2,1)S(1)}, bf16[64,512]{1,0:T(8,128)(2,1)S(1)}, u32[]{:S(2)}, u32[]{:S(2)}) collective-permute-start(bf16[64,512]{1,0:T(8,128)(2,1)S(1)} %slice.57), channel_id=1, source_target_pairs={{0,2},{1,3},{2,0},{3,1},{4,6},{5,7},{6,4},{7,5},{8,10},{9,11},{10,... | collective-permute-start | bytes 196616 | tf_op jit(solution)/shard_map/ppermute | solution.py:16
  12.4 8.9 %collective-permute-start = (bf16[64,512]{1,0:T(8,128)(2,1)S(1)}, bf16[64,512]{1,0:T(8,128)(2,1)S(1)}, u32[]{:S(2)}, u32[]{:S(2)}) collective-permute-start(bf16[64,512]{1,0:T(8,128)(2,1)S(1)} %slice.57), channel_id=1, source_target_pairs={{0,1},{1,0},{2,3},{3,2},{4,5},{5,4},{6,7},{7,6},{8,9},{9,8},{10,11... | collective-permute-start | bytes 196616 | tf_op jit(solution)/shard_map/ppermute | solution.py:16
  13.0 11.8 %collective-permute-start.11 = (bf16[256,256]{1,0:T(8,128)(2,1)S(1)}, bf16[256,256]{1,0:T(8,128)(2,1)S(1)}, u32[]{:S(2)}, u32[]{:S(2)}) collective-permute-start(bf16[256,256]{1,0:T(8,128)(2,1)S(1)} %pad_maximum_fusion.1.refs_4_), channel_id=1, source_target_pairs={{0,3},{1,2},{2,1},{3,0},{4,7},{5,6},{6,5},{7,4},{8,11},{9,10},{10,... | collective-permute-start | bytes 393224 | tf_op jit(solution)/shard_map/ppermute | solution.py:16
  21.2 11.2 %collective-permute-start.5 = (bf16[64,2048]{1,0:T(8,128)(2,1)S(1)}, bf16[64,2048]{1,0:T(8,128)(2,1)S(1)}, u32[]{:S(2)}, u32[]{:S(2)}) collective-permute-start(bf16[64,2048]{1,0:T(8,128)(2,1)S(1)} %pad_maximum_fusion.refs_0_), channel_id=1, source_target_pairs={{0,12},{4,8},{8,4},{12,0},{1,13},{5,9},{9,5},{13,1},{2,14},{6,10},... | collective-permute-start | bytes 786440 | tf_op jit(solution)/shard_map/ppermute | solution.py:16
  23.8 8.7 %collective-permute-start.4 = (bf16[64,2048]{1,0:T(8,128)(2,1)S(1)}, bf16[64,2048]{1,0:T(8,128)(2,1)S(1)}, u32[]{:S(2)}, u32[]{:S(2)}) collective-permute-start(bf16[64,2048]{1,0:T(8,128)(2,1)S(1)} %pad_maximum_fusion.refs_0_), channel_id=1, source_target_pairs={{0,8},{4,12},{8,0},{12,4},{1,9},{5,13},{9,1},{13,5},{2,10},{6,14},... | collective-permute-start | bytes 786440 | tf_op jit(solution)/shard_map/ppermute | solution.py:16
  24.3 8.2 %collective-permute-start.3 = (bf16[64,2048]{1,0:T(8,128)(2,1)S(1)}, bf16[64,2048]{1,0:T(8,128)(2,1)S(1)}, u32[]{:S(2)}, u32[]{:S(2)}) collective-permute-start(bf16[64,2048]{1,0:T(8,128)(2,1)S(1)} %pad_maximum_fusion.refs_0_), channel_id=1, source_target_pairs={{0,4},{4,0},{8,12},{12,8},{1,5},{5,1},{9,13},{13,9},{2,6},{6,2},{1... | collective-permute-start | bytes 786440 | tf_op jit(solution)/shard_map/ppermute | solution.py:16
  24.8 7.2 %collective-permute-start.10 = (bf16[256,256]{1,0:T(8,128)(2,1)S(1)}, bf16[256,256]{1,0:T(8,128)(2,1)S(1)}, u32[]{:S(2)}, u32[]{:S(2)}) collective-permute-start(bf16[256,256]{1,0:T(8,128)(2,1)S(1)} %pad_maximum_fusion.1.refs_4_), channel_id=1, source_target_pairs={{0,2},{1,3},{2,0},{3,1},{4,6},{5,7},{6,4},{7,5},{8,10},{9,11},{10,... | collective-permute-start | bytes 393224 | tf_op jit(solution)/shard_map/ppermute | solution.py:16
  24.8 7.6 %collective-permute-start.9 = (bf16[256,256]{1,0:T(8,128)(2,1)S(1)}, bf16[256,256]{1,0:T(8,128)(2,1)S(1)}, u32[]{:S(2)}, u32[]{:S(2)}) collective-permute-start(bf16[256,256]{1,0:T(8,128)(2,1)S(1)} %pad_maximum_fusion.1.refs_4_), channel_id=1, source_target_pairs={{0,1},{1,0},{2,3},{3,2},{4,5},{5,4},{6,7},{7,6},{8,9},{9,8},{10,11... | collective-permute-start | bytes 393224 | tf_op jit(solution)/shard_map/ppermute | solution.py:16
  72.1 7.5 %collective-permute-start.18 = (bf16[256,256]{1,0:T(8,128)(2,1)S(1)}, bf16[256,256]{1,0:T(8,128)(2,1)S(1)}, u32[]{:S(2)}, u32[]{:S(2)}) collective-permute-start(bf16[256,256]{1,0:T(8,128)(2,1)S(1)} %get-tuple-element.18), channel_id=1, source_target_pairs={{0,1},{1,0},{2,3},{3,2},{4,5},{5,4},{6,7},{7,6},{8,9},{9,8},{10,11... | collective-permute-start | bytes 393224 | tf_op jit(solution)/shard_map/ppermute | solution.py:16
  72.9 9.7 %collective-permute-start.19 = (bf16[256,256]{1,0:T(8,128)(2,1)S(1)}, bf16[256,256]{1,0:T(8,128)(2,1)S(1)}, u32[]{:S(2)}, u32[]{:S(2)}) collective-permute-start(bf16[256,256]{1,0:T(8,128)(2,1)S(1)} %get-tuple-element.19), channel_id=1, source_target_pairs={{0,2},{1,3},{2,0},{3,1},{4,6},{5,7},{6,4},{7,5},{8,10},{9,11},{10,... | collective-permute-start | bytes 393224 | tf_op jit(solution)/shard_map/ppermute | solution.py:16
  74.6 8.0 %collective-permute-start.20 = (bf16[256,256]{1,0:T(8,128)(2,1)S(1)}, bf16[256,256]{1,0:T(8,128)(2,1)S(1)}, u32[]{:S(2)}, u32[]{:S(2)}) collective-permute-start(bf16[256,256]{1,0:T(8,128)(2,1)S(1)} %get-tuple-element.20), channel_id=1, source_target_pairs={{0,3},{1,2},{2,1},{3,0},{4,7},{5,6},{6,5},{7,4},{8,11},{9,10},{10,... | collective-permute-start | bytes 393224 | tf_op jit(solution)/shard_map/ppermute | solution.py:16
  76.6 9.6 %collective-permute-start.12 = (bf16[64,2048]{1,0:T(8,128)(2,1)S(1)}, bf16[64,2048]{1,0:T(8,128)(2,1)S(1)}, u32[]{:S(2)}, u32[]{:S(2)}) collective-permute-start(bf16[64,2048]{1,0:T(8,128)(2,1)S(1)} %get-tuple-element.14), channel_id=1, source_target_pairs={{0,4},{4,0},{8,12},{12,8},{1,5},{5,1},{9,13},{13,9},{2,6},{6,2},{1... | collective-permute-start | bytes 786440 | tf_op jit(solution)/shard_map/ppermute | solution.py:16
  78.1 9.9 %collective-permute-start.13 = (bf16[64,2048]{1,0:T(8,128)(2,1)S(1)}, bf16[64,2048]{1,0:T(8,128)(2,1)S(1)}, u32[]{:S(2)}, u32[]{:S(2)}) collective-permute-start(bf16[64,2048]{1,0:T(8,128)(2,1)S(1)} %get-tuple-element.15), channel_id=1, source_target_pairs={{0,8},{4,12},{8,0},{12,4},{1,9},{5,13},{9,1},{13,5},{2,10},{6,14},... | collective-permute-start | bytes 786440 | tf_op jit(solution)/shard_map/ppermute | solution.py:16
  79.6 8.3 %collective-permute-start.14 = (bf16[64,2048]{1,0:T(8,128)(2,1)S(1)}, bf16[64,2048]{1,0:T(8,128)(2,1)S(1)}, u32[]{:S(2)}, u32[]{:S(2)}) collective-permute-start(bf16[64,2048]{1,0:T(8,128)(2,1)S(1)} %get-tuple-element.16), channel_id=1, source_target_pairs={{0,12},{4,8},{8,4},{12,0},{1,13},{5,9},{9,5},{13,1},{2,14},{6,10},... | collective-permute-start | bytes 786440 | tf_op jit(solution)/shard_map/ppermute | solution.py:16
  82.6 8.3 %collective-permute-start.21 = (bf16[64,256]{1,0:T(8,128)(2,1)S(1)}, bf16[64,256]{1,0:T(8,128)(2,1)S(1)}, u32[]{:S(2)}, u32[]{:S(2)}) collective-permute-start(bf16[64,256]{1,0:T(8,128)(2,1)S(1)} %get-tuple-element.28), channel_id=1, source_target_pairs={{0,4},{4,0},{8,12},{12,8},{1,5},{5,1},{9,13},{13,9},{2,6},{6,2},{1... | collective-permute-start | bytes 98312 | tf_op jit(solution)/shard_map/ppermute | solution.py:16
  84.6 7.0 %collective-permute-start.23 = (bf16[64,256]{1,0:T(8,128)(2,1)S(1)}, bf16[64,256]{1,0:T(8,128)(2,1)S(1)}, u32[]{:S(2)}, u32[]{:S(2)}) collective-permute-start(bf16[64,256]{1,0:T(8,128)(2,1)S(1)} %get-tuple-element.29), channel_id=1, source_target_pairs={{0,12},{4,8},{8,4},{12,0},{1,13},{5,9},{9,5},{13,1},{2,14},{6,10},... | collective-permute-start | bytes 98312 | tf_op jit(solution)/shard_map/ppermute | solution.py:16
  86.2 5.5 %collective-permute-start.22 = (bf16[64,256]{1,0:T(8,128)(2,1)S(1)}, bf16[64,256]{1,0:T(8,128)(2,1)S(1)}, u32[]{:S(2)}, u32[]{:S(2)}) collective-permute-start(bf16[64,256]{1,0:T(8,128)(2,1)S(1)} %get-tuple-element.30), channel_id=1, source_target_pairs={{0,8},{4,12},{8,0},{12,4},{1,9},{5,13},{9,1},{13,5},{2,10},{6,14},... | collective-permute-start | bytes 98312 | tf_op jit(solution)/shard_map/ppermute | solution.py:16
  88.1 4.8 %collective-permute-start.15 = (bf16[64,512]{1,0:T(8,128)(2,1)S(1)}, bf16[64,512]{1,0:T(8,128)(2,1)S(1)}, u32[]{:S(2)}, u32[]{:S(2)}) collective-permute-start(bf16[64,512]{1,0:T(8,128)(2,1)S(1)} %get-tuple-element.25), channel_id=1, source_target_pairs={{0,1},{1,0},{2,3},{3,2},{4,5},{5,4},{6,7},{7,6},{8,9},{9,8},{10,11... | collective-permute-start | bytes 196616 | tf_op jit(solution)/shard_map/ppermute | solution.py:16
  88.4 6.2 %collective-permute-start.17 = (bf16[64,512]{1,0:T(8,128)(2,1)S(1)}, bf16[64,512]{1,0:T(8,128)(2,1)S(1)}, u32[]{:S(2)}, u32[]{:S(2)}) collective-permute-start(bf16[64,512]{1,0:T(8,128)(2,1)S(1)} %get-tuple-element.26), channel_id=1, source_target_pairs={{0,3},{1,2},{2,1},{3,0},{4,7},{5,6},{6,5},{7,4},{8,11},{9,10},{10,... | collective-permute-start | bytes 196616 | tf_op jit(solution)/shard_map/ppermute | solution.py:16
  90.9 6.0 %collective-permute-start.16 = (bf16[64,512]{1,0:T(8,128)(2,1)S(1)}, bf16[64,512]{1,0:T(8,128)(2,1)S(1)}, u32[]{:S(2)}, u32[]{:S(2)}) collective-permute-start(bf16[64,512]{1,0:T(8,128)(2,1)S(1)} %get-tuple-element.27), channel_id=1, source_target_pairs={{0,2},{1,3},{2,0},{3,1},{4,6},{5,7},{6,4},{7,5},{8,10},{9,11},{10,... | collective-permute-start | bytes 196616 | tf_op jit(solution)/shard_map/ppermute | solution.py:16

commit v2 on v0

v2 whole, which is shorter than its diff:
```python
import functools

import jax
import jax.numpy as jnp
from jax import lax
from jax.experimental import pallas as pl
from jax.experimental.pallas import tpu as pltpu
from jax.sharding import PartitionSpec as P


SEND_CAP = 21
LANES = 128


def hop(value, axis, k):
    n = lax.axis_size(axis)
    return lax.ppermute(value, axis, [(i, i ^ k) for i in range(n)])


def up_to(value, multiple):
    return -(-value // multiple) * multiple


def call(body, ins, outs, scratch, limit, flops=0, moved=0):
    return pl.pallas_call(
        body,
        in_specs=[pl.BlockSpec(memory_space=space) for _, space in ins],
        out_specs=[pl.BlockSpec(memory_space=pltpu.VMEM) for _ in outs],
        out_shape=outs,
        scratch_shapes=scratch,
        compiler_params=pltpu.CompilerParams(vmem_limit_bytes=limit << 20),
        cost_estimate=pl.CostEstimate(flops=flops, bytes_accessed=moved, transcendentals=0),
    )(*[value for value, _ in ins])


def first_kernel(topk, col_a, place, tokens, ids, route, out_a, out_b):
    tok = tokens.shape[0]
    col_b = out_b.shape[1]
    out_a[...] = tokens[:, :col_a]
    out_b[:tok, :] = tokens[:, col_a:]
    weight = route[...]
    norm = weight / jnp.sum(weight, axis=0, keepdims=True)
    high = norm.astype(jnp.bfloat16).astype(jnp.float32)
    info = jnp.concatenate([ids[...].astype(jnp.float32), high, norm - high], axis=0)
    rows = out_b.shape[0] - tok
    info = jnp.concatenate([info, jnp.zeros((rows - 3 * topk, tok), jnp.float32)], axis=0)
    info = jnp.concatenate([info, jnp.zeros((rows, col_b - tok), jnp.float32)], axis=1)
    out_b[tok:, :] = info.astype(jnp.bfloat16)


def fetch_kernel(lo, w_ref, after, *refs):
    outs, sem = refs[:-1], refs[-1]
    copies = [
        pltpu.make_async_copy(w_ref.at[lo + i], out, sem.at[i]) for i, out in enumerate(outs)
    ]
    for copy in copies:
        copy.start()
    for copy in copies:
        copy.wait()


def fetch(w, lo, hi, after):
    return call(
        functools.partial(fetch_kernel, lo),
        [(w, pltpu.HBM), (after, pltpu.HBM)], [pltpu.VMEM(w.shape[1:], w.dtype)] * (hi - lo),
        [pltpu.SemaphoreType.DMA((hi - lo,))], 20, moved=2 * w[0].size * (hi - lo),
    )


def route_rows(meta, n_loc, rows, topk, first_expert, pick, pick_t, row_w):
    tokens = pick.shape[1]
    info = meta[...].astype(jnp.float32)
    ids = info[:topk]
    weights = info[topk:2 * topk] + info[2 * topk:3 * topk]
    earlier = (
        lax.broadcasted_iota(jnp.int32, (tokens, tokens), 0)
        < lax.broadcasted_iota(jnp.int32, (tokens, tokens), 1)
    ).astype(jnp.float32).astype(jnp.bfloat16)
    slot_of_row = lax.broadcasted_iota(jnp.int32, (rows, tokens), 0).astype(jnp.float32)
    for e in range(n_loc):
        here = (ids == (first_expert + e).astype(jnp.float32)).astype(jnp.float32)
        mask = jnp.sum(here, axis=0, keepdims=True)
        gain = jnp.sum(here * weights, axis=0, keepdims=True)
        before = jnp.dot(
            jnp.broadcast_to(mask, (16, tokens)).astype(jnp.bfloat16), earlier,
            preferred_element_type=jnp.float32,
        )
        chosen = jnp.where((slot_of_row == before[:1]) & (mask > 0.5), 1.0, 0.0)
        pick[e * rows:(e + 1) * rows, :] = chosen.astype(jnp.bfloat16)
        row_w[e * rows:(e + 1) * rows, :] = jnp.sum(chosen * gain, axis=1, keepdims=True)
    pick_t[...] = jnp.transpose(pick[...].astype(jnp.float32)).astype(jnp.bfloat16)


def down_tile(hidden, weight, pick_t, row_w, rows):
    total = None
    for e in range(weight.shape[0]):
        at = slice(e * rows, (e + 1) * rows)
        result = jnp.dot(hidden[at, :], weight[e], preferred_element_type=jnp.float32)
        result = result * row_w[at, :]
        high = result.astype(jnp.bfloat16)
        low = (result - high.astype(jnp.float32)).astype(jnp.bfloat16)
        back = pick_t[:, at]
        part = jnp.dot(back, high, preferred_element_type=jnp.float32)
        part = part + jnp.dot(back, low, preferred_element_type=jnp.float32)
        total = part if total is None else total + part
    return total


def columns_of(w_down, at, wide):
    return w_down.at[:, :, pl.ds(pl.multiple_of(at, LANES), wide)]


def up_kernel(sizes, place, *refs):
    n_exp, n_seg, n_loc, rows, tok, col_a, col_b, tile_f, topk, n_held = sizes
    xa, refs = refs[:n_exp], refs[n_exp:]
    xb, refs = refs[:n_seg], refs[n_seg:]
    meta, refs = refs[0], refs[1:]
    w_held, refs = refs[:n_held], refs[n_held:]
    (w_up, w_down), refs = refs[:2], refs[2:]
    cb, refs = refs[:n_seg], refs[n_seg:]
    hidden, pick_t, row_w, pick, joined, packed, buf_u, buf_d, sem_u, sem_d = refs
    seg_at = place[0]
    slice_d = col_a + col_b
    per = w_up.shape[2] // tile_f
    tiles = (n_loc - n_held) * per
    deep_u, deep_d = buf_u.shape[0], buf_d.shape[0]

    def tile_u(t):
        cols = pl.ds(pl.multiple_of(lax.rem(t, per) * tile_f, LANES), tile_f)
        slot = lax.rem(t, deep_u)
        return pltpu.make_async_copy(
            w_up.at[n_held + lax.div(t, per), :, cols], buf_u.at[slot], sem_u.at[slot]
        )

    def tile_d(j):
        slot = lax.rem(j, deep_d)
        return pltpu.make_async_copy(
            columns_of(w_down, (seg_at ^ j) * slice_d + col_a, col_b), buf_d.at[slot], sem_d.at[slot]
        )

    for t in range(min(deep_u, tiles)):
        tile_u(jnp.int32(t)).start()
    for j in range(min(deep_d, n_seg)):
        tile_d(jnp.int32(j)).start()
    for k in range(n_exp):
        joined[k * tok:(k + 1) * tok, :] = xa[k][...]
    route_rows(meta, n_loc, rows, topk, place[1] * n_loc, pick, pick_t, row_w)
    for j in range(n_seg):
        at = pl.multiple_of((seg_at ^ j) * slice_d, LANES)
        part = jnp.dot(
            pick[...], joined[:, j * col_a:(j + 1) * col_a], preferred_element_type=jnp.float32
        )
        packed[:, pl.ds(at, col_a)] = part.astype(jnp.bfloat16)
        part = jnp.dot(pick[...], xb[j][...], preferred_element_type=jnp.float32)
        packed[:, pl.ds(pl.multiple_of(at + col_a, LANES), col_b)] = part.astype(jnp.bfloat16)

    def up(at, f, weight):
        value = jnp.dot(packed[at, :], weight, preferred_element_type=jnp.float32)
        value = value / (1.0 + jnp.exp(-value))
        cols = pl.ds(pl.multiple_of(f * tile_f, LANES), tile_f)
        hidden[at, cols] = value.astype(jnp.bfloat16)

    for e, held in enumerate(w_held):
        def from_held(f, carry, e=e, held=held):
            cols = pl.ds(pl.multiple_of(f * tile_f, LANES), tile_f)
            up(slice(e * rows, (e + 1) * rows), f, held[:, cols])
            return carry

        lax.fori_loop(0, per, from_held, 0)

    def from_ring(t, carry):
        tile_u(t).wait()
        at = pl.ds(pl.multiple_of((n_held + lax.div(t, per)) * rows, 16), rows)
        up(at, lax.rem(t, per), buf_u[lax.rem(t, deep_u)])

        @pl.when(t + deep_u < tiles)
        def _():
            tile_u(t + deep_u).start()

        return carry

    lax.fori_loop(0, tiles, from_ring, 0)

    def down(j, carry):
        tile_d(j).wait()
        total = down_tile(hidden, buf_d.at[lax.rem(j, deep_d)], pick_t, row_w, rows).astype(jnp.bfloat16)
        for i in range(n_seg):
            @pl.when(j == i)
            def _(i=i):
                cb[i][...] = total

        @pl.when(j + deep_d < n_seg)
        def _():
            tile_d(j + deep_d).start()

        return carry

    lax.fori_loop(0, n_seg, down, 0)


def down_kernel(sizes, place, hidden, pick_t, row_w, w_down, *refs):
    n_exp, n_seg, rows, tok, slice_d, lo = sizes
    ca = refs[:n_exp]
    buf, sem = refs[n_exp:]
    deep, wide = buf.shape[0], buf.shape[3]

    def tile_d(j):
        slot = lax.rem(j, deep)
        return pltpu.make_async_copy(
            columns_of(w_down, (place[0] ^ j) * slice_d + lo, wide), buf.at[slot], sem.at[slot]
        )

    for j in range(min(deep, n_seg)):
        tile_d(jnp.int32(j)).start()

    def down(j, carry):
        tile_d(j).wait()
        total = down_tile(hidden, buf.at[lax.rem(j, deep)], pick_t, row_w, rows).astype(jnp.bfloat16)
        for k in range(n_exp):
            ca[k][:, pl.ds(pl.multiple_of(j * wide, LANES), wide)] = total[k * tok:(k + 1) * tok]

        @pl.when(j + deep < n_seg)
        def _():
            tile_d(j + deep).start()

        return carry

    lax.fori_loop(0, n_seg, down, 0)


def experts_up(place, xa, xb, meta, w_held, w_up, w_down, topk):
    n_exp, n_seg = len(xa), len(xb)
    n_loc, ff, width = w_down.shape
    tok = xa[0].shape[0]
    col_a = xa[0].shape[1] // n_seg
    col_b = xb[0].shape[1]
    tokens = n_exp * tok
    rows = up_to(SEND_CAP * n_exp, 16)
    sizes = (n_exp, n_seg, n_loc, rows, tok, col_a, col_b, ff // 3, topk, len(w_held))
    bf16 = jnp.bfloat16
    vmem = lambda values: [(value, pltpu.VMEM) for value in values]
    outs = call(
        functools.partial(up_kernel, sizes),
        [(place, pltpu.SMEM)] + vmem(xa) + vmem(xb) + vmem([meta]) + vmem(w_held)
        + [(w_up, pltpu.HBM), (w_down, pltpu.HBM)],
        [jax.ShapeDtypeStruct((tokens, col_b), bf16)] * n_seg
        + [jax.ShapeDtypeStruct((n_loc * rows, ff), bf16),
           jax.ShapeDtypeStruct((tokens, n_loc * rows), bf16),
           jax.ShapeDtypeStruct((n_loc * rows, 1), jnp.float32)],
        [pltpu.VMEM((n_loc * rows, tokens), bf16),
         pltpu.VMEM((tokens, n_seg * col_a), bf16),
         pltpu.VMEM((n_loc * rows, width), bf16),
         pltpu.VMEM((3, width, ff // 3), bf16),
         pltpu.VMEM((3, n_loc, ff, col_b), bf16),
         pltpu.SemaphoreType.DMA((3,)),
         pltpu.SemaphoreType.DMA((3,))],
        24, flops=2 * n_loc * 256 * width * ff, moved=2 * n_loc * ff * col_b * n_seg,
    )
    return outs[:n_seg], outs[n_seg:]


def experts_down(place, held, w_down, lo, wide, tok, n_exp, n_seg, slice_d):
    n_loc, ff, _ = w_down.shape
    hidden, pick_t, row_w = held
    rows = hidden.shape[0] // n_loc
    return call(
        functools.partial(down_kernel, (n_exp, n_seg, rows, tok, slice_d, lo)),
        [(place, pltpu.SMEM), (hidden, pltpu.VMEM), (pick_t, pltpu.VMEM), (row_w, pltpu.VMEM),
         (w_down, pltpu.HBM)],
        [jax.ShapeDtypeStruct((tok, n_seg * wide), jnp.bfloat16)] * n_exp,
        [pltpu.VMEM((n_seg, n_loc, ff, wide), jnp.bfloat16), pltpu.SemaphoreType.DMA((n_seg,))],
        20, flops=2 * n_loc * 256 * n_seg * wide * ff, moved=2 * n_loc * ff * wide * n_seg,
    )


def total_of(parts):
    total = parts[0].astype(jnp.float32)
    for part in parts[1:]:
        total = total + part.astype(jnp.float32)
    return total


def staged(tokens, expert_ids, route_weight, w_up, w_down):
    n_exp = lax.axis_size("expert")
    n_seg = lax.axis_size("seg")
    tok, slice_d = tokens.shape
    topk = expert_ids.shape[1]
    col_b = slice_d // 3
    col_a = slice_d - col_b
    place = jnp.stack([lax.axis_index("seg"), lax.axis_index("expert")]).astype(jnp.int32)

    tok_rows = up_to(3 * topk, 16)
    first_a, first_b = call(
        functools.partial(first_kernel, topk, col_a),
        [(place, pltpu.SMEM), (tokens, pltpu.VMEM), (expert_ids.T, pltpu.VMEM),
         (route_weight.T, pltpu.VMEM)],
        [jax.ShapeDtypeStruct((tok, col_a), jnp.bfloat16),
         jax.ShapeDtypeStruct((tok + tok_rows, col_b), jnp.bfloat16)],
        [], 2,
    )
    n_loc = w_up.shape[0]
    cut, held_loc = n_loc // 4, n_loc // 2
    got_a = {k: hop(first_a, "seg", k) for k in reversed(range(1, n_seg))}
    got_b = {k: hop(first_b, "expert", k) for k in reversed(range(1, n_exp))}
    up_1 = fetch(w_up, 0, cut, first_a)
    mine_a = jnp.concatenate([first_a] + [got_a[k] for k in range(1, n_seg)], axis=1)
    all_b = [first_b] + [got_b[k] for k in range(1, n_exp)]
    mine_b = jnp.concatenate([b[:tok] for b in all_b], axis=0)
    meta = jnp.concatenate([b[tok:, :tok] for b in all_b], axis=1)
    xa = {k: hop(mine_a, "expert", k) for k in reversed(range(1, n_exp))}
    xb = {k: hop(mine_b, "seg", k) for k in reversed(range(1, n_seg))}
    xa[0], xb[0] = mine_a, mine_b
    up_2 = fetch(w_up, cut, held_loc, mine_a)

    cb, held = experts_up(
        place, [xa[k] for k in range(n_exp)], [xb[k] for k in range(n_seg)], meta, [*up_1, *up_2], w_up, w_down, topk
    )
    rb = {k: hop(cb[k], "seg", k) for k in reversed(range(1, n_seg))}
    wide = col_b
    outs = []
    part_a = []
    for lo in range(0, col_a, wide):
        ca = experts_down(place, held, w_down, lo, wide, tok, n_exp, n_seg, slice_d)
        ra = {k: hop(ca[k], "expert", k) for k in reversed(range(1, n_exp))}
        sum_a = total_of([ca[0]] + [ra[k] for k in range(1, n_exp)])
        part_a.append([sum_a[:, j * wide:(j + 1) * wide] for j in range(n_seg)])
    sum_b = total_of([cb[0]] + [rb[k] for k in range(1, n_seg)])
    part_b = [sum_b[k * tok:(k + 1) * tok] for k in range(n_exp)]
    fb = {k: hop(part_b[k].astype(jnp.bfloat16), "expert", k) for k in reversed(range(1, n_exp))}
    for part in part_a:
        fa = {j: hop(part[j].astype(jnp.bfloat16), "seg", j) for j in reversed(range(1, n_seg))}
        outs.append(total_of([part[0]] + [fa[j] for j in range(1, n_seg)]))
    outs.append(total_of([part_b[0]] + [fb[k] for k in range(1, n_exp)]))
    return jnp.concatenate(outs, axis=1).astype(jnp.bfloat16)


def plain(tokens, expert_ids, route_weight, w_up, w_down):
    n_exp = lax.axis_size("expert")
    exp_local, width = w_up.shape[:2]
    n_experts = n_exp * exp_local
    topk = expert_ids.shape[1]
    tok_rows, width_seg = tokens.shape
    flat = expert_ids.reshape(-1)
    onehot = (flat[:, None] == jnp.arange(n_experts, dtype=jnp.int32)[None, :]).astype(jnp.int32)
    before = jnp.cumsum(onehot, axis=0) - onehot
    target = flat * SEND_CAP + jnp.sum(before * onehot, axis=1)
    norm_weight = route_weight / jnp.sum(route_weight, axis=1, keepdims=True)
    buffer = jnp.zeros((n_experts * SEND_CAP, width_seg), tokens.dtype)
    packed = buffer.at[target].set(jnp.repeat(tokens, topk, axis=0))
    packed = packed.reshape(n_exp, exp_local * SEND_CAP, width_seg)
    arrived = lax.all_to_all(packed, "expert", split_axis=0, concat_axis=0, tiled=True)
    piece = lax.all_gather(arrived, "seg", axis=2, tiled=True)
    block = piece.reshape(n_exp, exp_local, SEND_CAP, width)
    up_sum = jnp.einsum("sekd,edf->eskf", block, w_up, preferred_element_type=jnp.float32)
    hidden = jax.nn.silu(up_sum).astype(jnp.bfloat16)
    partial_out = jnp.einsum("eskf,efd->sekd", hidden, w_down, preferred_element_type=jnp.float32)
    partial_out = partial_out.reshape(n_exp, exp_local * SEND_CAP, width)
    returned = lax.all_to_all(partial_out, "expert", split_axis=0, concat_axis=0, tiled=True)
    picked = returned.reshape(n_experts * SEND_CAP, width)[target]
    weighted = (picked * norm_weight.reshape(-1)[:, None]).reshape(tok_rows, topk, width).sum(axis=1)
    return lax.psum_scatter(weighted, "seg", scatter_dimension=1, tiled=True).astype(jnp.bfloat16)


def shards(tokens, expert_ids, route_weight, w_up, w_down):
    if tokens.shape[1] % (3 * LANES):
        return plain(tokens, expert_ids, route_weight, w_up, w_down)
    return staged(tokens, expert_ids, route_weight, w_up, w_down)


def solution(mesh):
    placed = (
        P(("dp", "expert"), "seg"),
        P(("dp", "expert"), None),
        P(("dp", "expert"), None),
        P("expert", None, "seg"),
        P("expert", "seg", None),
    )
    return jax.shard_map(
        shards, mesh=mesh, in_specs=placed, out_specs=P(("dp", "expert"), "seg"), check_vma=False
    )
```

time: 215 us -> 96.6 us (0.45)
  waiting for transfers between devices: 117 us -> 9.08 us
  Pallas kernels: 0 us -> 40.5 us
  starting transfers between devices: 5.27 us -> 43 us
  local copies, waits for them, and re-layouts: 30.8 us -> 2.33 us
  matrix products: 28.4 us -> 0 us
  blocking collectives: 14.1 us -> 0 us
  between operations: 13.5 us -> 0.27 us
  other arithmetic: 6.14 us -> 1.08 us
    all_to_all x1 -> x0, waiting for transfers between devices: 48.5 us -> none  [shards(): lax.all_to_all(partial_out, 'expert', split_axis=0, concat_axis=0, tiled=...]
    all_gather x1 -> x0, waiting for transfers between devices: 46.3 us -> none  [shards(): piece = lax.all_gather(arrived, 'seg', axis=2, tiled=True)]
    ppermute x0 -> x30, starting transfers between devices: none -> 43 us  [hop(): return lax.ppermute(value, axis, [(i, i ^ k) for i in range(n)])]
    pallas_call x0 -> x6, Pallas kernels: none -> 40.5 us  [call(): pl.pallas_call(body, in_specs=[pl.BlockSpec(memory_space=space) for _, sp...]
    dot_general x1 -> x0, matrix products: 28.4 us -> none  [shards(): jnp.einsum('eskf,efd->sekd', hidden, w_down, preferred_element_type=jnp.f...]
    reduce_scatter x1 -> x0, waiting for transfers between devices: 21.7 us -> none  [shards(): lax.psum_scatter(weighted, 'seg', scatter_dimension=1, tiled=True)]
    all_to_all x1 -> x0, blocking collectives: 14.1 us -> none  [shards(): lax.all_to_all(packed, 'expert', split_axis=0, concat_axis=0, tiled=True)]
    gather x2 -> x0, local copies, waits for them, and re-layouts: 9.95 us -> none  [shards(): picked = returned.reshape(EXPERTS * SEND_CAP, D)[target]]
  transfers between devices with their start and end apart: 3 -> 30, of which waited for: 3 -> 5; matrix products, arithmetic and copies ran while one was open for 0% -> 0% of each run, Pallas kernels for 0% -> 24%
where the time goes in v2:
time: 96.6 us; the launch traced here: 96.3 us
  starting transfers between devices  43 us (45%)
  Pallas kernels  40.5 us (42%)
  waiting for transfers between devices  9.08 us (9%)
  local copies, waits for them, and re-layouts  2.33 us (2%)
  other arithmetic  1.08 us (1%)
    ppermute x30, starting transfers between devices, hop(): return lax.ppermute(value, axis, [(i, i ^ k) for i in range(n)])  43 us
    pallas_call x6, Pallas kernels, call(): pl.pallas_call(body, in_specs=[pl.BlockSpec(memory_space=space) for _, sp...  40.5 us
    ppermute x30, waiting for transfers between devices, hop(): return lax.ppermute(value, axis, [(i, i ^ k) for i in range(n)])  9.08 us
    unnamed x9, local copies, waits for them, and re-layouts  2.27 us
  transfers between devices with their start and end apart: 30, of which 5 were waited for; matrix products, arithmetic and copies ran while one was open for 0% of the time, Pallas kernels for 24%

profile of v2, /device:TPU:0, one launch (start us, length us, event | category | flops | bytes accessed | tf_op | source)
XLA Modules:
  0.0 96.3 jit_solution(17847094284203121797)
XLA Ops:
  0.0 0.1 pad_add_fusion.place
  0.1 0.9 copy-done
  1.0 0.7 copy-done.1
  1.7 0.7 copy-done.2
  2.3 0.6 shard_map.55
  2.9 4.0 %collective-permute-start.8 = (bf16[80,256]{1,0:T(8,128)(2,1)S(1)}, bf16[80,256]{1,0:T(8,128)(2,1)S(1)}, u32[]{:S(2)}, u32[]{:S(2)}) collective-permute-start(bf16[80,256]{1,0:T(8,128)(2,1)S(1)} %get-tuple-element.23), channel_id=1, source_target_pairs={{0,12},{4,8},{8,4},{12,0},{1,13},{5,9},{9,5},{13,1},{2,14},{6,10},... | collective-permute-start | bytes 122888 | tf_op jit(solution)/shard_map/ppermute | solution.py:17
  6.9 0.5 collective-permute-start.7
  7.4 0.1 collective-permute-start.6
  7.5 4.0 %collective-permute-start.2 = (bf16[64,512]{1,0:T(8,128)(2,1)S(1)}, bf16[64,512]{1,0:T(8,128)(2,1)S(1)}, u32[]{:S(2)}, u32[]{:S(2)}) collective-permute-start(bf16[64,512]{1,0:T(8,128)(2,1)S(1)} %get-tuple-element.22.after), channel_id=1, source_target_pairs={{0,3},{1,2},{2,1},{3,0},{4,7},{5,6},{6,5},{7,4},{8,11},{9,10},{10,... | collective-permute-start | bytes 196616 | tf_op jit(solution)/shard_map/ppermute | solution.py:17
  11.6 0.6 collective-permute-start
  12.2 3.9 %collective-permute-start.11 = (bf16[256,256]{1,0:T(8,128)(2,1)S(1)}, bf16[256,256]{1,0:T(8,128)(2,1)S(1)}, u32[]{:S(2)}, u32[]{:S(2)}) collective-permute-start(bf16[256,256]{1,0:T(8,128)(2,1)S(1)} %pad_maximum_fusion.refs_4_), channel_id=1, source_target_pairs={{0,3},{1,2},{2,1},{3,0},{4,7},{5,6},{6,5},{7,4},{8,11},{9,10},{10,... | collective-permute-start | bytes 393224 | tf_op jit(solution)/shard_map/ppermute | solution.py:17
  16.1 0.0 collective-permute-done
  16.2 4.2 %collective-permute-done.1 = bf16[64,512]{1,0:T(8,128)(2,1)S(1)} collective-permute-done((bf16[64,512]{1,0:T(8,128)(2,1)S(1)}, bf16[64,512]{1,0:T(8,128)(2,1)S(1)}, u32[]{:S(2)}, u32[]{:S(2)}) %collective-permute-start.1) | collective-permute-done | bytes 65568 | tf_op jit(solution)/shard_map/ppermute | solution.py:17
  20.4 2.5 %collective-permute-start.5 = (bf16[64,2048]{1,0:T(8,128)(2,1)S(1)}, bf16[64,2048]{1,0:T(8,128)(2,1)S(1)}, u32[]{:S(2)}, u32[]{:S(2)}) collective-permute-start(bf16[64,2048]{1,0:T(8,128)(2,1)S(1)} %constant_dynamic-update-slice_fusion.after.refs_0_), channel_id=1, source_target_pairs={{0,12},{4,8},{8,4},{12,0},{1,13},{5,9},{9,5},{13,1},{2,14},{6,10},... | collective-permute-start | bytes 786440 | tf_op jit(solution)/shard_map/ppermute | solution.py:17
  22.9 0.5 collective-permute-start.4
  23.4 0.5 collective-permute-start.3
  24.0 3.2 %collective-permute-start.9 = (bf16[256,256]{1,0:T(8,128)(2,1)S(1)}, bf16[256,256]{1,0:T(8,128)(2,1)S(1)}, u32[]{:S(2)}, u32[]{:S(2)}) collective-permute-start(bf16[256,256]{1,0:T(8,128)(2,1)S(1)} %pad_maximum_fusion.refs_4_), channel_id=1, source_target_pairs={{0,1},{1,0},{2,3},{3,2},{4,5},{5,4},{6,7},{7,6},{8,9},{9,8},{10,11... | collective-permute-start | bytes 393224 | tf_op jit(solution)/shard_map/ppermute | solution.py:17
  27.2 3.7 %shard_map.56.refs_9_ = bf16[3072,1536]{1,0:T(8,128)(2,1)S(1)} custom-call(bf16[4,3072,1536]{2,1,0:T(8,128)(2,1)} %refs_11_.1, bf16[64,512]{1,0:T(8,128)(2,1)S(1)} %get-tuple-element.22.after), custom_call_target="tpu_custom_call" | custom-call | bytes 9437184 | tf_op jit(solution)/shard_map/pallas_call | solution.py:25
  30.9 0.1 pad_maximum_fusion.2.refs_8_
  31.0 3.7 %shard_map.57.refs_10_ = bf16[3072,1536]{1,0:T(8,128)(2,1)S(1)} custom-call(bf16[4,3072,1536]{2,1,0:T(8,128)(2,1)} %refs_11_.1, bf16[64,2048]{1,0:T(8,128)(2,1)S(1)} %constant_dynamic-update-slice_fusion.after.refs_0_), custom_call_target="tpu_custom_call" | custom-call | bytes 9437184 | tf_op jit(solution)/shard_map/pallas_call | solution.py:25
  34.7 17.1 %shard_map.58 = (bf16[256,256]{1,0:T(8,128)(2,1)S(1)}, bf16[256,256]{1,0:T(8,128)(2,1)S(1)}, bf16[256,256]{1,0:T(8,128)(2,1)S(1)}, bf16[256,256]{1,0:T(8,128)(2,...) custom-call(s32[2]{0:T(128)S(1)} %pad_add_fusion.place, ...), custom_call_target="tpu_custom_call" | custom-call | flops 9663676416 | bytes 12582912 | tf_op jit(solution)/shard_map/pallas_call | solution.py:25
  51.8 0.1 collective-permute-start.24
  51.9 1.7 %collective-permute-start.25 = (bf16[256,256]{1,0:T(8,128)(2,1)S(1)}, bf16[256,256]{1,0:T(8,128)(2,1)S(1)}, u32[]{:S(2)}, u32[]{:S(2)}) collective-permute-start(bf16[256,256]{1,0:T(8,128)(2,1)S(1)} %get-tuple-element.37), channel_id=1, source_target_pairs={{0,2},{1,3},{2,0},{3,1},{4,6},{5,7},{6,4},{7,5},{8,10},{9,11},{10,... | collective-permute-start | bytes 393224 | tf_op jit(solution)/shard_map/ppermute | solution.py:17
  53.6 2.7 %collective-permute-start.26 = (bf16[256,256]{1,0:T(8,128)(2,1)S(1)}, bf16[256,256]{1,0:T(8,128)(2,1)S(1)}, u32[]{:S(2)}, u32[]{:S(2)}) collective-permute-start(bf16[256,256]{1,0:T(8,128)(2,1)S(1)} %get-tuple-element.38), channel_id=1, source_target_pairs={{0,3},{1,2},{2,1},{3,0},{4,7},{5,6},{6,5},{7,4},{8,11},{9,10},{10,... | collective-permute-start | bytes 393224 | tf_op jit(solution)/shard_map/ppermute | solution.py:17
  56.3 7.8 %shard_map.60 = (bf16[64,1024]{1,0:T(8,128)(2,1)S(1)}, bf16[64,1024]{1,0:T(8,128)(2,1)S(1)}, bf16[64,1024]{1,0:T(8,128)(2,1)S(1)}, bf16[64,1024]{1,0:T(8,128)(2,1)S(1)}) custom-call(s32[2]{0:T(128)S(1)} %pad_add_fusion.place, bf16[384,1536]{1,0:T(8,128)(2,1)S(1)} %get-tuple-element.24.hidden, bf16[256,384]{1,0:T(8,128)(2,1)S(1)} %get-tuple-element.25.pick_t, ...), custom_call_target="tpu_custom_call" | custom-call | flops 3221225472 | bytes 12582912 | tf_op jit(solution)/shard_map/pallas_call | solution.py:25
  64.0 7.8 %shard_map.59 = (bf16[64,1024]{1,0:T(8,128)(2,1)S(1)}, bf16[64,1024]{1,0:T(8,128)(2,1)S(1)}, bf16[64,1024]{1,0:T(8,128)(2,1)S(1)}, bf16[64,1024]{1,0:T(8,128)(2,1)S(1)}) custom-call(s32[2]{0:T(128)S(1)} %pad_add_fusion.place, bf16[384,1536]{1,0:T(8,128)(2,1)S(1)} %get-tuple-element.24.hidden, bf16[256,384]{1,0:T(8,128)(2,1)S(1)} %get-tuple-element.25.pick_t, ...), custom_call_target="tpu_custom_call" | custom-call | flops 3221225472 | bytes 12582912 | tf_op jit(solution)/shard_map/pallas_call | solution.py:25
  71.8 1.6 %collective-permute-start.18 = (bf16[64,1024]{1,0:T(8,128)(2,1)S(1)}, bf16[64,1024]{1,0:T(8,128)(2,1)S(1)}, u32[]{:S(2)}, u32[]{:S(2)}) collective-permute-start(bf16[64,1024]{1,0:T(8,128)(2,1)S(1)} %get-tuple-element.32), channel_id=1, source_target_pairs={{0,4},{4,0},{8,12},{12,8},{1,5},{5,1},{9,13},{13,9},{2,6},{6,2},{1... | collective-permute-start | bytes 393224 | tf_op jit(solution)/shard_map/ppermute | solution.py:17
  73.4 1.5 %collective-permute-start.19 = (bf16[64,1024]{1,0:T(8,128)(2,1)S(1)}, bf16[64,1024]{1,0:T(8,128)(2,1)S(1)}, u32[]{:S(2)}, u32[]{:S(2)}) collective-permute-start(bf16[64,1024]{1,0:T(8,128)(2,1)S(1)} %get-tuple-element.33), channel_id=1, source_target_pairs={{0,8},{4,12},{8,0},{12,4},{1,9},{5,13},{9,1},{13,5},{2,10},{6,14},... | collective-permute-start | bytes 393224 | tf_op jit(solution)/shard_map/ppermute | solution.py:17
  74.9 0.5 collective-permute-start.20
  75.4 1.5 %collective-permute-start.12 = (bf16[64,1024]{1,0:T(8,128)(2,1)S(1)}, bf16[64,1024]{1,0:T(8,128)(2,1)S(1)}, u32[]{:S(2)}, u32[]{:S(2)}) collective-permute-start(bf16[64,1024]{1,0:T(8,128)(2,1)S(1)} %get-tuple-element.28), channel_id=1, source_target_pairs={{0,4},{4,0},{8,12},{12,8},{1,5},{5,1},{9,13},{13,9},{2,6},{6,2},{1... | collective-permute-start | bytes 393224 | tf_op jit(solution)/shard_map/ppermute | solution.py:17
  76.9 1.5 %collective-permute-start.13 = (bf16[64,1024]{1,0:T(8,128)(2,1)S(1)}, bf16[64,1024]{1,0:T(8,128)(2,1)S(1)}, u32[]{:S(2)}, u32[]{:S(2)}) collective-permute-start(bf16[64,1024]{1,0:T(8,128)(2,1)S(1)} %get-tuple-element.29), channel_id=1, source_target_pairs={{0,8},{4,12},{8,0},{12,4},{1,9},{5,13},{9,1},{13,5},{2,10},{6,14},... | collective-permute-start | bytes 393224 | tf_op jit(solution)/shard_map/ppermute | solution.py:17
  78.4 0.1 fusion.11
  78.5 1.5 %collective-permute-start.14 = (bf16[64,1024]{1,0:T(8,128)(2,1)S(1)}, bf16[64,1024]{1,0:T(8,128)(2,1)S(1)}, u32[]{:S(2)}, u32[]{:S(2)}) collective-permute-start(bf16[64,1024]{1,0:T(8,128)(2,1)S(1)} %get-tuple-element.30), channel_id=1, source_target_pairs={{0,12},{4,8},{8,4},{12,0},{1,13},{5,9},{9,5},{13,1},{2,14},{6,10},... | collective-permute-start | bytes 393224 | tf_op jit(solution)/shard_map/ppermute | solution.py:17
  80.0 1.0 %collective-permute-done.19 = bf16[64,1024]{1,0:T(8,128)(2,1)S(1)} collective-permute-done((bf16[64,1024]{1,0:T(8,128)(2,1)S(1)}, bf16[64,1024]{1,0:T(8,128)(2,1)S(1)}, u32[]{:S(2)}, u32[]{:S(2)}) %collective-permute-start.19) | collective-permute-done | bytes 131104 | tf_op jit(solution)/shard_map/ppermute | solution.py:17
  81.0 0.3 collective-permute-start.27
  81.3 2.4 %collective-permute-start.29 = (bf16[64,256]{1,0:T(8,128)(2,1)S(1)}, bf16[64,256]{1,0:T(8,128)(2,1)S(1)}, u32[]{:S(2)}, u32[]{:S(2)}) collective-permute-start(bf16[64,256]{1,0:T(8,128)(2,1)S(1)} %get-tuple-element.52), channel_id=1, source_target_pairs={{0,12},{4,8},{8,4},{12,0},{1,13},{5,9},{9,5},{13,1},{2,14},{6,10},... | collective-permute-start | bytes 98312 | tf_op jit(solution)/shard_map/ppermute | solution.py:17
  83.6 0.1 fusion.10
  83.7 0.9 collective-permute-start.28
  84.6 1.0 %collective-permute-start.23 = (bf16[64,256]{1,0:T(8,128)(2,1)S(1)}, bf16[64,256]{1,0:T(8,128)(2,1)S(1)}, u32[]{:S(2)}, u32[]{:S(2)}) collective-permute-start(bf16[64,256]{1,0:T(8,128)(2,1)S(1)} %get-tuple-element.49), channel_id=1, source_target_pairs={{0,3},{1,2},{2,1},{3,0},{4,7},{5,6},{6,5},{7,4},{8,11},{9,10},{10,... | collective-permute-start | bytes 98312 | tf_op jit(solution)/shard_map/ppermute | solution.py:17
  85.6 0.1 fusion.9
  85.7 2.6 %collective-permute-start.22 = (bf16[64,256]{1,0:T(8,128)(2,1)S(1)}, bf16[64,256]{1,0:T(8,128)(2,1)S(1)}, u32[]{:S(2)}, u32[]{:S(2)}) collective-permute-start(bf16[64,256]{1,0:T(8,128)(2,1)S(1)} %get-tuple-element.50), channel_id=1, source_target_pairs={{0,2},{1,3},{2,0},{3,1},{4,6},{5,7},{6,4},{7,5},{8,10},{9,11},{10,... | collective-permute-start | bytes 98312 | tf_op jit(solution)/shard_map/ppermute | solution.py:17
  88.3 1.0 %collective-permute-start.15 = (bf16[64,256]{1,0:T(8,128)(2,1)S(1)}, bf16[64,256]{1,0:T(8,128)(2,1)S(1)}, u32[]{:S(2)}, u32[]{:S(2)}) collective-permute-start(bf16[64,256]{1,0:T(8,128)(2,1)S(1)} %get-tuple-element.45), channel_id=1, source_target_pairs={{0,1},{1,0},{2,3},{3,2},{4,5},{5,4},{6,7},{7,6},{8,9},{9,8},{10,11... | collective-permute-start | bytes 98312 | tf_op jit(solution)/shard_map/ppermute | solution.py:17
  89.3 0.9 collective-permute-start.17
  90.2 1.7 %collective-permute-start.16 = (bf16[64,256]{1,0:T(8,128)(2,1)S(1)}, bf16[64,256]{1,0:T(8,128)(2,1)S(1)}, u32[]{:S(2)}, u32[]{:S(2)}) collective-permute-start(bf16[64,256]{1,0:T(8,128)(2,1)S(1)} %get-tuple-element.47), channel_id=1, source_target_pairs={{0,2},{1,3},{2,0},{3,1},{4,6},{5,7},{6,4},{7,5},{8,10},{9,11},{10,... | collective-permute-start | bytes 98312 | tf_op jit(solution)/shard_map/ppermute | solution.py:17
  91.9 0.3 collective-permute-done.15
  92.2 2.8 %collective-permute-done.17 = bf16[64,256]{1,0:T(8,128)(2,1)S(1)} collective-permute-done((bf16[64,256]{1,0:T(8,128)(2,1)S(1)}, bf16[64,256]{1,0:T(8,128)(2,1)S(1)}, u32[]{:S(2)}, u32[]{:S(2)}) %collective-permute-start.17) | collective-permute-done | bytes 32800 | tf_op jit(solution)/shard_map/ppermute | solution.py:17
  95.0 0.7 collective-permute-done.16
  95.7 0.6 pad_maximum_fusion.1
  (49 shorter events, 0.2 us)
Async XLA Ops:
  0.1 0.9 copy-start
  1.0 0.7 copy-start.1
  1.7 0.7 copy-start.2
  2.9 8.7 %collective-permute-start.8 = (bf16[80,256]{1,0:T(8,128)(2,1)S(1)}, bf16[80,256]{1,0:T(8,128)(2,1)S(1)}, u32[]{:S(2)}, u32[]{:S(2)}) collective-permute-start(bf16[80,256]{1,0:T(8,128)(2,1)S(1)} %get-tuple-element.23), channel_id=1, source_target_pairs={{0,12},{4,8},{8,4},{12,0},{1,13},{5,9},{9,5},{13,1},{2,14},{6,10},... | collective-permute-start | bytes 122888 | tf_op jit(solution)/shard_map/ppermute | solution.py:17
  6.9 5.3 %collective-permute-start.7 = (bf16[80,256]{1,0:T(8,128)(2,1)S(1)}, bf16[80,256]{1,0:T(8,128)(2,1)S(1)}, u32[]{:S(2)}, u32[]{:S(2)}) collective-permute-start(bf16[80,256]{1,0:T(8,128)(2,1)S(1)} %get-tuple-element.23), channel_id=1, source_target_pairs={{0,8},{4,12},{8,0},{12,4},{1,9},{5,13},{9,1},{13,5},{2,10},{6,14},... | collective-permute-start | bytes 122888 | tf_op jit(solution)/shard_map/ppermute | solution.py:17
  7.4 4.8 %collective-permute-start.6 = (bf16[80,256]{1,0:T(8,128)(2,1)S(1)}, bf16[80,256]{1,0:T(8,128)(2,1)S(1)}, u32[]{:S(2)}, u32[]{:S(2)}) collective-permute-start(bf16[80,256]{1,0:T(8,128)(2,1)S(1)} %get-tuple-element.23), channel_id=1, source_target_pairs={{0,4},{4,0},{8,12},{12,8},{1,5},{5,1},{9,13},{13,9},{2,6},{6,2},{1... | collective-permute-start | bytes 122888 | tf_op jit(solution)/shard_map/ppermute | solution.py:17
  7.5 12.9 %collective-permute-start.2 = (bf16[64,512]{1,0:T(8,128)(2,1)S(1)}, bf16[64,512]{1,0:T(8,128)(2,1)S(1)}, u32[]{:S(2)}, u32[]{:S(2)}) collective-permute-start(bf16[64,512]{1,0:T(8,128)(2,1)S(1)} %get-tuple-element.22.after), channel_id=1, source_target_pairs={{0,3},{1,2},{2,1},{3,0},{4,7},{5,6},{6,5},{7,4},{8,11},{9,10},{10,... | collective-permute-start | bytes 196616 | tf_op jit(solution)/shard_map/ppermute | solution.py:17
  11.5 8.9 %collective-permute-start.1 = (bf16[64,512]{1,0:T(8,128)(2,1)S(1)}, bf16[64,512]{1,0:T(8,128)(2,1)S(1)}, u32[]{:S(2)}, u32[]{:S(2)}) collective-permute-start(bf16[64,512]{1,0:T(8,128)(2,1)S(1)} %get-tuple-element.22.after), channel_id=1, source_target_pairs={{0,2},{1,3},{2,0},{3,1},{4,6},{5,7},{6,4},{7,5},{8,10},{9,11},{10,... | collective-permute-start | bytes 196616 | tf_op jit(solution)/shard_map/ppermute | solution.py:17
  11.6 4.6 %collective-permute-start = (bf16[64,512]{1,0:T(8,128)(2,1)S(1)}, bf16[64,512]{1,0:T(8,128)(2,1)S(1)}, u32[]{:S(2)}, u32[]{:S(2)}) collective-permute-start(bf16[64,512]{1,0:T(8,128)(2,1)S(1)} %get-tuple-element.22.after), channel_id=1, source_target_pairs={{0,1},{1,0},{2,3},{3,2},{4,5},{5,4},{6,7},{7,6},{8,9},{9,8},{10,11... | collective-permute-start | bytes 196616 | tf_op jit(solution)/shard_map/ppermute | solution.py:17
  12.2 11.7 %collective-permute-start.11 = (bf16[256,256]{1,0:T(8,128)(2,1)S(1)}, bf16[256,256]{1,0:T(8,128)(2,1)S(1)}, u32[]{:S(2)}, u32[]{:S(2)}) collective-permute-start(bf16[256,256]{1,0:T(8,128)(2,1)S(1)} %pad_maximum_fusion.refs_4_), channel_id=1, source_target_pairs={{0,3},{1,2},{2,1},{3,0},{4,7},{5,6},{6,5},{7,4},{8,11},{9,10},{10,... | collective-permute-start | bytes 393224 | tf_op jit(solution)/shard_map/ppermute | solution.py:17
  20.4 14.3 %collective-permute-start.5 = (bf16[64,2048]{1,0:T(8,128)(2,1)S(1)}, bf16[64,2048]{1,0:T(8,128)(2,1)S(1)}, u32[]{:S(2)}, u32[]{:S(2)}) collective-permute-start(bf16[64,2048]{1,0:T(8,128)(2,1)S(1)} %constant_dynamic-update-slice_fusion.after.refs_0_), channel_id=1, source_target_pairs={{0,12},{4,8},{8,4},{12,0},{1,13},{5,9},{9,5},{13,1},{2,14},{6,10},... | collective-permute-start | bytes 786440 | tf_op jit(solution)/shard_map/ppermute | solution.py:17
  22.9 11.8 %collective-permute-start.4 = (bf16[64,2048]{1,0:T(8,128)(2,1)S(1)}, bf16[64,2048]{1,0:T(8,128)(2,1)S(1)}, u32[]{:S(2)}, u32[]{:S(2)}) collective-permute-start(bf16[64,2048]{1,0:T(8,128)(2,1)S(1)} %constant_dynamic-update-slice_fusion.after.refs_0_), channel_id=1, source_target_pairs={{0,8},{4,12},{8,0},{12,4},{1,9},{5,13},{9,1},{13,5},{2,10},{6,14},... | collective-permute-start | bytes 786440 | tf_op jit(solution)/shard_map/ppermute | solution.py:17
  23.4 11.3 %collective-permute-start.3 = (bf16[64,2048]{1,0:T(8,128)(2,1)S(1)}, bf16[64,2048]{1,0:T(8,128)(2,1)S(1)}, u32[]{:S(2)}, u32[]{:S(2)}) collective-permute-start(bf16[64,2048]{1,0:T(8,128)(2,1)S(1)} %constant_dynamic-update-slice_fusion.after.refs_0_), channel_id=1, source_target_pairs={{0,4},{4,0},{8,12},{12,8},{1,5},{5,1},{9,13},{13,9},{2,6},{6,2},{1... | collective-permute-start | bytes 786440 | tf_op jit(solution)/shard_map/ppermute | solution.py:17
  24.0 10.7 %collective-permute-start.10 = (bf16[256,256]{1,0:T(8,128)(2,1)S(1)}, bf16[256,256]{1,0:T(8,128)(2,1)S(1)}, u32[]{:S(2)}, u32[]{:S(2)}) collective-permute-start(bf16[256,256]{1,0:T(8,128)(2,1)S(1)} %pad_maximum_fusion.refs_4_), channel_id=1, source_target_pairs={{0,2},{1,3},{2,0},{3,1},{4,6},{5,7},{6,4},{7,5},{8,10},{9,11},{10,... | collective-permute-start | bytes 393224 | tf_op jit(solution)/shard_map/ppermute | solution.py:17
  24.0 10.7 %collective-permute-start.9 = (bf16[256,256]{1,0:T(8,128)(2,1)S(1)}, bf16[256,256]{1,0:T(8,128)(2,1)S(1)}, u32[]{:S(2)}, u32[]{:S(2)}) collective-permute-start(bf16[256,256]{1,0:T(8,128)(2,1)S(1)} %pad_maximum_fusion.refs_4_), channel_id=1, source_target_pairs={{0,1},{1,0},{2,3},{3,2},{4,5},{5,4},{6,7},{7,6},{8,9},{9,8},{10,11... | collective-permute-start | bytes 393224 | tf_op jit(solution)/shard_map/ppermute | solution.py:17
  51.8 23.1 %collective-permute-start.24 = (bf16[256,256]{1,0:T(8,128)(2,1)S(1)}, bf16[256,256]{1,0:T(8,128)(2,1)S(1)}, u32[]{:S(2)}, u32[]{:S(2)}) collective-permute-start(bf16[256,256]{1,0:T(8,128)(2,1)S(1)} %get-tuple-element.36), channel_id=1, source_target_pairs={{0,1},{1,0},{2,3},{3,2},{4,5},{5,4},{6,7},{7,6},{8,9},{9,8},{10,11... | collective-permute-start | bytes 393224 | tf_op jit(solution)/shard_map/ppermute | solution.py:17
  51.9 23.5 %collective-permute-start.25 = (bf16[256,256]{1,0:T(8,128)(2,1)S(1)}, bf16[256,256]{1,0:T(8,128)(2,1)S(1)}, u32[]{:S(2)}, u32[]{:S(2)}) collective-permute-start(bf16[256,256]{1,0:T(8,128)(2,1)S(1)} %get-tuple-element.37), channel_id=1, source_target_pairs={{0,2},{1,3},{2,0},{3,1},{4,6},{5,7},{6,4},{7,5},{8,10},{9,11},{10,... | collective-permute-start | bytes 393224 | tf_op jit(solution)/shard_map/ppermute | solution.py:17
  53.6 23.3 %collective-permute-start.26 = (bf16[256,256]{1,0:T(8,128)(2,1)S(1)}, bf16[256,256]{1,0:T(8,128)(2,1)S(1)}, u32[]{:S(2)}, u32[]{:S(2)}) collective-permute-start(bf16[256,256]{1,0:T(8,128)(2,1)S(1)} %get-tuple-element.38), channel_id=1, source_target_pairs={{0,3},{1,2},{2,1},{3,0},{4,7},{5,6},{6,5},{7,4},{8,11},{9,10},{10,... | collective-permute-start | bytes 393224 | tf_op jit(solution)/shard_map/ppermute | solution.py:17
  71.8 6.7 %collective-permute-start.18 = (bf16[64,1024]{1,0:T(8,128)(2,1)S(1)}, bf16[64,1024]{1,0:T(8,128)(2,1)S(1)}, u32[]{:S(2)}, u32[]{:S(2)}) collective-permute-start(bf16[64,1024]{1,0:T(8,128)(2,1)S(1)} %get-tuple-element.32), channel_id=1, source_target_pairs={{0,4},{4,0},{8,12},{12,8},{1,5},{5,1},{9,13},{13,9},{2,6},{6,2},{1... | collective-permute-start | bytes 393224 | tf_op jit(solution)/shard_map/ppermute | solution.py:17
  73.4 7.6 %collective-permute-start.19 = (bf16[64,1024]{1,0:T(8,128)(2,1)S(1)}, bf16[64,1024]{1,0:T(8,128)(2,1)S(1)}, u32[]{:S(2)}, u32[]{:S(2)}) collective-permute-start(bf16[64,1024]{1,0:T(8,128)(2,1)S(1)} %get-tuple-element.33), channel_id=1, source_target_pairs={{0,8},{4,12},{8,0},{12,4},{1,9},{5,13},{9,1},{13,5},{2,10},{6,14},... | collective-permute-start | bytes 393224 | tf_op jit(solution)/shard_map/ppermute | solution.py:17
  74.9 6.3 %collective-permute-start.20 = (bf16[64,1024]{1,0:T(8,128)(2,1)S(1)}, bf16[64,1024]{1,0:T(8,128)(2,1)S(1)}, u32[]{:S(2)}, u32[]{:S(2)}) collective-permute-start(bf16[64,1024]{1,0:T(8,128)(2,1)S(1)} %get-tuple-element.34), channel_id=1, source_target_pairs={{0,12},{4,8},{8,4},{12,0},{1,13},{5,9},{9,5},{13,1},{2,14},{6,10},... | collective-permute-start | bytes 393224 | tf_op jit(solution)/shard_map/ppermute | solution.py:17
  75.4 8.3 %collective-permute-start.12 = (bf16[64,1024]{1,0:T(8,128)(2,1)S(1)}, bf16[64,1024]{1,0:T(8,128)(2,1)S(1)}, u32[]{:S(2)}, u32[]{:S(2)}) collective-permute-start(bf16[64,1024]{1,0:T(8,128)(2,1)S(1)} %get-tuple-element.28), channel_id=1, source_target_pairs={{0,4},{4,0},{8,12},{12,8},{1,5},{5,1},{9,13},{13,9},{2,6},{6,2},{1... | collective-permute-start | bytes 393224 | tf_op jit(solution)/shard_map/ppermute | solution.py:17
  76.9 7.7 %collective-permute-start.13 = (bf16[64,1024]{1,0:T(8,128)(2,1)S(1)}, bf16[64,1024]{1,0:T(8,128)(2,1)S(1)}, u32[]{:S(2)}, u32[]{:S(2)}) collective-permute-start(bf16[64,1024]{1,0:T(8,128)(2,1)S(1)} %get-tuple-element.29), channel_id=1, source_target_pairs={{0,8},{4,12},{8,0},{12,4},{1,9},{5,13},{9,1},{13,5},{2,10},{6,14},... | collective-permute-start | bytes 393224 | tf_op jit(solution)/shard_map/ppermute | solution.py:17
  78.5 6.1 %collective-permute-start.14 = (bf16[64,1024]{1,0:T(8,128)(2,1)S(1)}, bf16[64,1024]{1,0:T(8,128)(2,1)S(1)}, u32[]{:S(2)}, u32[]{:S(2)}) collective-permute-start(bf16[64,1024]{1,0:T(8,128)(2,1)S(1)} %get-tuple-element.30), channel_id=1, source_target_pairs={{0,12},{4,8},{8,4},{12,0},{1,13},{5,9},{9,5},{13,1},{2,14},{6,10},... | collective-permute-start | bytes 393224 | tf_op jit(solution)/shard_map/ppermute | solution.py:17
  81.0 4.7 %collective-permute-start.27 = (bf16[64,256]{1,0:T(8,128)(2,1)S(1)}, bf16[64,256]{1,0:T(8,128)(2,1)S(1)}, u32[]{:S(2)}, u32[]{:S(2)}) collective-permute-start(bf16[64,256]{1,0:T(8,128)(2,1)S(1)} %get-tuple-element.51), channel_id=1, source_target_pairs={{0,4},{4,0},{8,12},{12,8},{1,5},{5,1},{9,13},{13,9},{2,6},{6,2},{1... | collective-permute-start | bytes 98312 | tf_op jit(solution)/shard_map/ppermute | solution.py:17
  81.3 7.0 %collective-permute-start.29 = (bf16[64,256]{1,0:T(8,128)(2,1)S(1)}, bf16[64,256]{1,0:T(8,128)(2,1)S(1)}, u32[]{:S(2)}, u32[]{:S(2)}) collective-permute-start(bf16[64,256]{1,0:T(8,128)(2,1)S(1)} %get-tuple-element.52), channel_id=1, source_target_pairs={{0,12},{4,8},{8,4},{12,0},{1,13},{5,9},{9,5},{13,1},{2,14},{6,10},... | collective-permute-start | bytes 98312 | tf_op jit(solution)/shard_map/ppermute | solution.py:17
  83.7 5.5 %collective-permute-start.28 = (bf16[64,256]{1,0:T(8,128)(2,1)S(1)}, bf16[64,256]{1,0:T(8,128)(2,1)S(1)}, u32[]{:S(2)}, u32[]{:S(2)}) collective-permute-start(bf16[64,256]{1,0:T(8,128)(2,1)S(1)} %get-tuple-element.53), channel_id=1, source_target_pairs={{0,8},{4,12},{8,0},{12,4},{1,9},{5,13},{9,1},{13,5},{2,10},{6,14},... | collective-permute-start | bytes 98312 | tf_op jit(solution)/shard_map/ppermute | solution.py:17
  84.6 5.6 %collective-permute-start.21 = (bf16[64,256]{1,0:T(8,128)(2,1)S(1)}, bf16[64,256]{1,0:T(8,128)(2,1)S(1)}, u32[]{:S(2)}, u32[]{:S(2)}) collective-permute-start(bf16[64,256]{1,0:T(8,128)(2,1)S(1)} %get-tuple-element.48), channel_id=1, source_target_pairs={{0,1},{1,0},{2,3},{3,2},{4,5},{5,4},{6,7},{7,6},{8,9},{9,8},{10,11... | collective-permute-start | bytes 98312 | tf_op jit(solution)/shard_map/ppermute | solution.py:17
  84.6 7.2 %collective-permute-start.23 = (bf16[64,256]{1,0:T(8,128)(2,1)S(1)}, bf16[64,256]{1,0:T(8,128)(2,1)S(1)}, u32[]{:S(2)}, u32[]{:S(2)}) collective-permute-start(bf16[64,256]{1,0:T(8,128)(2,1)S(1)} %get-tuple-element.49), channel_id=1, source_target_pairs={{0,3},{1,2},{2,1},{3,0},{4,7},{5,6},{6,5},{7,4},{8,11},{9,10},{10,... | collective-permute-start | bytes 98312 | tf_op jit(solution)/shard_map/ppermute | solution.py:17
  85.7 6.2 %collective-permute-start.22 = (bf16[64,256]{1,0:T(8,128)(2,1)S(1)}, bf16[64,256]{1,0:T(8,128)(2,1)S(1)}, u32[]{:S(2)}, u32[]{:S(2)}) collective-permute-start(bf16[64,256]{1,0:T(8,128)(2,1)S(1)} %get-tuple-element.50), channel_id=1, source_target_pairs={{0,2},{1,3},{2,0},{3,1},{4,6},{5,7},{6,4},{7,5},{8,10},{9,11},{10,... | collective-permute-start | bytes 98312 | tf_op jit(solution)/shard_map/ppermute | solution.py:17
  88.3 3.9 %collective-permute-start.15 = (bf16[64,256]{1,0:T(8,128)(2,1)S(1)}, bf16[64,256]{1,0:T(8,128)(2,1)S(1)}, u32[]{:S(2)}, u32[]{:S(2)}) collective-permute-start(bf16[64,256]{1,0:T(8,128)(2,1)S(1)} %get-tuple-element.45), channel_id=1, source_target_pairs={{0,1},{1,0},{2,3},{3,2},{4,5},{5,4},{6,7},{7,6},{8,9},{9,8},{10,11... | collective-permute-start | bytes 98312 | tf_op jit(solution)/shard_map/ppermute | solution.py:17
  89.3 5.7 %collective-permute-start.17 = (bf16[64,256]{1,0:T(8,128)(2,1)S(1)}, bf16[64,256]{1,0:T(8,128)(2,1)S(1)}, u32[]{:S(2)}, u32[]{:S(2)}) collective-permute-start(bf16[64,256]{1,0:T(8,128)(2,1)S(1)} %get-tuple-element.46), channel_id=1, source_target_pairs={{0,3},{1,2},{2,1},{3,0},{4,7},{5,6},{6,5},{7,4},{8,11},{9,10},{10,... | collective-permute-start | bytes 98312 | tf_op jit(solution)/shard_map/ppermute | solution.py:17
  90.2 5.5 %collective-permute-start.16 = (bf16[64,256]{1,0:T(8,128)(2,1)S(1)}, bf16[64,256]{1,0:T(8,128)(2,1)S(1)}, u32[]{:S(2)}, u32[]{:S(2)}) collective-permute-start(bf16[64,256]{1,0:T(8,128)(2,1)S(1)} %get-tuple-element.47), channel_id=1, source_target_pairs={{0,2},{1,3},{2,0},{3,1},{4,6},{5,7},{6,4},{7,5},{8,10},{9,11},{10,... | collective-permute-start | bytes 98312 | tf_op jit(solution)/shard_map/ppermute | solution.py:17

commit v3 on v2

v3 whole, which is shorter than its diff:
```python
import functools

import jax
import jax.numpy as jnp
from jax import lax
from jax.experimental import pallas as pl
from jax.experimental.pallas import tpu as pltpu
from jax.sharding import PartitionSpec as P


SEND_CAP = 21
LANES = 128


def hop(value, axis, k):
    n = lax.axis_size(axis)
    return lax.ppermute(value, axis, [(i, i ^ k) for i in range(n)])


def up_to(value, multiple):
    return -(-value // multiple) * multiple


def call(body, ins, outs, scratch, limit, flops=0, moved=0):
    return pl.pallas_call(
        body,
        in_specs=[pl.BlockSpec(memory_space=space) for _, space in ins],
        out_specs=[pl.BlockSpec(memory_space=pltpu.VMEM) for _ in outs],
        out_shape=outs,
        scratch_shapes=scratch,
        compiler_params=pltpu.CompilerParams(vmem_limit_bytes=limit << 20),
        cost_estimate=pl.CostEstimate(flops=flops, bytes_accessed=moved, transcendentals=0),
    )(*[value for value, _ in ins])


def first_kernel(topk, place, tokens, ids, route, out, ids_v, route_v, sem):
    tok, slice_d = tokens.shape
    copies = [
        pltpu.make_async_copy(ids, ids_v, sem.at[0]),
        pltpu.make_async_copy(route, route_v, sem.at[1]),
        pltpu.make_async_copy(tokens, out.at[pl.ds(0, tok)], sem.at[2]),
    ]
    for copy in copies:
        copy.start()
    for copy in copies:
        copy.wait()
    weight = route_v[...]
    norm = weight / jnp.sum(weight, axis=0, keepdims=True)
    high = norm.astype(jnp.bfloat16).astype(jnp.float32)
    info = jnp.concatenate([ids_v[...].astype(jnp.float32), high, norm - high], axis=0)
    rows = out.shape[0] - tok
    info = jnp.concatenate([info, jnp.zeros((rows - 3 * topk, tok), jnp.float32)], axis=0)
    info = jnp.concatenate([info, jnp.zeros((rows, slice_d - tok), jnp.float32)], axis=1)
    out[tok:, :] = info.astype(jnp.bfloat16)


def fetch_kernel(lo, w_ref, after, *refs):
    outs, sem = refs[:-1], refs[-1]
    copies = [
        pltpu.make_async_copy(w_ref.at[lo + i], out, sem.at[i]) for i, out in enumerate(outs)
    ]
    for copy in copies:
        copy.start()
    for copy in copies:
        copy.wait()


def fetch(w, lo, hi, after):
    return call(
        functools.partial(fetch_kernel, lo),
        [(w, pltpu.HBM), (after, pltpu.HBM)], [pltpu.VMEM(w.shape[1:], w.dtype)] * (hi - lo),
        [pltpu.SemaphoreType.DMA((hi - lo,))], 20, moved=2 * w[0].size * (hi - lo),
    )


def route_rows(meta, n_loc, rows, topk, first_expert, pick, pick_t, row_w):
    tokens = pick.shape[1]
    info = meta[...].astype(jnp.float32)
    ids = info[:topk]
    weights = info[topk:2 * topk] + info[2 * topk:3 * topk]
    earlier = (
        lax.broadcasted_iota(jnp.int32, (tokens, tokens), 0)
        < lax.broadcasted_iota(jnp.int32, (tokens, tokens), 1)
    ).astype(jnp.float32).astype(jnp.bfloat16)
    slot_of_row = lax.broadcasted_iota(jnp.int32, (rows, tokens), 0).astype(jnp.float32)
    for e in range(n_loc):
        here = (ids == (first_expert + e).astype(jnp.float32)).astype(jnp.float32)
        mask = jnp.sum(here, axis=0, keepdims=True)
        gain = jnp.sum(here * weights, axis=0, keepdims=True)
        before = jnp.dot(
            jnp.broadcast_to(mask, (16, tokens)).astype(jnp.bfloat16), earlier,
            preferred_element_type=jnp.float32,
        )
        chosen = jnp.where((slot_of_row == before[:1]) & (mask > 0.5), 1.0, 0.0)
        pick[e * rows:(e + 1) * rows, :] = chosen.astype(jnp.bfloat16)
        row_w[e * rows:(e + 1) * rows, :] = jnp.sum(chosen * gain, axis=1, keepdims=True)
    pick_t[...] = jnp.transpose(pick[...].astype(jnp.float32)).astype(jnp.bfloat16)


def down_loop(first, count, slice_d, rows, place, hidden, pick_t, row_w, w_down, write, scratch):
    buf, sem, high, low = scratch
    deep = buf.shape[0]
    n_loc = w_down.shape[0]
    tiles = count * n_loc

    def tile(t):
        slot = lax.rem(t, deep)
        at = (place[0] ^ (first + lax.div(t, n_loc))) * slice_d
        return pltpu.make_async_copy(
            w_down.at[lax.rem(t, n_loc), :, pl.ds(pl.multiple_of(at, LANES), slice_d)],
            buf.at[slot], sem.at[slot],
        )

    def begin():
        for t in range(min(deep, tiles)):
            tile(jnp.int32(t)).start()

    def body(t, carry):
        tile(t).wait()
        e = lax.rem(t, n_loc)
        at = pl.ds(pl.multiple_of(e * rows, 16), rows)
        result = jnp.dot(hidden[at, :], buf[lax.rem(t, deep)], preferred_element_type=jnp.float32)

        @pl.when(t + deep < tiles)
        def _():
            tile(t + deep).start()

        result = result * row_w[at, :]
        upper = result.astype(jnp.bfloat16)
        high[at, :] = upper
        low[at, :] = (result - upper.astype(jnp.float32)).astype(jnp.bfloat16)

        @pl.when(e == n_loc - 1)
        def _():
            total = jnp.dot(pick_t[...], high[...], preferred_element_type=jnp.float32)
            total = total + jnp.dot(pick_t[...], low[...], preferred_element_type=jnp.float32)
            write(lax.div(t, n_loc), total)

        return carry

    return begin, lambda: lax.fori_loop(0, tiles, body, 0)


def up_kernel(sizes, place, *refs):
    n_exp, n_seg, n_loc, rows, tok, slice_d, tile_f, topk, n_held = sizes
    far = n_seg - 2
    near, refs = refs[:2], refs[2:]
    blocks, refs = refs[:n_exp], refs[n_exp:]
    meta, refs = refs[0], refs[1:]
    w_held, refs = refs[:n_held], refs[n_held:]
    (w_up, w_down), refs = refs[:2], refs[2:]
    outs, refs = refs[:n_exp], refs[n_exp:]
    hidden, pick_t, row_w, pick, joined, packed, buf_u, sem_u = refs[:8]
    per = w_up.shape[2] // tile_f
    tiles = (n_loc - n_held) * per
    deep_u = buf_u.shape[0]

    def tile_u(t):
        cols = pl.ds(pl.multiple_of(lax.rem(t, per) * tile_f, LANES), tile_f)
        slot = lax.rem(t, deep_u)
        return pltpu.make_async_copy(
            w_up.at[n_held + lax.div(t, per), :, cols], buf_u.at[slot], sem_u.at[slot]
        )

    def write(j, total):
        total = total.astype(jnp.bfloat16)
        cols = pl.ds(pl.multiple_of(j * slice_d, LANES), slice_d)
        for k, out in enumerate(outs):
            out[:, cols] = total[k * tok:(k + 1) * tok]

    begin_down, run_down = down_loop(
        2, far, slice_d, rows, place, hidden, pick_t, row_w, w_down, write, refs[8:]
    )
    for t in range(min(deep_u, tiles)):
        tile_u(jnp.int32(t)).start()
    begin_down()
    for k in range(n_exp):
        joined[k * tok:(k + 1) * tok, :] = blocks[k][...]
    route_rows(meta, n_loc, rows, topk, place[1] * n_loc, pick, pick_t, row_w)
    for j in range(n_seg):
        x = near[j][...] if j < 2 else joined[:, (j - 2) * slice_d:(j - 1) * slice_d]
        part = jnp.dot(pick[...], x, preferred_element_type=jnp.float32)
        at = pl.multiple_of((place[0] ^ j) * slice_d, LANES)
        packed[:, pl.ds(at, slice_d)] = part.astype(jnp.bfloat16)

    def up(at, f, weight):
        value = jnp.dot(packed[at, :], weight, preferred_element_type=jnp.float32)
        value = value / (1.0 + jnp.exp(-value))
        cols = pl.ds(pl.multiple_of(f * tile_f, LANES), tile_f)
        hidden[at, cols] = value.astype(jnp.bfloat16)

    for e, held in enumerate(w_held):
        def from_held(f, carry, e=e, held=held):
            cols = pl.ds(pl.multiple_of(f * tile_f, LANES), tile_f)
            up(slice(e * rows, (e + 1) * rows), f, held[:, cols])
            return carry

        lax.fori_loop(0, per, from_held, 0)

    def from_ring(t, carry):
        tile_u(t).wait()
        at = pl.ds(pl.multiple_of((n_held + lax.div(t, per)) * rows, 16), rows)
        up(at, lax.rem(t, per), buf_u[lax.rem(t, deep_u)])

        @pl.when(t + deep_u < tiles)
        def _():
            tile_u(t + deep_u).start()

        return carry

    lax.fori_loop(0, tiles, from_ring, 0)
    run_down()


def down_kernel(j, rows, place, hidden, pick_t, row_w, w_down, out, *scratch):
    def write(_, total):
        out[...] = total.astype(out.dtype)

    begin, run = down_loop(
        j, 1, out.shape[1], rows, place, hidden, pick_t, row_w, w_down, write, scratch
    )
    begin()
    run()


def down_scratch(n_loc, rows, ff, slice_d, deep):
    bf16 = jnp.bfloat16
    return [
        pltpu.VMEM((deep, ff, slice_d), bf16), pltpu.SemaphoreType.DMA((deep,)),
        pltpu.VMEM((n_loc * rows, slice_d), bf16), pltpu.VMEM((n_loc * rows, slice_d), bf16),
    ]


def experts_up(place, near, blocks, meta, w_held, w_up, w_down, topk):
    n_exp, n_seg = len(blocks), lax.axis_size("seg")
    n_loc, ff, width = w_down.shape
    tok = blocks[0].shape[0]
    tokens, slice_d = near[0].shape
    rows = up_to(SEND_CAP * n_exp, 16)
    tile_f = ff // 3
    sizes = (n_exp, n_seg, n_loc, rows, tok, slice_d, tile_f, topk, len(w_held))
    bf16 = jnp.bfloat16
    vmem = lambda values: [(value, pltpu.VMEM) for value in values]
    outs = call(
        functools.partial(up_kernel, sizes),
        [(place, pltpu.SMEM)] + vmem(near) + vmem(blocks) + vmem([meta]) + vmem(w_held)
        + [(w_up, pltpu.HBM), (w_down, pltpu.HBM)],
        [jax.ShapeDtypeStruct(blocks[0].shape, bf16)] * n_exp
        + [jax.ShapeDtypeStruct((n_loc * rows, ff), bf16),
           jax.ShapeDtypeStruct((tokens, n_loc * rows), bf16),
           jax.ShapeDtypeStruct((n_loc * rows, 1), jnp.float32)],
        [pltpu.VMEM((n_loc * rows, tokens), bf16),
         pltpu.VMEM((tokens, blocks[0].shape[1]), bf16),
         pltpu.VMEM((n_loc * rows, width), bf16),
         pltpu.VMEM((3, width, tile_f), bf16),
         pltpu.SemaphoreType.DMA((3,))] + down_scratch(n_loc, rows, ff, slice_d, 4),
        26, flops=2 * n_loc * 256 * width * ff, moved=n_loc * ff * width * 2,
    )
    return outs[:n_exp], outs[n_exp:]


def experts_down(place, held, w_down, j, slice_d, dtype):
    n_loc, ff, _ = w_down.shape
    hidden, pick_t, row_w = held
    rows = hidden.shape[0] // n_loc
    return call(
        functools.partial(down_kernel, j, rows),
        [(place, pltpu.SMEM), (hidden, pltpu.VMEM), (pick_t, pltpu.VMEM), (row_w, pltpu.VMEM),
         (w_down, pltpu.HBM)],
        [jax.ShapeDtypeStruct((pick_t.shape[0], slice_d), dtype)],
        down_scratch(n_loc, rows, ff, slice_d, 4),
        20, flops=2 * n_loc * 256 * slice_d * ff, moved=2 * n_loc * ff * slice_d,
    )[0]


def total_of(parts):
    total = parts[0].astype(jnp.float32)
    for part in parts[1:]:
        total = total + part.astype(jnp.float32)
    return total


def staged(tokens, expert_ids, route_weight, w_up, w_down):
    n_exp = lax.axis_size("expert")
    n_seg = lax.axis_size("seg")
    tok, slice_d = tokens.shape
    topk = expert_ids.shape[1]
    far = range(2, n_seg)
    peers = range(1, n_exp)
    place = jnp.stack([lax.axis_index("seg"), lax.axis_index("expert")]).astype(jnp.int32)

    a = [hop(tokens, "seg", k) for k in far]
    rows = tok + up_to(3 * topk, 16)
    first = call(
        functools.partial(first_kernel, topk),
        [(place, pltpu.SMEM), (tokens, pltpu.HBM), (expert_ids.T, pltpu.HBM),
         (route_weight.T, pltpu.HBM)],
        [jax.ShapeDtypeStruct((rows, slice_d), tokens.dtype)],
        [pltpu.VMEM((topk, tok), jnp.int32), pltpu.VMEM((topk, tok), jnp.float32),
         pltpu.SemaphoreType.DMA((3,))], 62,
    )[0]
    b = [first] + [hop(first, "expert", k) for k in peers]
    near = jnp.concatenate([x[:tok] for x in b], axis=0)
    e = hop(near, "seg", 1)
    block = jnp.concatenate(a, axis=1)
    blocks = [block] + [hop(block, "expert", k) for k in peers]
    w_held = fetch(w_up, 0, w_up.shape[0] // 2, block)
    meta = jnp.concatenate([x[tok:, :tok] for x in b], axis=1)

    c, held = experts_up(place, [near, e], blocks, meta, w_held, w_up, w_down, topk)
    c = [c[0]] + [hop(c[k], "expert", k) for k in peers]
    g = hop(experts_down(place, held, w_down, 1, slice_d, jnp.bfloat16), "seg", 1)
    own = experts_down(place, held, w_down, 0, slice_d, jnp.float32)
    total = total_of(c).astype(jnp.bfloat16)
    sent = [total[:, (k - 2) * slice_d:(k - 1) * slice_d] for k in far]
    d = [hop(x, "seg", k) for x, k in zip(sent, far)]
    own = total_of([own, g])
    mine = own[:tok]
    own = own.astype(jnp.bfloat16)
    h = [hop(own[k * tok:(k + 1) * tok], "expert", k) for k in peers]
    return total_of([mine] + h + d).astype(jnp.bfloat16)


def plain(tokens, expert_ids, route_weight, w_up, w_down):
    n_exp = lax.axis_size("expert")
    exp_local, width = w_up.shape[:2]
    n_experts = n_exp * exp_local
    topk = expert_ids.shape[1]
    tok_rows, width_seg = tokens.shape
    flat = expert_ids.reshape(-1)
    onehot = (flat[:, None] == jnp.arange(n_experts, dtype=jnp.int32)[None, :]).astype(jnp.int32)
    before = jnp.cumsum(onehot, axis=0) - onehot
    target = flat * SEND_CAP + jnp.sum(before * onehot, axis=1)
    norm_weight = route_weight / jnp.sum(route_weight, axis=1, keepdims=True)
    buffer = jnp.zeros((n_experts * SEND_CAP, width_seg), tokens.dtype)
    packed = buffer.at[target].set(jnp.repeat(tokens, topk, axis=0))
    packed = packed.reshape(n_exp, exp_local * SEND_CAP, width_seg)
    arrived = lax.all_to_all(packed, "expert", split_axis=0, concat_axis=0, tiled=True)
    piece = lax.all_gather(arrived, "seg", axis=2, tiled=True)
    block = piece.reshape(n_exp, exp_local, SEND_CAP, width)
    up_sum = jnp.einsum("sekd,edf->eskf", block, w_up, preferred_element_type=jnp.float32)
    hidden = jax.nn.silu(up_sum).astype(jnp.bfloat16)
    partial_out = jnp.einsum("eskf,efd->sekd", hidden, w_down, preferred_element_type=jnp.float32)
    partial_out = partial_out.reshape(n_exp, exp_local * SEND_CAP, width)
    returned = lax.all_to_all(partial_out, "expert", split_axis=0, concat_axis=0, tiled=True)
    picked = returned.reshape(n_experts * SEND_CAP, width)[target]
    weighted = (picked * norm_weight.reshape(-1)[:, None]).reshape(tok_rows, topk, width).sum(axis=1)
    return lax.psum_scatter(weighted, "seg", scatter_dimension=1, tiled=True).astype(jnp.bfloat16)


def shards(tokens, expert_ids, route_weight, w_up, w_down):
    if tokens.shape[1] % LANES:
        return plain(tokens, expert_ids, route_weight, w_up, w_down)
    return staged(tokens, expert_ids, route_weight, w_up, w_down)


def solution(mesh):
    placed = (
        P(("dp", "expert"), "seg"),
        P(("dp", "expert"), None),
        P(("dp", "expert"), None),
        P("expert", None, "seg"),
        P("expert", "seg", None),
    )
    return jax.shard_map(
        shards, mesh=mesh, in_specs=placed, out_specs=P(("dp", "expert"), "seg"), check_vma=False
    )
```

time: 96.6 us -> 78.1 us (0.81)
  starting transfers between devices: 43 us -> 25.4 us
  Pallas kernels: 40.5 us -> 36.7 us
  waiting for transfers between devices: 9.08 us -> 12.2 us
    ppermute x30 -> x18, starting transfers between devices: 43 us -> 25.4 us  [hop(): return lax.ppermute(value, axis, [(i, i ^ k) for i in range(n)])]
    pallas_call x6 -> x5, Pallas kernels: 40.5 us -> 36.7 us  [call(): pl.pallas_call(body, in_specs=[pl.BlockSpec(memory_space=space) for _, sp...]
    ppermute x30 -> x18, waiting for transfers between devices: 9.08 us -> 12.2 us  [hop(): return lax.ppermute(value, axis, [(i, i ^ k) for i in range(n)])]
    unnamed x9 -> x3, local copies, waits for them, and re-layouts: 2.27 us -> 0.01 us
    slice x11 -> x10, local copies, waits for them, and re-layouts: 0.05 us -> 1.65 us  [the longest x4 0.92 us: staged(): near = jnp.concatenate([x[:tok] for x in b], axis=0)]
  transfers between devices with their start and end apart: 30 -> 18, of which waited for: 5 -> 9; matrix products, arithmetic and copies ran while one was open for 0% -> 3% of each run, Pallas kernels for 24% -> 22%
where the time goes in v3:
time: 78.1 us; the launch traced here: 77.8 us
  Pallas kernels  36.7 us (47%)
  starting transfers between devices  25.4 us (33%)
  waiting for transfers between devices  12.2 us (16%)
  other arithmetic  1.69 us (2%)
  local copies, waits for them, and re-layouts  1.67 us (2%)
    pallas_call x5, Pallas kernels, call(): pl.pallas_call(body, in_specs=[pl.BlockSpec(memory_space=space) for _, sp...  36.7 us
    ppermute x18, starting transfers between devices, hop(): return lax.ppermute(value, axis, [(i, i ^ k) for i in range(n)])  25.4 us
    ppermute x18, waiting for transfers between devices, hop(): return lax.ppermute(value, axis, [(i, i ^ k) for i in range(n)])  12.2 us
  transfers between devices with their start and end apart: 18, of which 9 were waited for; matrix products, arithmetic and copies ran while one was open for 3% of the time, Pallas kernels for 22%

profile of v3, /device:TPU:0, one launch (start us, length us, event | category | flops | bytes accessed | tf_op | source)
XLA Modules:
  0.0 77.8 jit_solution(10724961381029468165)
XLA Ops:
  0.0 0.7 pad_add_fusion.place
  0.7 2.3 %shard_map.55 = bf16[80,768]{1,0:T(8,128)(2,1)} custom-call(s32[2]{0:T(128)} %pad_add_fusion.place, bf16[64,768]{1,0:T(8,128)(2,1)} %tokens.1, s32[4,64]{1,0:T(4,128)} %bitcast.4, f32[4,64]{1,0:T(4,128)} %bitcast.5), custom_call_target="tpu_custom_call" | custom-call | tf_op jit(solution)/shard_map/pallas_call | solution.py:25
  3.0 4.0 %collective-permute-start.2 = (bf16[80,768]{1,0:T(8,128)(2,1)}, bf16[80,768]{1,0:T(8,128)(2,1)S(1)}, u32[]{:S(2)}, u32[]{:S(2)}) collective-permute-start(bf16[80,768]{1,0:T(8,128)(2,1)} %shard_map.55), channel_id=1, source_target_pairs={{0,12},{4,8},{8,4},{12,0},{1,13},{5,9},{9,5},{13,1},{2,14},{6,10},... | collective-permute-start | bytes 368648 | tf_op jit(solution)/shard_map/ppermute | solution.py:17
  6.9 0.5 collective-permute-start.1
  7.4 0.1 collective-permute-start
  7.6 4.0 %collective-permute-start.5 = (bf16[64,768]{1,0:T(8,128)(2,1)}, bf16[64,768]{1,0:T(8,128)(2,1)S(1)}, u32[]{:S(2)}, u32[]{:S(2)}) collective-permute-start(bf16[64,768]{1,0:T(8,128)(2,1)} %tokens.1), channel_id=1, source_target_pairs={{0,3},{1,2},{2,1},{3,0},{4,7},{5,6},{6,5},{7,4},{8,11},{9,10},{10,... | collective-permute-start | bytes 294920 | tf_op jit(solution)/shard_map/ppermute | solution.py:17
  11.6 0.0 collective-permute-start.4
  11.6 0.9 %slice.56 = bf16[64,768]{1,0:T(8,128)(2,1)S(1)} slice(bf16[80,768]{1,0:T(8,128)(2,1)} %shard_map.55), slice={[0:64], [0:768]} | slice | bytes 196608 | tf_op jit(solution)/shard_map/slice | solution.py:303
  12.5 0.0 collective-permute-done.2
  12.5 0.6 collective-permute-done.1
  13.1 0.2 collective-permute-done
  13.4 1.6 %collective-permute-start.3 = (bf16[256,768]{1,0:T(8,128)(2,1)S(1)}, bf16[256,768]{1,0:T(8,128)(2,1)S(1)}, u32[]{:S(2)}, u32[]{:S(2)}) collective-permute-start(bf16[256,768]{1,0:T(8,128)(2,1)S(1)} %pad_maximum_fusion.refs_0_), channel_id=1, source_target_pairs={{0,1},{1,0},{2,3},{3,2},{4,5},{5,4},{6,7},{7,6},{8,9},{9,8},{10,11... | collective-permute-start | bytes 1179656 | tf_op jit(solution)/shard_map/ppermute | solution.py:17
  15.0 4.3 %collective-permute-done.4 = bf16[64,768]{1,0:T(8,128)(2,1)S(1)} collective-permute-done((bf16[64,768]{1,0:T(8,128)(2,1)}, bf16[64,768]{1,0:T(8,128)(2,1)S(1)}, u32[]{:S(2)}, u32[]{:S(2)}) %collective-permute-start.4) | collective-permute-done | bytes 98336 | tf_op jit(solution)/shard_map/ppermute | solution.py:17
  19.3 0.0 collective-permute-done.5
  19.4 2.5 %collective-permute-start.8 = (bf16[64,1536]{1,0:T(8,128)(2,1)S(1)}, bf16[64,1536]{1,0:T(8,128)(2,1)S(1)}, u32[]{:S(2)}, u32[]{:S(2)}) collective-permute-start(bf16[64,1536]{1,0:T(8,128)(2,1)S(1)} %constant_dynamic-update-slice_fusion.after.refs_2_), channel_id=1, source_target_pairs={{0,12},{4,8},{8,4},{12,0},{1,13},{5,9},{9,5},{13,1},{2,14},{6,10},... | collective-permute-start | bytes 589832 | tf_op jit(solution)/shard_map/ppermute | solution.py:17
  21.9 0.5 collective-permute-start.7
  22.4 0.5 collective-permute-start.6
  22.9 0.7 slice.60
  23.6 6.4 %shard_map.56 = (bf16[3072,1536]{1,0:T(8,128)(2,1)S(1)}, bf16[3072,1536]{1,0:T(8,128)(2,1)S(1)}) custom-call(bf16[4,3072,1536]{2,1,0:T(8,128)(2,1)} %refs_9_.1, bf16[64,1536]{1,0:T(8,128)(2,1)S(1)} %constant_dynamic-update-slice_fusion.after.refs_2_), custom_call_target="tpu_custom_call" | custom-call | bytes 18874368 | tf_op jit(solution)/shard_map/pallas_call | solution.py:25
  30.0 0.1 pad_maximum_fusion.1.refs_6_
  30.1 0.0 collective-permute-done.8.refs_5_
  30.1 0.3 collective-permute-done.7.refs_4_
  30.4 0.1 collective-permute-done.6.refs_3_
  30.5 0.0 collective-permute-done.3.refs_1_
  30.5 17.1 %shard_map.57 = (bf16[64,1536]{1,0:T(8,128)(2,1)S(1)}, bf16[64,1536]{1,0:T(8,128)(2,1)S(1)}, bf16[64,1536]{1,0:T(8,128)(2,1)S(1)}, bf16[64,1536]{1,0:T(8,128)(2,...) custom-call(s32[2]{0:T(128)S(1)} %copy-done, ...), custom_call_target="tpu_custom_call" | custom-call | flops 9663676416 | bytes 37748736 | tf_op jit(solution)/shard_map/pallas_call | solution.py:25
  47.6 1.5 %collective-permute-start.13 = (bf16[64,1536]{1,0:T(8,128)(2,1)S(1)}, bf16[64,1536]{1,0:T(8,128)(2,1)S(1)}, u32[]{:S(2)}, u32[]{:S(2)}) collective-permute-start(bf16[64,1536]{1,0:T(8,128)(2,1)S(1)} %get-tuple-element.20), channel_id=1, source_target_pairs={{0,4},{4,0},{8,12},{12,8},{1,5},{5,1},{9,13},{13,9},{2,6},{6,2},{1... | collective-permute-start | bytes 589832 | tf_op jit(solution)/shard_map/ppermute | solution.py:17
  49.1 1.2 %collective-permute-start.14 = (bf16[64,1536]{1,0:T(8,128)(2,1)S(1)}, bf16[64,1536]{1,0:T(8,128)(2,1)S(1)}, u32[]{:S(2)}, u32[]{:S(2)}) collective-permute-start(bf16[64,1536]{1,0:T(8,128)(2,1)S(1)} %get-tuple-element.21), channel_id=1, source_target_pairs={{0,8},{4,12},{8,0},{12,4},{1,9},{5,13},{9,1},{13,5},{2,10},{6,14},... | collective-permute-start | bytes 589832 | tf_op jit(solution)/shard_map/ppermute | solution.py:17
  50.3 0.8 %collective-permute-start.15 = (bf16[64,1536]{1,0:T(8,128)(2,1)S(1)}, bf16[64,1536]{1,0:T(8,128)(2,1)S(1)}, u32[]{:S(2)}, u32[]{:S(2)}) collective-permute-start(bf16[64,1536]{1,0:T(8,128)(2,1)S(1)} %get-tuple-element.22), channel_id=1, source_target_pairs={{0,12},{4,8},{8,4},{12,0},{1,13},{5,9},{9,5},{13,1},{2,14},{6,10},... | collective-permute-start | bytes 589832 | tf_op jit(solution)/shard_map/ppermute | solution.py:17
  51.1 5.5 %shard_map.59 = bf16[256,768]{1,0:T(8,128)(2,1)S(1)} custom-call(s32[2]{0:T(128)S(1)} %copy-done, bf16[384,1536]{1,0:T(8,128)(2,1)S(1)} %get-tuple-element.16.hidden, bf16[256,384]{1,0:T(8,128)(2,1)S(1)} %get-tuple-element.17.pick_t, f32[384,1]{1,0:T(8,128)S(1)} %get-tuple-element.18.row_w, bf16[4,1536,3072]{2,1,0:T(8,128)(2,1)} %w_down.3), custom_call_target="tpu_custom_call" | custom-call | flops 2415919104 | bytes 9437184 | tf_op jit(solution)/shard_map/pallas_call | solution.py:25
  56.6 0.1 collective-permute-start.9
  56.7 5.5 %shard_map.58 = f32[256,768]{1,0:T(8,128)S(1)} custom-call(s32[2]{0:T(128)S(1)} %copy-done, bf16[384,1536]{1,0:T(8,128)(2,1)S(1)} %get-tuple-element.16.hidden, bf16[256,384]{1,0:T(8,128)(2,1)S(1)} %get-tuple-element.17.pick_t, f32[384,1]{1,0:T(8,128)S(1)} %get-tuple-element.18.row_w, bf16[4,1536,3072]{2,1,0:T(8,128)(2,1)} %w_down.3), custom_call_target="tpu_custom_call" | custom-call | flops 2415919104 | bytes 9437184 | tf_op jit(solution)/shard_map/pallas_call | solution.py:25
  62.2 0.0 collective-permute-done.13
  62.2 0.0 collective-permute-done.14
  62.2 0.0 collective-permute-done.15
  62.2 0.1 add_convert_fusion
  62.3 2.7 %collective-permute-start.16 = (bf16[64,768]{1,0:T(8,128)(2,1)S(1)}, bf16[64,768]{1,0:T(8,128)(2,1)S(1)}, u32[]{:S(2)}, u32[]{:S(2)}) collective-permute-start(bf16[64,768]{1,0:T(8,128)(2,1)S(1)} %get-tuple-element.28), channel_id=1, source_target_pairs={{0,2},{1,3},{2,0},{3,1},{4,6},{5,7},{6,4},{7,5},{8,10},{9,11},{10,... | collective-permute-start | bytes 294920 | tf_op jit(solution)/shard_map/ppermute | solution.py:17
  65.0 1.7 %collective-permute-start.17 = (bf16[64,768]{1,0:T(8,128)(2,1)S(1)}, bf16[64,768]{1,0:T(8,128)(2,1)S(1)}, u32[]{:S(2)}, u32[]{:S(2)}) collective-permute-start(bf16[64,768]{1,0:T(8,128)(2,1)S(1)} %get-tuple-element.29), channel_id=1, source_target_pairs={{0,3},{1,2},{2,1},{3,0},{4,7},{5,6},{6,5},{7,4},{8,11},{9,10},{10,... | collective-permute-start | bytes 294920 | tf_op jit(solution)/shard_map/ppermute | solution.py:17
  66.8 2.0 %collective-permute-done.9 = bf16[256,768]{1,0:T(8,128)(2,1)S(1)} collective-permute-done((bf16[256,768]{1,0:T(8,128)(2,1)S(1)}, bf16[256,768]{1,0:T(8,128)(2,1)S(1)}, u32[]{:S(2)}, u32[]{:S(2)}) %collective-permute-start.9) | collective-permute-done | bytes 393248 | tf_op jit(solution)/shard_map/ppermute | solution.py:17
  68.7 0.1 fusion.5
  68.9 1.7 %collective-permute-start.10 = (bf16[64,768]{1,0:T(8,128)(2,1)S(1)}, bf16[64,768]{1,0:T(8,128)(2,1)S(1)}, u32[]{:S(2)}, u32[]{:S(2)}) collective-permute-start(bf16[64,768]{1,0:T(8,128)(2,1)S(1)} %get-tuple-element.25), channel_id=1, source_target_pairs={{0,4},{4,0},{8,12},{12,8},{1,5},{5,1},{9,13},{13,9},{2,6},{6,2},{1... | collective-permute-start | bytes 294920 | tf_op jit(solution)/shard_map/ppermute | solution.py:17
  70.6 1.5 %collective-permute-start.12 = (bf16[64,768]{1,0:T(8,128)(2,1)S(1)}, bf16[64,768]{1,0:T(8,128)(2,1)S(1)}, u32[]{:S(2)}, u32[]{:S(2)}) collective-permute-start(bf16[64,768]{1,0:T(8,128)(2,1)S(1)} %get-tuple-element.26), channel_id=1, source_target_pairs={{0,12},{4,8},{8,4},{12,0},{1,13},{5,9},{9,5},{13,1},{2,14},{6,10},... | collective-permute-start | bytes 294920 | tf_op jit(solution)/shard_map/ppermute | solution.py:17
  72.1 0.4 collective-permute-start.11
  72.4 0.0 collective-permute-done.16
  72.4 0.0 collective-permute-done.17
  72.4 1.1 %collective-permute-done.10 = bf16[64,768]{1,0:T(8,128)(2,1)S(1)} collective-permute-done((bf16[64,768]{1,0:T(8,128)(2,1)S(1)}, bf16[64,768]{1,0:T(8,128)(2,1)S(1)}, u32[]{:S(2)}, u32[]{:S(2)}) %collective-permute-start.10) | collective-permute-done | bytes 98336 | tf_op jit(solution)/shard_map/ppermute | solution.py:17
  73.6 2.6 %collective-permute-done.12 = bf16[64,768]{1,0:T(8,128)(2,1)S(1)} collective-permute-done((bf16[64,768]{1,0:T(8,128)(2,1)S(1)}, bf16[64,768]{1,0:T(8,128)(2,1)S(1)}, u32[]{:S(2)}, u32[]{:S(2)}) %collective-permute-start.12) | collective-permute-done | bytes 98336 | tf_op jit(solution)/shard_map/ppermute | solution.py:17
  76.1 1.0 %collective-permute-done.11 = bf16[64,768]{1,0:T(8,128)(2,1)S(1)} collective-permute-done((bf16[64,768]{1,0:T(8,128)(2,1)S(1)}, bf16[64,768]{1,0:T(8,128)(2,1)S(1)}, u32[]{:S(2)}, u32[]{:S(2)}) %collective-permute-start.11) | collective-permute-done | bytes 98336 | tf_op jit(solution)/shard_map/ppermute | solution.py:17
  77.1 0.7 fusion.4
  (13 shorter events, 0.1 us)
Async XLA Ops:
  3.0 9.5 %collective-permute-start.2 = (bf16[80,768]{1,0:T(8,128)(2,1)}, bf16[80,768]{1,0:T(8,128)(2,1)S(1)}, u32[]{:S(2)}, u32[]{:S(2)}) collective-permute-start(bf16[80,768]{1,0:T(8,128)(2,1)} %shard_map.55), channel_id=1, source_target_pairs={{0,12},{4,8},{8,4},{12,0},{1,13},{5,9},{9,5},{13,1},{2,14},{6,10},... | collective-permute-start | bytes 368648 | tf_op jit(solution)/shard_map/ppermute | solution.py:17
  6.9 6.2 %collective-permute-start.1 = (bf16[80,768]{1,0:T(8,128)(2,1)}, bf16[80,768]{1,0:T(8,128)(2,1)S(1)}, u32[]{:S(2)}, u32[]{:S(2)}) collective-permute-start(bf16[80,768]{1,0:T(8,128)(2,1)} %shard_map.55), channel_id=1, source_target_pairs={{0,8},{4,12},{8,0},{12,4},{1,9},{5,13},{9,1},{13,5},{2,10},{6,14},... | collective-permute-start | bytes 368648 | tf_op jit(solution)/shard_map/ppermute | solution.py:17
  7.4 5.9 %collective-permute-start = (bf16[80,768]{1,0:T(8,128)(2,1)}, bf16[80,768]{1,0:T(8,128)(2,1)S(1)}, u32[]{:S(2)}, u32[]{:S(2)}) collective-permute-start(bf16[80,768]{1,0:T(8,128)(2,1)} %shard_map.55), channel_id=1, source_target_pairs={{0,4},{4,0},{8,12},{12,8},{1,5},{5,1},{9,13},{13,9},{2,6},{6,2},{1... | collective-permute-start | bytes 368648 | tf_op jit(solution)/shard_map/ppermute | solution.py:17
  7.6 11.8 %collective-permute-start.5 = (bf16[64,768]{1,0:T(8,128)(2,1)}, bf16[64,768]{1,0:T(8,128)(2,1)S(1)}, u32[]{:S(2)}, u32[]{:S(2)}) collective-permute-start(bf16[64,768]{1,0:T(8,128)(2,1)} %tokens.1), channel_id=1, source_target_pairs={{0,3},{1,2},{2,1},{3,0},{4,7},{5,6},{6,5},{7,4},{8,11},{9,10},{10,... | collective-permute-start | bytes 294920 | tf_op jit(solution)/shard_map/ppermute | solution.py:17
  11.6 7.7 %collective-permute-start.4 = (bf16[64,768]{1,0:T(8,128)(2,1)}, bf16[64,768]{1,0:T(8,128)(2,1)S(1)}, u32[]{:S(2)}, u32[]{:S(2)}) collective-permute-start(bf16[64,768]{1,0:T(8,128)(2,1)} %tokens.1), channel_id=1, source_target_pairs={{0,2},{1,3},{2,0},{3,1},{4,6},{5,7},{6,4},{7,5},{8,10},{9,11},{10,... | collective-permute-start | bytes 294920 | tf_op jit(solution)/shard_map/ppermute | solution.py:17
  13.4 17.1 %collective-permute-start.3 = (bf16[256,768]{1,0:T(8,128)(2,1)S(1)}, bf16[256,768]{1,0:T(8,128)(2,1)S(1)}, u32[]{:S(2)}, u32[]{:S(2)}) collective-permute-start(bf16[256,768]{1,0:T(8,128)(2,1)S(1)} %pad_maximum_fusion.refs_0_), channel_id=1, source_target_pairs={{0,1},{1,0},{2,3},{3,2},{4,5},{5,4},{6,7},{7,6},{8,9},{9,8},{10,11... | collective-permute-start | bytes 1179656 | tf_op jit(solution)/shard_map/ppermute | solution.py:17
  19.4 10.7 %collective-permute-start.8 = (bf16[64,1536]{1,0:T(8,128)(2,1)S(1)}, bf16[64,1536]{1,0:T(8,128)(2,1)S(1)}, u32[]{:S(2)}, u32[]{:S(2)}) collective-permute-start(bf16[64,1536]{1,0:T(8,128)(2,1)S(1)} %constant_dynamic-update-slice_fusion.after.refs_2_), channel_id=1, source_target_pairs={{0,12},{4,8},{8,4},{12,0},{1,13},{5,9},{9,5},{13,1},{2,14},{6,10},... | collective-permute-start | bytes 589832 | tf_op jit(solution)/shard_map/ppermute | solution.py:17
  21.9 8.5 %collective-permute-start.7 = (bf16[64,1536]{1,0:T(8,128)(2,1)S(1)}, bf16[64,1536]{1,0:T(8,128)(2,1)S(1)}, u32[]{:S(2)}, u32[]{:S(2)}) collective-permute-start(bf16[64,1536]{1,0:T(8,128)(2,1)S(1)} %constant_dynamic-update-slice_fusion.after.refs_2_), channel_id=1, source_target_pairs={{0,8},{4,12},{8,0},{12,4},{1,9},{5,13},{9,1},{13,5},{2,10},{6,14},... | collective-permute-start | bytes 589832 | tf_op jit(solution)/shard_map/ppermute | solution.py:17
  22.4 8.1 %collective-permute-start.6 = (bf16[64,1536]{1,0:T(8,128)(2,1)S(1)}, bf16[64,1536]{1,0:T(8,128)(2,1)S(1)}, u32[]{:S(2)}, u32[]{:S(2)}) collective-permute-start(bf16[64,1536]{1,0:T(8,128)(2,1)S(1)} %constant_dynamic-update-slice_fusion.after.refs_2_), channel_id=1, source_target_pairs={{0,4},{4,0},{8,12},{12,8},{1,5},{5,1},{9,13},{13,9},{2,6},{6,2},{1... | collective-permute-start | bytes 589832 | tf_op jit(solution)/shard_map/ppermute | solution.py:17
  23.6 6.9 %copy-start = (s32[2]{0:T(128)S(1)}, s32[2]{0:T(128)}, u32[]{:S(2)}) copy-start(s32[2]{0:T(128)} %pad_add_fusion.place) | copy-start | bytes 28
  47.6 14.6 %collective-permute-start.13 = (bf16[64,1536]{1,0:T(8,128)(2,1)S(1)}, bf16[64,1536]{1,0:T(8,128)(2,1)S(1)}, u32[]{:S(2)}, u32[]{:S(2)}) collective-permute-start(bf16[64,1536]{1,0:T(8,128)(2,1)S(1)} %get-tuple-element.20), channel_id=1, source_target_pairs={{0,4},{4,0},{8,12},{12,8},{1,5},{5,1},{9,13},{13,9},{2,6},{6,2},{1... | collective-permute-start | bytes 589832 | tf_op jit(solution)/shard_map/ppermute | solution.py:17
  49.1 13.1 %collective-permute-start.14 = (bf16[64,1536]{1,0:T(8,128)(2,1)S(1)}, bf16[64,1536]{1,0:T(8,128)(2,1)S(1)}, u32[]{:S(2)}, u32[]{:S(2)}) collective-permute-start(bf16[64,1536]{1,0:T(8,128)(2,1)S(1)} %get-tuple-element.21), channel_id=1, source_target_pairs={{0,8},{4,12},{8,0},{12,4},{1,9},{5,13},{9,1},{13,5},{2,10},{6,14},... | collective-permute-start | bytes 589832 | tf_op jit(solution)/shard_map/ppermute | solution.py:17
  50.3 11.9 %collective-permute-start.15 = (bf16[64,1536]{1,0:T(8,128)(2,1)S(1)}, bf16[64,1536]{1,0:T(8,128)(2,1)S(1)}, u32[]{:S(2)}, u32[]{:S(2)}) collective-permute-start(bf16[64,1536]{1,0:T(8,128)(2,1)S(1)} %get-tuple-element.22), channel_id=1, source_target_pairs={{0,12},{4,8},{8,4},{12,0},{1,13},{5,9},{9,5},{13,1},{2,14},{6,10},... | collective-permute-start | bytes 589832 | tf_op jit(solution)/shard_map/ppermute | solution.py:17
  56.6 12.1 %collective-permute-start.9 = (bf16[256,768]{1,0:T(8,128)(2,1)S(1)}, bf16[256,768]{1,0:T(8,128)(2,1)S(1)}, u32[]{:S(2)}, u32[]{:S(2)}) collective-permute-start(bf16[256,768]{1,0:T(8,128)(2,1)S(1)} %shard_map.59), channel_id=1, source_target_pairs={{0,1},{1,0},{2,3},{3,2},{4,5},{5,4},{6,7},{7,6},{8,9},{9,8},{10,11... | collective-permute-start | bytes 1179656 | tf_op jit(solution)/shard_map/ppermute | solution.py:17
  62.3 10.1 %collective-permute-start.16 = (bf16[64,768]{1,0:T(8,128)(2,1)S(1)}, bf16[64,768]{1,0:T(8,128)(2,1)S(1)}, u32[]{:S(2)}, u32[]{:S(2)}) collective-permute-start(bf16[64,768]{1,0:T(8,128)(2,1)S(1)} %get-tuple-element.28), channel_id=1, source_target_pairs={{0,2},{1,3},{2,0},{3,1},{4,6},{5,7},{6,4},{7,5},{8,10},{9,11},{10,... | collective-permute-start | bytes 294920 | tf_op jit(solution)/shard_map/ppermute | solution.py:17
  65.0 7.4 %collective-permute-start.17 = (bf16[64,768]{1,0:T(8,128)(2,1)S(1)}, bf16[64,768]{1,0:T(8,128)(2,1)S(1)}, u32[]{:S(2)}, u32[]{:S(2)}) collective-permute-start(bf16[64,768]{1,0:T(8,128)(2,1)S(1)} %get-tuple-element.29), channel_id=1, source_target_pairs={{0,3},{1,2},{2,1},{3,0},{4,7},{5,6},{6,5},{7,4},{8,11},{9,10},{10,... | collective-permute-start | bytes 294920 | tf_op jit(solution)/shard_map/ppermute | solution.py:17
  68.9 4.7 %collective-permute-start.10 = (bf16[64,768]{1,0:T(8,128)(2,1)S(1)}, bf16[64,768]{1,0:T(8,128)(2,1)S(1)}, u32[]{:S(2)}, u32[]{:S(2)}) collective-permute-start(bf16[64,768]{1,0:T(8,128)(2,1)S(1)} %get-tuple-element.25), channel_id=1, source_target_pairs={{0,4},{4,0},{8,12},{12,8},{1,5},{5,1},{9,13},{13,9},{2,6},{6,2},{1... | collective-permute-start | bytes 294920 | tf_op jit(solution)/shard_map/ppermute | solution.py:17
  70.6 5.6 %collective-permute-start.12 = (bf16[64,768]{1,0:T(8,128)(2,1)S(1)}, bf16[64,768]{1,0:T(8,128)(2,1)S(1)}, u32[]{:S(2)}, u32[]{:S(2)}) collective-permute-start(bf16[64,768]{1,0:T(8,128)(2,1)S(1)} %get-tuple-element.26), channel_id=1, source_target_pairs={{0,12},{4,8},{8,4},{12,0},{1,13},{5,9},{9,5},{13,1},{2,14},{6,10},... | collective-permute-start | bytes 294920 | tf_op jit(solution)/shard_map/ppermute | solution.py:17
  72.1 5.1 %collective-permute-start.11 = (bf16[64,768]{1,0:T(8,128)(2,1)S(1)}, bf16[64,768]{1,0:T(8,128)(2,1)S(1)}, u32[]{:S(2)}, u32[]{:S(2)}) collective-permute-start(bf16[64,768]{1,0:T(8,128)(2,1)S(1)} %get-tuple-element.27), channel_id=1, source_target_pairs={{0,8},{4,12},{8,0},{12,4},{1,9},{5,13},{9,1},{13,5},{2,10},{6,14},... | collective-permute-start | bytes 294920 | tf_op jit(solution)/shard_map/ppermute | solution.py:17

commit v4 on v3

v4 whole, which is shorter than its diff:
```python
import functools

import jax
import jax.numpy as jnp
from jax import lax
from jax.experimental import pallas as pl
from jax.experimental.pallas import tpu as pltpu
from jax.sharding import PartitionSpec as P


SEND_CAP = 21
LANES = 128


def hop(value, axis, k):
    n = lax.axis_size(axis)
    return lax.ppermute(value, axis, [(i, i ^ k) for i in range(n)])


def up_to(value, multiple):
    return -(-value // multiple) * multiple


def call(body, ins, outs, scratch, limit, flops=0, moved=0, aliases=()):
    return pl.pallas_call(
        body,
        in_specs=[pl.BlockSpec(memory_space=space) for _, space in ins],
        out_specs=[pl.BlockSpec(memory_space=pltpu.VMEM) for _ in outs],
        out_shape=outs,
        scratch_shapes=scratch,
        input_output_aliases=dict(aliases),
        compiler_params=pltpu.CompilerParams(vmem_limit_bytes=limit << 20),
        cost_estimate=pl.CostEstimate(flops=flops, bytes_accessed=moved, transcendentals=0),
    )(*[value for value, _ in ins])


def route_kernel(topk, place, ids, route, w_up, out, weights, sem):
    copy = pltpu.make_async_copy(w_up.at[0], weights, sem)
    copy.start()
    tok = ids.shape[1]
    rows = up_to(3 * topk, 16)
    weight = route[...]
    norm = weight / jnp.sum(weight, axis=0, keepdims=True)
    high = norm.astype(jnp.bfloat16).astype(jnp.float32)
    info = jnp.concatenate([ids[...].astype(jnp.float32), high, norm - high], axis=0)
    info = jnp.concatenate([info, jnp.zeros((rows - 3 * topk, tok), jnp.float32)], axis=0)
    info = jnp.concatenate([info, jnp.zeros((rows, out.shape[1] - tok), jnp.float32)], axis=1)
    out[...] = jnp.zeros(out.shape, out.dtype)
    out[:rows, :] = info.astype(jnp.bfloat16)
    copy.wait()


def fetch_kernel(lo, w_ref, after, place, *refs):
    outs, sem = refs[:-1], refs[-1]
    copies = [
        pltpu.make_async_copy(w_ref.at[lo + i], out, sem.at[i]) for i, out in enumerate(outs)
    ]
    for copy in copies:
        copy.start()
    for copy in copies:
        copy.wait()


def fetch(w, lo, hi, after, place):
    return call(
        functools.partial(fetch_kernel, lo),
        [(w, pltpu.HBM), (after, pltpu.HBM), (place, pltpu.SMEM)], [pltpu.VMEM(w.shape[1:], w.dtype)] * (hi - lo),
        [pltpu.SemaphoreType.DMA((hi - lo,))], 20, moved=2 * w[0].size * (hi - lo),
    )


def route_rows(info, n_loc, rows, topk, first_expert, pick, pick_t, row_w):
    tokens = pick.shape[1]
    info = info.astype(jnp.float32)
    ids = info[:topk]
    weights = info[topk:2 * topk] + info[2 * topk:3 * topk]
    earlier = (
        lax.broadcasted_iota(jnp.int32, (tokens, tokens), 0)
        < lax.broadcasted_iota(jnp.int32, (tokens, tokens), 1)
    ).astype(jnp.float32).astype(jnp.bfloat16)
    slot_of_row = lax.broadcasted_iota(jnp.int32, (rows, tokens), 0).astype(jnp.float32)
    for e in range(n_loc):
        here = (ids == (first_expert + e).astype(jnp.float32)).astype(jnp.float32)
        mask = jnp.sum(here, axis=0, keepdims=True)
        gain = jnp.sum(here * weights, axis=0, keepdims=True)
        before = jnp.dot(
            jnp.broadcast_to(mask, (16, tokens)).astype(jnp.bfloat16), earlier,
            preferred_element_type=jnp.float32,
        )
        chosen = jnp.where((slot_of_row == before[:1]) & (mask > 0.5), 1.0, 0.0)
        pick[e * rows:(e + 1) * rows, :] = chosen.astype(jnp.bfloat16)
        row_w[e * rows:(e + 1) * rows, :] = jnp.sum(chosen * gain, axis=1, keepdims=True)
    pick_t[...] = jnp.transpose(pick[...].astype(jnp.float32)).astype(jnp.bfloat16)


def piece(e, ff, slice_d):
    per = ff // slice_d
    return slice(e // per * ff, (e // per + 1) * ff), slice(e % per * slice_d, (e % per + 1) * slice_d)


def slice_copies(place, j, slice_d, w_down, ahead, sem):
    n_loc, ff, _ = w_down.shape
    at = pl.multiple_of((place[0] ^ j) * slice_d, LANES)
    return [
        pltpu.make_async_copy(
            w_down.at[e, :, pl.ds(at, slice_d)], ahead.at[piece(e, ff, slice_d)], sem.at[e]
        )
        for e in range(n_loc)
    ]


def down_rows(hidden, weight, row_w, at, high, low):
    result = jnp.dot(hidden[at, :], weight, preferred_element_type=jnp.float32)
    result = result * row_w[at, :]
    upper = result.astype(jnp.bfloat16)
    high[at, :] = upper
    low[at, :] = (result - upper.astype(jnp.float32)).astype(jnp.bfloat16)


def combine(pick_t, high, low):
    total = jnp.dot(pick_t[...], high[...], preferred_element_type=jnp.float32)
    return total + jnp.dot(pick_t[...], low[...], preferred_element_type=jnp.float32)


def down_slice(weights, hidden, pick_t, row_w, rows, n_loc, slice_d, high, low):
    for e in range(n_loc):
        at = slice(e * rows, (e + 1) * rows)
        weight = weights[piece(e, hidden.shape[1], slice_d)]
        down_rows(hidden, weight, row_w, at, high, low)
    return combine(pick_t, high, low)


def up_kernel(sizes, place, *refs):
    n_exp, n_seg, n_loc, rows, tok, slice_d, tile_f, topk, n_held = sizes
    far = n_seg - 2
    near, refs = refs[:2], refs[2:]
    blocks, refs = refs[:n_exp], refs[n_exp:]
    w_held, refs = refs[:n_held], refs[n_held:]
    (w_up, w_down), refs = refs[:2], refs[2:]
    outs, refs = refs[:n_exp], refs[n_exp:]
    (hidden, pick_t, row_w), room, refs = refs[:3], refs[3:3 + n_held], refs[3 + n_held:]
    pick, joined, packed, buf_u, sem_u, sem_a, high, low = refs
    per = w_up.shape[2] // tile_f
    tiles = (n_loc - n_held) * per
    deep_u = buf_u.shape[0]

    def tile_u(t):
        cols = pl.ds(pl.multiple_of(lax.rem(t, per) * tile_f, LANES), tile_f)
        slot = lax.rem(t, deep_u)
        return pltpu.make_async_copy(
            w_up.at[n_held + lax.div(t, per), :, cols], buf_u.at[slot], sem_u.at[slot]
        )

    for t in range(min(deep_u, tiles)):
        tile_u(jnp.int32(t)).start()
    wide = far * slice_d
    for k in range(n_exp):
        joined[k * tok:(k + 1) * tok, :] = blocks[k][:, :wide]
    info = jnp.concatenate([x[:up_to(3 * topk, 16), wide:wide + tok] for x in blocks], axis=1)
    route_rows(info, n_loc, rows, topk, place[1] * n_loc, pick, pick_t, row_w)
    for j in range(n_seg):
        x = near[j][...] if j < 2 else joined[:, (j - 2) * slice_d:(j - 1) * slice_d]
        part = jnp.dot(pick[...], x, preferred_element_type=jnp.float32)
        at = pl.multiple_of((place[0] ^ j) * slice_d, LANES)
        packed[:, pl.ds(at, slice_d)] = part.astype(jnp.bfloat16)

    def up(at, f, weight):
        value = jnp.dot(packed[at, :], weight, preferred_element_type=jnp.float32)
        value = value / (1.0 + jnp.exp(-value))
        cols = pl.ds(pl.multiple_of(f * tile_f, LANES), tile_f)
        hidden[at, cols] = value.astype(jnp.bfloat16)

    slices = list(range(2, n_seg)) + [1]
    copies = [
        slice_copies(place, j, slice_d, w_down, room[i], sem_a.at[i]) for i, j in enumerate(slices)
    ]
    for e, held in enumerate(w_held):
        def from_held(f, carry, e=e, held=held):
            cols = pl.ds(pl.multiple_of(f * tile_f, LANES), tile_f)
            up(slice(e * rows, (e + 1) * rows), f, held[:, cols])
            return carry

        lax.fori_loop(0, per, from_held, 0)
        for copy in copies[e]:
            copy.start()

    def from_ring(t, carry):
        tile_u(t).wait()
        at = pl.ds(pl.multiple_of((n_held + lax.div(t, per)) * rows, 16), rows)
        up(at, lax.rem(t, per), buf_u[lax.rem(t, deep_u)])

        @pl.when(t + deep_u < tiles)
        def _():
            tile_u(t + deep_u).start()

        return carry

    lax.fori_loop(0, tiles, from_ring, 0)
    for i in range(far):
        for copy in copies[i]:
            copy.wait()
        total = down_slice(room[i], hidden, pick_t, row_w, rows, n_loc, slice_d, high, low)
        total = total.astype(jnp.bfloat16)
        for k, out in enumerate(outs):
            out[:, i * slice_d:(i + 1) * slice_d] = total[k * tok:(k + 1) * tok]
    for copy in copies[far]:
        copy.wait()


def down_kernel(rows, n_loc, hidden, pick_t, row_w, weights, out, high, low):
    total = down_slice(weights, hidden, pick_t, row_w, rows, n_loc, out.shape[1], high, low)
    out[...] = total.astype(out.dtype)


def own_kernel(rows, place, hidden, pick_t, row_w, w_down, out, buf, sem, high, low):
    n_loc = w_down.shape[0]
    at = pl.multiple_of(place[0] * out.shape[1], LANES)
    copies = [
        pltpu.make_async_copy(w_down.at[e, :, pl.ds(at, out.shape[1])], buf.at[e], sem.at[e])
        for e in range(n_loc)
    ]
    for copy in copies:
        copy.start()
    for e, copy in enumerate(copies):
        copy.wait()
        down_rows(hidden, buf[e], row_w, slice(e * rows, (e + 1) * rows), high, low)
    out[...] = combine(pick_t, high, low).astype(out.dtype)


def down_scratch(n_loc, rows, ff, slice_d, deep):
    bf16 = jnp.bfloat16
    return [
        pltpu.VMEM((deep, ff, slice_d), bf16), pltpu.SemaphoreType.DMA((deep,)),
        pltpu.VMEM((n_loc * rows, slice_d), bf16), pltpu.VMEM((n_loc * rows, slice_d), bf16),
    ]


def experts_up(place, near, blocks, w_held, w_up, w_down, topk):
    n_exp, n_seg = len(blocks), lax.axis_size("seg")
    n_loc, ff, width = w_down.shape
    tok = blocks[0].shape[0]
    tokens, slice_d = near[0].shape
    rows = up_to(SEND_CAP * n_exp, 16)
    tile_f = ff // 3
    wide = (n_seg - 2) * slice_d
    sizes = (n_exp, n_seg, n_loc, rows, tok, slice_d, tile_f, topk, len(w_held))
    bf16 = jnp.bfloat16
    vmem = lambda values: [(value, pltpu.VMEM) for value in values]
    outs = call(
        functools.partial(up_kernel, sizes),
        [(place, pltpu.SMEM)] + vmem(near) + vmem(blocks) + vmem(w_held)
        + [(w_up, pltpu.HBM), (w_down, pltpu.HBM)],
        [jax.ShapeDtypeStruct((tok, wide), bf16)] * n_exp
        + [jax.ShapeDtypeStruct((n_loc * rows, ff), bf16),
           jax.ShapeDtypeStruct((tokens, n_loc * rows), bf16),
           jax.ShapeDtypeStruct((n_loc * rows, 1), jnp.float32)]
        + [pltpu.VMEM(w.shape, bf16) for w in w_held],
        [pltpu.VMEM((n_loc * rows, tokens), bf16),
         pltpu.VMEM((tokens, wide), bf16),
         pltpu.VMEM((n_loc * rows, width), bf16),
         pltpu.VMEM((3, width, tile_f), bf16),
         pltpu.SemaphoreType.DMA((3,)),
         pltpu.SemaphoreType.DMA((len(w_held), n_loc)),
         pltpu.VMEM((n_loc * rows, slice_d), bf16), pltpu.VMEM((n_loc * rows, slice_d), bf16)],
        15, flops=2 * n_loc * 256 * width * ff, moved=n_loc * ff * width * 2,
        aliases=[(3 + n_exp + i, n_exp + 3 + i) for i in range(len(w_held))],
    )
    return outs[:n_exp], outs[n_exp:n_exp + 3], outs[n_exp + 3:]


def experts_down(held, weights, n_loc, slice_d, dtype):
    hidden, pick_t, row_w = held
    rows, ff = hidden.shape[0] // n_loc, hidden.shape[1]
    bf16 = jnp.bfloat16
    return call(
        functools.partial(down_kernel, rows, n_loc),
        [(x, pltpu.VMEM) for x in (hidden, pick_t, row_w, weights)],
        [jax.ShapeDtypeStruct((pick_t.shape[0], slice_d), dtype)],
        [pltpu.VMEM((n_loc * rows, slice_d), bf16), pltpu.VMEM((n_loc * rows, slice_d), bf16)],
        16, flops=2 * n_loc * 256 * slice_d * ff,
    )[0]


def experts_own(place, held, w_down, slice_d):
    hidden, pick_t, row_w = held
    n_loc, ff, _ = w_down.shape
    rows = hidden.shape[0] // n_loc
    return call(
        functools.partial(own_kernel, rows),
        [(place, pltpu.SMEM)] + [(x, pltpu.VMEM) for x in (hidden, pick_t, row_w)]
        + [(w_down, pltpu.HBM)],
        [jax.ShapeDtypeStruct((pick_t.shape[0], slice_d), jnp.float32)],
        down_scratch(n_loc, rows, ff, slice_d, n_loc),
        16, flops=2 * n_loc * 256 * slice_d * ff, moved=2 * n_loc * ff * slice_d,
    )[0]


def total_of(parts):
    total = parts[0].astype(jnp.float32)
    for part in parts[1:]:
        total = total + part.astype(jnp.float32)
    return total


def staged(tokens, expert_ids, route_weight, w_up, w_down):
    n_exp = lax.axis_size("expert")
    n_seg = lax.axis_size("seg")
    tok, slice_d = tokens.shape
    topk = expert_ids.shape[1]
    far = range(2, n_seg)
    peers = range(1, n_exp)
    place = jnp.stack([lax.axis_index("seg"), lax.axis_index("expert")]).astype(jnp.int32)

    a = [hop(tokens, "seg", k) for k in far]
    b = [tokens] + [hop(tokens, "expert", k) for k in peers]
    route, held_0 = call(
        functools.partial(route_kernel, topk),
        [(place, pltpu.SMEM), (expert_ids.T, pltpu.VMEM), (route_weight.T, pltpu.VMEM),
         (w_up, pltpu.HBM)],
        [jax.ShapeDtypeStruct((tok, LANES), tokens.dtype), pltpu.VMEM(w_up.shape[1:], w_up.dtype)],
        [pltpu.SemaphoreType.DMA], 20,
    )
    near = jnp.concatenate(b, axis=0)
    e = hop(near, "seg", 1)
    block = jnp.concatenate(a + [route], axis=1)
    blocks = [block] + [hop(block, "expert", k) for k in peers]
    w_held = [held_0, *fetch(w_up, 1, n_seg - 1, block, place)]

    c, held, ahead = experts_up(place, [near, e], blocks, w_held, w_up, w_down, topk)
    c = [c[0]] + [hop(c[k], "expert", k) for k in peers]
    n_loc = w_up.shape[0]
    g = hop(experts_down(held, ahead[-1], n_loc, slice_d, jnp.bfloat16), "seg", 1)
    own = experts_own(place, held, w_down, slice_d)
    total = total_of(c).astype(jnp.bfloat16)
    sent = [total[:, (k - 2) * slice_d:(k - 1) * slice_d] for k in far]
    d = [hop(x, "seg", k) for x, k in zip(sent, far)]
    own = total_of([own, g])
    mine = own[:tok]
    own = own.astype(jnp.bfloat16)
    h = [hop(own[k * tok:(k + 1) * tok], "expert", k) for k in peers]
    return total_of([mine] + h + d).astype(jnp.bfloat16)


def plain(tokens, expert_ids, route_weight, w_up, w_down):
    n_exp = lax.axis_size("expert")
    exp_local, width = w_up.shape[:2]
    n_experts = n_exp * exp_local
    topk = expert_ids.shape[1]
    tok_rows, width_seg = tokens.shape
    flat = expert_ids.reshape(-1)
    onehot = (flat[:, None] == jnp.arange(n_experts, dtype=jnp.int32)[None, :]).astype(jnp.int32)
    before = jnp.cumsum(onehot, axis=0) - onehot
    target = flat * SEND_CAP + jnp.sum(before * onehot, axis=1)
    norm_weight = route_weight / jnp.sum(route_weight, axis=1, keepdims=True)
    buffer = jnp.zeros((n_experts * SEND_CAP, width_seg), tokens.dtype)
    packed = buffer.at[target].set(jnp.repeat(tokens, topk, axis=0))
    packed = packed.reshape(n_exp, exp_local * SEND_CAP, width_seg)
    arrived = lax.all_to_all(packed, "expert", split_axis=0, concat_axis=0, tiled=True)
    piece = lax.all_gather(arrived, "seg", axis=2, tiled=True)
    block = piece.reshape(n_exp, exp_local, SEND_CAP, width)
    up_sum = jnp.einsum("sekd,edf->eskf", block, w_up, preferred_element_type=jnp.float32)
    hidden = jax.nn.silu(up_sum).astype(jnp.bfloat16)
    partial_out = jnp.einsum("eskf,efd->sekd", hidden, w_down, preferred_element_type=jnp.float32)
    partial_out = partial_out.reshape(n_exp, exp_local * SEND_CAP, width)
    returned = lax.all_to_all(partial_out, "expert", split_axis=0, concat_axis=0, tiled=True)
    picked = returned.reshape(n_experts * SEND_CAP, width)[target]
    weighted = (picked * norm_weight.reshape(-1)[:, None]).reshape(tok_rows, topk, width).sum(axis=1)
    return lax.psum_scatter(weighted, "seg", scatter_dimension=1, tiled=True).astype(jnp.bfloat16)


def shards(tokens, expert_ids, route_weight, w_up, w_down):
    n_exp, n_seg = lax.axis_size("expert"), lax.axis_size("seg")
    n_loc, ff, width = w_down.shape
    slice_d = tokens.shape[1]
    paired = n_exp & (n_exp - 1) == 0 and n_seg & (n_seg - 1) == 0
    room = n_loc >= n_seg > 2 and n_loc * slice_d <= width and ff % (3 * LANES) == 0
    if not (paired and room and slice_d % LANES == 0 and ff % slice_d == 0):
        return plain(tokens, expert_ids, route_weight, w_up, w_down)
    return staged(tokens, expert_ids, route_weight, w_up, w_down)


def solution(mesh):
    placed = (
        P(("dp", "expert"), "seg"),
        P(("dp", "expert"), None),
        P(("dp", "expert"), None),
        P("expert", None, "seg"),
        P("expert", "seg", None),
    )
    return jax.shard_map(
        shards, mesh=mesh, in_specs=placed, out_specs=P(("dp", "expert"), "seg"), check_vma=False
    )
```

time: 78.1 us -> 69.5 us (0.89)
  Pallas kernels: 36.7 us -> 32.9 us
  waiting for transfers between devices: 12.2 us -> 9 us
    pallas_call x5, Pallas kernels: 36.7 us -> 32.9 us  [call(): pl.pallas_call(body, in_specs=[pl.BlockSpec(memory_space=space) for _, sp...]
    ppermute x18, waiting for transfers between devices: 12.2 us -> 9 us  [hop(): return lax.ppermute(value, axis, [(i, i ^ k) for i in range(n)])]
    slice x8 -> x0, local copies, waits for them, and re-layouts: 1.61 us -> none  [the longest x4 0.92 us: staged(): near = jnp.concatenate([x[:tok] for x in b], axis=0)]
    unnamed x3 -> x11, local copies, waits for them, and re-layouts: 0.01 us -> 1.41 us
  transfers between devices with their start and end apart: 18 -> 18, of which waited for: 9 -> 9; matrix products, arithmetic and copies ran while one was open for 3% -> 1% of each run, Pallas kernels for 22% -> 27%
where the time goes in v4:
time: 69.5 us; the launch traced here: 69.4 us
  Pallas kernels  32.9 us (47%)
  starting transfers between devices  24.8 us (36%)
  waiting for transfers between devices  9 us (13%)
  local copies, waits for them, and re-layouts  1.47 us (2%)
  other arithmetic  0.98 us (1%)
    pallas_call x5, Pallas kernels, call(): pl.pallas_call(body, in_specs=[pl.BlockSpec(memory_space=space) for _, sp...  32.9 us
    ppermute x18, starting transfers between devices, hop(): return lax.ppermute(value, axis, [(i, i ^ k) for i in range(n)])  24.8 us
    ppermute x18, waiting for transfers between devices, hop(): return lax.ppermute(value, axis, [(i, i ^ k) for i in range(n)])  9 us
    unnamed x11, local copies, waits for them, and re-layouts  1.41 us
  transfers between devices with their start and end apart: 18, of which 9 were waited for; matrix products, arithmetic and copies ran while one was open for 1% of the time, Pallas kernels for 27%

profile of v4, /device:TPU:0, one launch (start us, length us, event | category | flops | bytes accessed | tf_op | source)
XLA Modules:
  0.0 69.4 jit_solution(4769713066060893635)
XLA Ops:
  0.0 3.9 %collective-permute-start.2 = (bf16[64,768]{1,0:T(8,128)(2,1)}, bf16[64,768]{1,0:T(8,128)(2,1)S(1)}, u32[]{:S(2)}, u32[]{:S(2)}) collective-permute-start(bf16[64,768]{1,0:T(8,128)(2,1)} %param.5), channel_id=1, source_target_pairs={{0,12},{4,8},{8,4},{12,0},{1,13},{5,9},{9,5},{13,1},{2,14},{6,10},... | collective-permute-start | bytes 294920 | tf_op jit(solution)/shard_map/ppermute | solution.py:17
  3.9 0.5 collective-permute-start.1
  4.4 0.1 collective-permute-start
  4.5 4.1 %collective-permute-start.5 = (bf16[64,768]{1,0:T(8,128)(2,1)}, bf16[64,768]{1,0:T(8,128)(2,1)S(1)}, u32[]{:S(2)}, u32[]{:S(2)}) collective-permute-start(bf16[64,768]{1,0:T(8,128)(2,1)} %param.5), channel_id=1, source_target_pairs={{0,3},{1,2},{2,1},{3,0},{4,7},{5,6},{6,5},{7,4},{8,11},{9,10},{10,... | collective-permute-start | bytes 294920 | tf_op jit(solution)/shard_map/ppermute | solution.py:17
  8.6 0.0 collective-permute-start.4
  8.6 0.1 pad_add_fusion.place
  8.6 0.7 copy-done
  9.3 0.7 copy-done.1
  10.0 4.2 %shard_map.55 = (bf16[64,128]{1,0:T(8,128)(2,1)S(1)}, bf16[3072,1536]{1,0:T(8,128)(2,1)S(1)}) custom-call(s32[2]{0:T(128)S(1)} %pad_add_fusion.place, s32[4,64]{1,0:T(4,128)S(1)} %bitcast.4, f32[4,64]{1,0:T(4,128)S(1)} %bitcast.5, bf16[4,3072,1536]{2,1,0:T(8,128)(2,1)} %refs_9_.1), custom_call_target="tpu_custom_call" | custom-call | tf_op jit(solution)/shard_map/pallas_call | solution.py:25
  14.2 0.0 copy-done.2
  14.3 0.0 collective-permute-done
  14.3 0.0 collective-permute-done.1
  14.3 0.0 collective-permute-done.2
  14.4 0.6 collective-permute-start.3
  15.0 1.3 %collective-permute-done.4 = bf16[64,768]{1,0:T(8,128)(2,1)S(1)} collective-permute-done((bf16[64,768]{1,0:T(8,128)(2,1)}, bf16[64,768]{1,0:T(8,128)(2,1)S(1)}, u32[]{:S(2)}, u32[]{:S(2)}) %collective-permute-start.4) | collective-permute-done | bytes 98336 | tf_op jit(solution)/shard_map/ppermute | solution.py:17
  16.3 0.0 collective-permute-done.5
  16.3 2.5 %collective-permute-start.8 = (bf16[64,1664]{1,0:T(8,128)(2,1)S(1)}, bf16[64,1664]{1,0:T(8,128)(2,1)S(1)}, u32[]{:S(2)}, u32[]{:S(2)}) collective-permute-start(bf16[64,1664]{1,0:T(8,128)(2,1)S(1)} %constant_dynamic-update-slice_fusion.4.after.refs_2_), channel_id=1, source_target_pairs={{0,12},{4,8},{8,4},{12,0},{1,13},{5,9},{9,5},{13,1},{2,14},{6,10},... | collective-permute-start | bytes 638984 | tf_op jit(solution)/shard_map/ppermute | solution.py:17
  18.8 0.5 collective-permute-start.7
  19.3 0.5 collective-permute-start.6
  19.9 6.9 %shard_map.56 = (bf16[3072,1536]{1,0:T(8,128)(2,1)S(1)}, bf16[3072,1536]{1,0:T(8,128)(2,1)S(1)}) custom-call(bf16[4,3072,1536]{2,1,0:T(8,128)(2,1)} %refs_9_.1, bf16[64,1664]{1,0:T(8,128)(2,1)S(1)} %constant_dynamic-update-slice_fusion.4.after.refs_2_, s32[2]{0:T(128)S(1)} %pad_add_fusion.place), custom_call_target="tpu_custom_call" | custom-call | bytes 18874368 | tf_op jit(solution)/shard_map/pallas_call | solution.py:25
  26.8 0.0 collective-permute-done.8.refs_5_
  26.8 1.3 %collective-permute-done.7.refs_4_ = bf16[64,1664]{1,0:T(8,128)(2,1)S(1)} collective-permute-done((bf16[64,1664]{1,0:T(8,128)(2,1)S(1)}, bf16[64,1664]{1,0:T(8,128)(2,1)S(1)}, u32[]{:S(2)}, u32[]{:S(2)}) %collective-permute-start.7) | collective-permute-done | bytes 213024 | tf_op jit(solution)/shard_map/ppermute | solution.py:17
  28.1 0.1 collective-permute-done.6.refs_3_
  28.2 0.0 collective-permute-done.3.refs_1_
  28.2 14.3 %shard_map.57 = (bf16[64,1536]{1,0:T(8,128)(2,1)S(1)}, bf16[64,1536]{1,0:T(8,128)(2,1)S(1)}, bf16[64,1536]{1,0:T(8,128)(2,1)S(1)}, bf16[64,1536]{1,0:T(8,128)(2,...) custom-call(s32[2]{0:T(128)S(1)} %pad_add_fusion.place, ...), custom_call_target="tpu_custom_call", output_to_operand_aliasing={{7}: (7, {}), {8}: (8, {}), {9}: (9, {})} | custom-call | flops 9663676416 | bytes 37748736 | tf_op jit(solution)/shard_map/pallas_call | solution.py:25
  42.5 1.6 %collective-permute-start.13 = (bf16[64,1536]{1,0:T(8,128)(2,1)S(1)}, bf16[64,1536]{1,0:T(8,128)(2,1)S(1)}, u32[]{:S(2)}, u32[]{:S(2)}) collective-permute-start(bf16[64,1536]{1,0:T(8,128)(2,1)S(1)} %get-tuple-element.26), channel_id=1, source_target_pairs={{0,4},{4,0},{8,12},{12,8},{1,5},{5,1},{9,13},{13,9},{2,6},{6,2},{1... | collective-permute-start | bytes 589832 | tf_op jit(solution)/shard_map/ppermute | solution.py:17
  44.1 0.7 %collective-permute-start.14 = (bf16[64,1536]{1,0:T(8,128)(2,1)S(1)}, bf16[64,1536]{1,0:T(8,128)(2,1)S(1)}, u32[]{:S(2)}, u32[]{:S(2)}) collective-permute-start(bf16[64,1536]{1,0:T(8,128)(2,1)S(1)} %get-tuple-element.27), channel_id=1, source_target_pairs={{0,8},{4,12},{8,0},{12,4},{1,9},{5,13},{9,1},{13,5},{2,10},{6,14},... | collective-permute-start | bytes 589832 | tf_op jit(solution)/shard_map/ppermute | solution.py:17
  44.8 1.3 %collective-permute-start.15 = (bf16[64,1536]{1,0:T(8,128)(2,1)S(1)}, bf16[64,1536]{1,0:T(8,128)(2,1)S(1)}, u32[]{:S(2)}, u32[]{:S(2)}) collective-permute-start(bf16[64,1536]{1,0:T(8,128)(2,1)S(1)} %get-tuple-element.28), channel_id=1, source_target_pairs={{0,12},{4,8},{8,4},{12,0},{1,13},{5,9},{9,5},{13,1},{2,14},{6,10},... | collective-permute-start | bytes 589832 | tf_op jit(solution)/shard_map/ppermute | solution.py:17
  46.1 2.1 %shard_map.59 = bf16[256,768]{1,0:T(8,128)(2,1)S(1)} custom-call(bf16[384,1536]{1,0:T(8,128)(2,1)S(1)} %get-tuple-element.21.hidden, bf16[256,384]{1,0:T(8,128)(2,1)S(1)} %get-tuple-element.22.pick_t, f32[384,1]{1,0:T(8,128)S(1)} %get-tuple-element.23.row_w, bf16[3072,1536]{1,0:T(8,128)(2,1)S(1)} %get-tuple-element.24.weights), custom_call_target="tpu_custom_call" | custom-call | flops 2415919104 | tf_op jit(solution)/shard_map/pallas_call | solution.py:25
  48.1 0.1 collective-permute-start.9
  48.2 5.4 %shard_map.58 = f32[256,768]{1,0:T(8,128)S(1)} custom-call(s32[2]{0:T(128)S(1)} %pad_add_fusion.place, bf16[384,1536]{1,0:T(8,128)(2,1)S(1)} %get-tuple-element.21.hidden, bf16[256,384]{1,0:T(8,128)(2,1)S(1)} %get-tuple-element.22.pick_t, f32[384,1]{1,0:T(8,128)S(1)} %get-tuple-element.23.row_w, bf16[4,1536,3072]{2,1,0:T(8,128)(2,1)} %w_down.1), custom_call_target="tpu_custom_call" | custom-call | flops 2415919104 | bytes 9437184 | tf_op jit(solution)/shard_map/pallas_call | solution.py:25
  53.6 0.0 collective-permute-done.13
  53.6 1.1 %collective-permute-done.14 = bf16[64,1536]{1,0:T(8,128)(2,1)S(1)} collective-permute-done((bf16[64,1536]{1,0:T(8,128)(2,1)S(1)}, bf16[64,1536]{1,0:T(8,128)(2,1)S(1)}, u32[]{:S(2)}, u32[]{:S(2)}) %collective-permute-start.14) | collective-permute-done | bytes 196640 | tf_op jit(solution)/shard_map/ppermute | solution.py:17
  54.7 0.0 collective-permute-done.15
  54.7 0.1 add_convert_fusion
  54.9 1.1 %collective-permute-start.16 = (bf16[64,768]{1,0:T(8,128)(2,1)S(1)}, bf16[64,768]{1,0:T(8,128)(2,1)S(1)}, u32[]{:S(2)}, u32[]{:S(2)}) collective-permute-start(bf16[64,768]{1,0:T(8,128)(2,1)S(1)} %get-tuple-element.34), channel_id=1, source_target_pairs={{0,2},{1,3},{2,0},{3,1},{4,6},{5,7},{6,4},{7,5},{8,10},{9,11},{10,... | collective-permute-start | bytes 294920 | tf_op jit(solution)/shard_map/ppermute | solution.py:17
  56.0 2.2 %collective-permute-start.17 = (bf16[64,768]{1,0:T(8,128)(2,1)S(1)}, bf16[64,768]{1,0:T(8,128)(2,1)S(1)}, u32[]{:S(2)}, u32[]{:S(2)}) collective-permute-start(bf16[64,768]{1,0:T(8,128)(2,1)S(1)} %get-tuple-element.35), channel_id=1, source_target_pairs={{0,3},{1,2},{2,1},{3,0},{4,7},{5,6},{6,5},{7,4},{8,11},{9,10},{10,... | collective-permute-start | bytes 294920 | tf_op jit(solution)/shard_map/ppermute | solution.py:17
  58.2 0.2 collective-permute-done.9
  58.4 0.1 fusion.5
  58.5 3.6 %collective-permute-start.10 = (bf16[64,768]{1,0:T(8,128)(2,1)S(1)}, bf16[64,768]{1,0:T(8,128)(2,1)S(1)}, u32[]{:S(2)}, u32[]{:S(2)}) collective-permute-start(bf16[64,768]{1,0:T(8,128)(2,1)S(1)} %get-tuple-element.31), channel_id=1, source_target_pairs={{0,4},{4,0},{8,12},{12,8},{1,5},{5,1},{9,13},{13,9},{2,6},{6,2},{1... | collective-permute-start | bytes 294920 | tf_op jit(solution)/shard_map/ppermute | solution.py:17
  62.1 1.5 %collective-permute-start.12 = (bf16[64,768]{1,0:T(8,128)(2,1)S(1)}, bf16[64,768]{1,0:T(8,128)(2,1)S(1)}, u32[]{:S(2)}, u32[]{:S(2)}) collective-permute-start(bf16[64,768]{1,0:T(8,128)(2,1)S(1)} %get-tuple-element.32), channel_id=1, source_target_pairs={{0,12},{4,8},{8,4},{12,0},{1,13},{5,9},{9,5},{13,1},{2,14},{6,10},... | collective-permute-start | bytes 294920 | tf_op jit(solution)/shard_map/ppermute | solution.py:17
  63.6 0.0 collective-permute-start.11
  63.6 0.3 collective-permute-done.16
  63.9 0.0 collective-permute-done.17
  64.0 0.7 %collective-permute-done.10 = bf16[64,768]{1,0:T(8,128)(2,1)S(1)} collective-permute-done((bf16[64,768]{1,0:T(8,128)(2,1)S(1)}, bf16[64,768]{1,0:T(8,128)(2,1)S(1)}, u32[]{:S(2)}, u32[]{:S(2)}) %collective-permute-start.10) | collective-permute-done | bytes 98336 | tf_op jit(solution)/shard_map/ppermute | solution.py:17
  64.7 3.0 %collective-permute-done.12 = bf16[64,768]{1,0:T(8,128)(2,1)S(1)} collective-permute-done((bf16[64,768]{1,0:T(8,128)(2,1)S(1)}, bf16[64,768]{1,0:T(8,128)(2,1)S(1)}, u32[]{:S(2)}, u32[]{:S(2)}) %collective-permute-start.12) | collective-permute-done | bytes 98336 | tf_op jit(solution)/shard_map/ppermute | solution.py:17
  67.6 1.0 %collective-permute-done.11 = bf16[64,768]{1,0:T(8,128)(2,1)S(1)} collective-permute-done((bf16[64,768]{1,0:T(8,128)(2,1)S(1)}, bf16[64,768]{1,0:T(8,128)(2,1)S(1)}, u32[]{:S(2)}, u32[]{:S(2)}) %collective-permute-start.11) | collective-permute-done | bytes 98336 | tf_op jit(solution)/shard_map/ppermute | solution.py:17
  68.6 0.7 %fusion.4 = bf16[64,768]{1,0:T(8,128)(2,1)} fusion(f32[256,768]{1,0:T(8,128)S(1)} %get-tuple-element.30, bf16[64,768]{1,0:T(8,128)(2,1)S(1)} %collective-permute-done.17, bf16[64,768]{1,0:T(8,128)(2,1)S(1)} %collective-permute-done.16, bf16[64,768]{1,0:T(8,128)(2,1)S(1)} %collective-permute-done.12, bf16[64,768]{1,0:T(8,128)(2,1)S(1)} %collective-permute-done.11, ...), kind=kLoop, calls=%fused_computation.7 | loop fusion | flops 540672 | bytes 786432 | tf_op jit(solution)/shard_map/convert_element_type | solution.py:341
  (12 shorter events, 0.1 us)
Async XLA Ops:
  0.0 14.3 %collective-permute-start.2 = (bf16[64,768]{1,0:T(8,128)(2,1)}, bf16[64,768]{1,0:T(8,128)(2,1)S(1)}, u32[]{:S(2)}, u32[]{:S(2)}) collective-permute-start(bf16[64,768]{1,0:T(8,128)(2,1)} %param.5), channel_id=1, source_target_pairs={{0,12},{4,8},{8,4},{12,0},{1,13},{5,9},{9,5},{13,1},{2,14},{6,10},... | collective-permute-start | bytes 294920 | tf_op jit(solution)/shard_map/ppermute | solution.py:17
  3.9 10.4 %collective-permute-start.1 = (bf16[64,768]{1,0:T(8,128)(2,1)}, bf16[64,768]{1,0:T(8,128)(2,1)S(1)}, u32[]{:S(2)}, u32[]{:S(2)}) collective-permute-start(bf16[64,768]{1,0:T(8,128)(2,1)} %param.5), channel_id=1, source_target_pairs={{0,8},{4,12},{8,0},{12,4},{1,9},{5,13},{9,1},{13,5},{2,10},{6,14},... | collective-permute-start | bytes 294920 | tf_op jit(solution)/shard_map/ppermute | solution.py:17
  4.4 9.8 %collective-permute-start = (bf16[64,768]{1,0:T(8,128)(2,1)}, bf16[64,768]{1,0:T(8,128)(2,1)S(1)}, u32[]{:S(2)}, u32[]{:S(2)}) collective-permute-start(bf16[64,768]{1,0:T(8,128)(2,1)} %param.5), channel_id=1, source_target_pairs={{0,4},{4,0},{8,12},{12,8},{1,5},{5,1},{9,13},{13,9},{2,6},{6,2},{1... | collective-permute-start | bytes 294920 | tf_op jit(solution)/shard_map/ppermute | solution.py:17
  4.5 11.8 %collective-permute-start.5 = (bf16[64,768]{1,0:T(8,128)(2,1)}, bf16[64,768]{1,0:T(8,128)(2,1)S(1)}, u32[]{:S(2)}, u32[]{:S(2)}) collective-permute-start(bf16[64,768]{1,0:T(8,128)(2,1)} %param.5), channel_id=1, source_target_pairs={{0,3},{1,2},{2,1},{3,0},{4,7},{5,6},{6,5},{7,4},{8,11},{9,10},{10,... | collective-permute-start | bytes 294920 | tf_op jit(solution)/shard_map/ppermute | solution.py:17
  8.6 7.7 %collective-permute-start.4 = (bf16[64,768]{1,0:T(8,128)(2,1)}, bf16[64,768]{1,0:T(8,128)(2,1)S(1)}, u32[]{:S(2)}, u32[]{:S(2)}) collective-permute-start(bf16[64,768]{1,0:T(8,128)(2,1)} %param.5), channel_id=1, source_target_pairs={{0,2},{1,3},{2,0},{3,1},{4,6},{5,7},{6,4},{7,5},{8,10},{9,11},{10,... | collective-permute-start | bytes 294920 | tf_op jit(solution)/shard_map/ppermute | solution.py:17
  8.6 0.7 copy-start
  9.3 0.7 copy-start.1
  10.0 4.2 %copy-start.2 = (bf16[64,768]{1,0:T(8,128)(2,1)S(1)}, bf16[64,768]{1,0:T(8,128)(2,1)}, u32[]{:S(2)}) copy-start(bf16[64,768]{1,0:T(8,128)(2,1)} %param.5) | copy-start | bytes 294916
  14.4 13.8 %collective-permute-start.3 = (bf16[256,768]{1,0:T(8,128)(2,1)S(1)}, bf16[256,768]{1,0:T(8,128)(2,1)S(1)}, u32[]{:S(2)}, u32[]{:S(2)}) collective-permute-start(bf16[256,768]{1,0:T(8,128)(2,1)S(1)} %constant_dynamic-update-slice_fusion.refs_0_), channel_id=1, source_target_pairs={{0,1},{1,0},{2,3},{3,2},{4,5},{5,4},{6,7},{7,6},{8,9},{9,8},{10,11... | collective-permute-start | bytes 1179656 | tf_op jit(solution)/shard_map/ppermute | solution.py:17
  16.3 10.5 %collective-permute-start.8 = (bf16[64,1664]{1,0:T(8,128)(2,1)S(1)}, bf16[64,1664]{1,0:T(8,128)(2,1)S(1)}, u32[]{:S(2)}, u32[]{:S(2)}) collective-permute-start(bf16[64,1664]{1,0:T(8,128)(2,1)S(1)} %constant_dynamic-update-slice_fusion.4.after.refs_2_), channel_id=1, source_target_pairs={{0,12},{4,8},{8,4},{12,0},{1,13},{5,9},{9,5},{13,1},{2,14},{6,10},... | collective-permute-start | bytes 638984 | tf_op jit(solution)/shard_map/ppermute | solution.py:17
  18.8 9.3 %collective-permute-start.7 = (bf16[64,1664]{1,0:T(8,128)(2,1)S(1)}, bf16[64,1664]{1,0:T(8,128)(2,1)S(1)}, u32[]{:S(2)}, u32[]{:S(2)}) collective-permute-start(bf16[64,1664]{1,0:T(8,128)(2,1)S(1)} %constant_dynamic-update-slice_fusion.4.after.refs_2_), channel_id=1, source_target_pairs={{0,8},{4,12},{8,0},{12,4},{1,9},{5,13},{9,1},{13,5},{2,10},{6,14},... | collective-permute-start | bytes 638984 | tf_op jit(solution)/shard_map/ppermute | solution.py:17
  19.3 8.9 %collective-permute-start.6 = (bf16[64,1664]{1,0:T(8,128)(2,1)S(1)}, bf16[64,1664]{1,0:T(8,128)(2,1)S(1)}, u32[]{:S(2)}, u32[]{:S(2)}) collective-permute-start(bf16[64,1664]{1,0:T(8,128)(2,1)S(1)} %constant_dynamic-update-slice_fusion.4.after.refs_2_), channel_id=1, source_target_pairs={{0,4},{4,0},{8,12},{12,8},{1,5},{5,1},{9,13},{13,9},{2,6},{6,2},{1... | collective-permute-start | bytes 638984 | tf_op jit(solution)/shard_map/ppermute | solution.py:17
  42.5 11.1 %collective-permute-start.13 = (bf16[64,1536]{1,0:T(8,128)(2,1)S(1)}, bf16[64,1536]{1,0:T(8,128)(2,1)S(1)}, u32[]{:S(2)}, u32[]{:S(2)}) collective-permute-start(bf16[64,1536]{1,0:T(8,128)(2,1)S(1)} %get-tuple-element.26), channel_id=1, source_target_pairs={{0,4},{4,0},{8,12},{12,8},{1,5},{5,1},{9,13},{13,9},{2,6},{6,2},{1... | collective-permute-start | bytes 589832 | tf_op jit(solution)/shard_map/ppermute | solution.py:17
  44.1 10.7 %collective-permute-start.14 = (bf16[64,1536]{1,0:T(8,128)(2,1)S(1)}, bf16[64,1536]{1,0:T(8,128)(2,1)S(1)}, u32[]{:S(2)}, u32[]{:S(2)}) collective-permute-start(bf16[64,1536]{1,0:T(8,128)(2,1)S(1)} %get-tuple-element.27), channel_id=1, source_target_pairs={{0,8},{4,12},{8,0},{12,4},{1,9},{5,13},{9,1},{13,5},{2,10},{6,14},... | collective-permute-start | bytes 589832 | tf_op jit(solution)/shard_map/ppermute | solution.py:17
  44.8 9.9 %collective-permute-start.15 = (bf16[64,1536]{1,0:T(8,128)(2,1)S(1)}, bf16[64,1536]{1,0:T(8,128)(2,1)S(1)}, u32[]{:S(2)}, u32[]{:S(2)}) collective-permute-start(bf16[64,1536]{1,0:T(8,128)(2,1)S(1)} %get-tuple-element.28), channel_id=1, source_target_pairs={{0,12},{4,8},{8,4},{12,0},{1,13},{5,9},{9,5},{13,1},{2,14},{6,10},... | collective-permute-start | bytes 589832 | tf_op jit(solution)/shard_map/ppermute | solution.py:17
  48.1 10.2 %collective-permute-start.9 = (bf16[256,768]{1,0:T(8,128)(2,1)S(1)}, bf16[256,768]{1,0:T(8,128)(2,1)S(1)}, u32[]{:S(2)}, u32[]{:S(2)}) collective-permute-start(bf16[256,768]{1,0:T(8,128)(2,1)S(1)} %shard_map.59), channel_id=1, source_target_pairs={{0,1},{1,0},{2,3},{3,2},{4,5},{5,4},{6,7},{7,6},{8,9},{9,8},{10,11... | collective-permute-start | bytes 1179656 | tf_op jit(solution)/shard_map/ppermute | solution.py:17
  54.9 9.1 %collective-permute-start.16 = (bf16[64,768]{1,0:T(8,128)(2,1)S(1)}, bf16[64,768]{1,0:T(8,128)(2,1)S(1)}, u32[]{:S(2)}, u32[]{:S(2)}) collective-permute-start(bf16[64,768]{1,0:T(8,128)(2,1)S(1)} %get-tuple-element.34), channel_id=1, source_target_pairs={{0,2},{1,3},{2,0},{3,1},{4,6},{5,7},{6,4},{7,5},{8,10},{9,11},{10,... | collective-permute-start | bytes 294920 | tf_op jit(solution)/shard_map/ppermute | solution.py:17
  56.0 8.0 %collective-permute-start.17 = (bf16[64,768]{1,0:T(8,128)(2,1)S(1)}, bf16[64,768]{1,0:T(8,128)(2,1)S(1)}, u32[]{:S(2)}, u32[]{:S(2)}) collective-permute-start(bf16[64,768]{1,0:T(8,128)(2,1)S(1)} %get-tuple-element.35), channel_id=1, source_target_pairs={{0,3},{1,2},{2,1},{3,0},{4,7},{5,6},{6,5},{7,4},{8,11},{9,10},{10,... | collective-permute-start | bytes 294920 | tf_op jit(solution)/shard_map/ppermute | solution.py:17
  58.5 6.2 %collective-permute-start.10 = (bf16[64,768]{1,0:T(8,128)(2,1)S(1)}, bf16[64,768]{1,0:T(8,128)(2,1)S(1)}, u32[]{:S(2)}, u32[]{:S(2)}) collective-permute-start(bf16[64,768]{1,0:T(8,128)(2,1)S(1)} %get-tuple-element.31), channel_id=1, source_target_pairs={{0,4},{4,0},{8,12},{12,8},{1,5},{5,1},{9,13},{13,9},{2,6},{6,2},{1... | collective-permute-start | bytes 294920 | tf_op jit(solution)/shard_map/ppermute | solution.py:17
  62.1 5.6 %collective-permute-start.12 = (bf16[64,768]{1,0:T(8,128)(2,1)S(1)}, bf16[64,768]{1,0:T(8,128)(2,1)S(1)}, u32[]{:S(2)}, u32[]{:S(2)}) collective-permute-start(bf16[64,768]{1,0:T(8,128)(2,1)S(1)} %get-tuple-element.32), channel_id=1, source_target_pairs={{0,12},{4,8},{8,4},{12,0},{1,13},{5,9},{9,5},{13,1},{2,14},{6,10},... | collective-permute-start | bytes 294920 | tf_op jit(solution)/shard_map/ppermute | solution.py:17
  63.6 5.1 %collective-permute-start.11 = (bf16[64,768]{1,0:T(8,128)(2,1)S(1)}, bf16[64,768]{1,0:T(8,128)(2,1)S(1)}, u32[]{:S(2)}, u32[]{:S(2)}) collective-permute-start(bf16[64,768]{1,0:T(8,128)(2,1)S(1)} %get-tuple-element.33), channel_id=1, source_target_pairs={{0,8},{4,12},{8,0},{12,4},{1,9},{5,13},{9,1},{13,5},{2,10},{6,14},... | collective-permute-start | bytes 294920 | tf_op jit(solution)/shard_map/ppermute | solution.py:17

commit v5 on v4

--- a/solution.py
+++ b/solution.py
@@ -34,20 +34,40 @@
     )(*[value for value, _ in ins])
 
 
-def route_kernel(topk, place, ids, route, w_up, out, weights, sem):
+def route_kernel(topk, place, routes, w_up, out, weights, sem):
     copy = pltpu.make_async_copy(w_up.at[0], weights, sem)
     copy.start()
-    tok = ids.shape[1]
+    tok = routes.shape[1]
     rows = up_to(3 * topk, 16)
-    weight = route[...]
+    weight = routes[topk:, :]
     norm = weight / jnp.sum(weight, axis=0, keepdims=True)
     high = norm.astype(jnp.bfloat16).astype(jnp.float32)
-    info = jnp.concatenate([ids[...].astype(jnp.float32), high, norm - high], axis=0)
+    info = jnp.concatenate([routes[:topk, :], high, norm - high], axis=0)
     info = jnp.concatenate([info, jnp.zeros((rows - 3 * topk, tok), jnp.float32)], axis=0)
     info = jnp.concatenate([info, jnp.zeros((rows, out.shape[1] - tok), jnp.float32)], axis=1)
     out[...] = jnp.zeros(out.shape, out.dtype)
     out[:rows, :] = info.astype(jnp.bfloat16)
     copy.wait()
+
+
+def join_kernel(axis, *refs):
+    at = 0
+    for x in refs[:-1]:
+        size = x.shape[axis]
+        if axis:
+            refs[-1][:, at:at + size] = x[...]
+        else:
+            refs[-1][at:at + size, :] = x[...]
+        at += size
+
+
+def join(values, axis):
+    shape = list(values[0].shape)
+    shape[axis] = sum(x.shape[axis] for x in values)
+    return call(
+        functools.partial(join_kernel, axis), [(x, pltpu.VMEM) for x in values],
+        [jax.ShapeDtypeStruct(tuple(shape), values[0].dtype)], [], 4,
+    )[0]
 
 
 def fetch_kernel(lo, w_ref, after, place, *refs):
@@ -164,10 +184,9 @@
         at = pl.multiple_of((place[0] ^ j) * slice_d, LANES)
         packed[:, pl.ds(at, slice_d)] = part.astype(jnp.bfloat16)
 
-    def up(at, f, weight):
+    def up(at, cols, weight):
         value = jnp.dot(packed[at, :], weight, preferred_element_type=jnp.float32)
         value = value / (1.0 + jnp.exp(-value))
-        cols = pl.ds(pl.multiple_of(f * tile_f, LANES), tile_f)
         hidden[at, cols] = value.astype(jnp.bfloat16)
 
     slices = list(range(2, n_seg)) + [1]
@@ -175,19 +194,22 @@
         slice_copies(place, j, slice_d, w_down, room[i], sem_a.at[i]) for i, j in enumerate(slices)
     ]
     for e, held in enumerate(w_held):
+        half = held.shape[1] // 2
+
         def from_held(f, carry, e=e, held=held):
-            cols = pl.ds(pl.multiple_of(f * tile_f, LANES), tile_f)
-            up(slice(e * rows, (e + 1) * rows), f, held[:, cols])
+            cols = pl.ds(pl.multiple_of(f * half, LANES), half)
+            up(slice(e * rows, (e + 1) * rows), cols, held[:, cols])
             return carry
 
-        lax.fori_loop(0, per, from_held, 0)
+        lax.fori_loop(0, 2, from_held, 0)
         for copy in copies[e]:
             copy.start()
 
     def from_ring(t, carry):
         tile_u(t).wait()
         at = pl.ds(pl.multiple_of((n_held + lax.div(t, per)) * rows, 16), rows)
-        up(at, lax.rem(t, per), buf_u[lax.rem(t, deep_u)])
+        cols = pl.ds(pl.multiple_of(lax.rem(t, per) * tile_f, LANES), tile_f)
+        up(at, cols, buf_u[lax.rem(t, deep_u)])
 
         @pl.when(t + deep_u < tiles)
         def _():
@@ -313,16 +335,16 @@
 
     a = [hop(tokens, "seg", k) for k in far]
     b = [tokens] + [hop(tokens, "expert", k) for k in peers]
+    routes = jnp.concatenate([expert_ids.T.astype(jnp.float32), route_weight.T], axis=0)
     route, held_0 = call(
         functools.partial(route_kernel, topk),
-        [(place, pltpu.SMEM), (expert_ids.T, pltpu.VMEM), (route_weight.T, pltpu.VMEM),
-         (w_up, pltpu.HBM)],
+        [(place, pltpu.SMEM), (routes, pltpu.VMEM), (w_up, pltpu.HBM)],
         [jax.ShapeDtypeStruct((tok, LANES), tokens.dtype), pltpu.VMEM(w_up.shape[1:], w_up.dtype)],
         [pltpu.SemaphoreType.DMA], 20,
     )
-    near = jnp.concatenate(b, axis=0)
+    near = join(b, 0)
     e = hop(near, "seg", 1)
-    block = jnp.concatenate(a + [route], axis=1)
+    block = join(a + [route], 1)
     blocks = [block] + [hop(block, "expert", k) for k in peers]
     w_held = [held_0, *fetch(w_up, 1, n_seg - 1, block, place)]
 

time: 69.5 us -> 69.4 us (level)
  other arithmetic: 0.98 us -> 2.36 us
    pallas_call x5 -> x7, Pallas kernels: 32.9 us -> 32.3 us  [call(): pl.pallas_call(body, in_specs=[pl.BlockSpec(memory_space=space) for _, sp...]
    unnamed x11 -> x2, local copies, waits for them, and re-layouts: 1.41 us -> 0.89 us
  transfers between devices with their start and end apart: 18 -> 18, of which waited for: 9 -> 8; matrix products, arithmetic and copies ran while one was open for 1% -> 2% of each run, Pallas kernels for 27% -> 27%
where the time goes in v5:
time: 69.4 us; the launch traced here: 69.2 us
  Pallas kernels  32.3 us (47%)
  starting transfers between devices  24.8 us (36%)
  waiting for transfers between devices  8.61 us (12%)
  other arithmetic  2.36 us (3%)
  local copies, waits for them, and re-layouts  0.93 us (1%)
    pallas_call x7, Pallas kernels, call(): pl.pallas_call(body, in_specs=[pl.BlockSpec(memory_space=space) for _, sp...  32.3 us
    ppermute x18, starting transfers between devices, hop(): return lax.ppermute(value, axis, [(i, i ^ k) for i in range(n)])  24.8 us
    ppermute x18, waiting for transfers between devices, hop(): return lax.ppermute(value, axis, [(i, i ^ k) for i in range(n)])  8.61 us
  transfers between devices with their start and end apart: 18, of which 8 were waited for; matrix products, arithmetic and copies ran while one was open for 2% of the time, Pallas kernels for 27%

profile of v5, /device:TPU:0, one launch (start us, length us, event | category | flops | bytes accessed | tf_op | source)
XLA Modules:
  0.0 69.2 jit_solution(15223710299856665695)
XLA Ops:
  0.0 3.9 %collective-permute-start.2 = (bf16[64,768]{1,0:T(8,128)(2,1)}, bf16[64,768]{1,0:T(8,128)(2,1)S(1)}, u32[]{:S(2)}, u32[]{:S(2)}) collective-permute-start(bf16[64,768]{1,0:T(8,128)(2,1)} %refs_0_.1), channel_id=1, source_target_pairs={{0,12},{4,8},{8,4},{12,0},{1,13},{5,9},{9,5},{13,1},{2,14},{6,10},... | collective-permute-start | bytes 294920 | tf_op jit(solution)/shard_map/ppermute | solution.py:17
  3.9 0.5 collective-permute-start.1
  4.4 0.1 collective-permute-start
  4.5 4.1 %collective-permute-start.5 = (bf16[64,768]{1,0:T(8,128)(2,1)}, bf16[64,768]{1,0:T(8,128)(2,1)S(1)}, u32[]{:S(2)}, u32[]{:S(2)}) collective-permute-start(bf16[64,768]{1,0:T(8,128)(2,1)} %refs_0_.1), channel_id=1, source_target_pairs={{0,3},{1,2},{2,1},{3,0},{4,7},{5,6},{6,5},{7,4},{8,11},{9,10},{10,... | collective-permute-start | bytes 294920 | tf_op jit(solution)/shard_map/ppermute | solution.py:17
  8.6 0.0 collective-permute-start.4
  8.6 0.7 convert_bitcast_fusion
  9.3 0.0 collective-permute-done.2.refs_3_
  9.3 0.0 collective-permute-done.1.refs_2_
  9.3 0.1 collective-permute-done.refs_1_
  9.4 0.9 %copy-done = bf16[64,768]{1,0:T(8,128)(2,1)S(1)} copy-done((bf16[64,768]{1,0:T(8,128)(2,1)S(1)}, bf16[64,768]{1,0:T(8,128)(2,1)}, u32[]{:S(2)}) %copy-start) | copy-done | bytes 98328
  10.3 1.6 %collective-permute-start.3 = (bf16[256,768]{1,0:T(8,128)(2,1)S(1)}, bf16[256,768]{1,0:T(8,128)(2,1)S(1)}, u32[]{:S(2)}, u32[]{:S(2)}) collective-permute-start(bf16[256,768]{1,0:T(8,128)(2,1)S(1)} %shard_map.55.refs_0_), channel_id=1, source_target_pairs={{0,1},{1,0},{2,3},{3,2},{4,5},{5,4},{6,7},{7,6},{8,9},{9,8},{10,11... | collective-permute-start | bytes 1179656 | tf_op jit(solution)/shard_map/ppermute | solution.py:17
  11.9 0.7 pad_maximum_fusion.routes
  12.6 0.1 pad_add_fusion.place
  12.7 4.2 %shard_map.56 = (bf16[64,128]{1,0:T(8,128)(2,1)S(1)}, bf16[3072,1536]{1,0:T(8,128)(2,1)S(1)}) custom-call(s32[2]{0:T(128)S(1)} %pad_add_fusion.place, f32[8,64]{1,0:T(8,128)S(1)} %pad_maximum_fusion.routes, bf16[4,3072,1536]{2,1,0:T(8,128)(2,1)} %refs_9_.1), custom_call_target="tpu_custom_call" | custom-call | tf_op jit(solution)/shard_map/pallas_call | solution.py:25
  16.9 0.0 collective-permute-done.5.refs_1_
  16.9 0.0 collective-permute-done.4.refs_0_
  17.0 1.9 %collective-permute-start.8 = (bf16[64,1664]{1,0:T(8,128)(2,1)S(1)}, bf16[64,1664]{1,0:T(8,128)(2,1)S(1)}, u32[]{:S(2)}, u32[]{:S(2)}) collective-permute-start(bf16[64,1664]{1,0:T(8,128)(2,1)S(1)} %shard_map.57.after.refs_2_), channel_id=1, source_target_pairs={{0,12},{4,8},{8,4},{12,0},{1,13},{5,9},{9,5},{13,1},{2,14},{6,10},... | collective-permute-start | bytes 638984 | tf_op jit(solution)/shard_map/ppermute | solution.py:17
  18.8 1.1 %collective-permute-start.7 = (bf16[64,1664]{1,0:T(8,128)(2,1)S(1)}, bf16[64,1664]{1,0:T(8,128)(2,1)S(1)}, u32[]{:S(2)}, u32[]{:S(2)}) collective-permute-start(bf16[64,1664]{1,0:T(8,128)(2,1)S(1)} %shard_map.57.after.refs_2_), channel_id=1, source_target_pairs={{0,8},{4,12},{8,0},{12,4},{1,9},{5,13},{9,1},{13,5},{2,10},{6,14},... | collective-permute-start | bytes 638984 | tf_op jit(solution)/shard_map/ppermute | solution.py:17
  20.0 0.6 collective-permute-start.6
  20.5 6.9 %shard_map.58 = (bf16[3072,1536]{1,0:T(8,128)(2,1)S(1)}, bf16[3072,1536]{1,0:T(8,128)(2,1)S(1)}) custom-call(bf16[4,3072,1536]{2,1,0:T(8,128)(2,1)} %refs_9_.1, bf16[64,1664]{1,0:T(8,128)(2,1)S(1)} %shard_map.57.after.refs_2_, s32[2]{0:T(128)S(1)} %pad_add_fusion.place), custom_call_target="tpu_custom_call" | custom-call | bytes 18874368 | tf_op jit(solution)/shard_map/pallas_call | solution.py:25
  27.5 0.0 collective-permute-done.8.refs_5_
  27.5 1.5 %collective-permute-done.7.refs_4_ = bf16[64,1664]{1,0:T(8,128)(2,1)S(1)} collective-permute-done((bf16[64,1664]{1,0:T(8,128)(2,1)S(1)}, bf16[64,1664]{1,0:T(8,128)(2,1)S(1)}, u32[]{:S(2)}, u32[]{:S(2)}) %collective-permute-start.7) | collective-permute-done | bytes 213024 | tf_op jit(solution)/shard_map/ppermute | solution.py:17
  28.9 0.3 collective-permute-done.6.refs_3_
  29.3 0.0 collective-permute-done.3.refs_1_
  29.3 13.7 %shard_map.59 = (bf16[64,1536]{1,0:T(8,128)(2,1)S(1)}, bf16[64,1536]{1,0:T(8,128)(2,1)S(1)}, bf16[64,1536]{1,0:T(8,128)(2,1)S(1)}, bf16[64,1536]{1,0:T(8,128)(2,...) custom-call(s32[2]{0:T(128)S(1)} %pad_add_fusion.place, ...), custom_call_target="tpu_custom_call", output_to_operand_aliasing={{7}: (7, {}), {8}: (8, {}), {9}: (9, {})} | custom-call | flops 9663676416 | bytes 37748736 | tf_op jit(solution)/shard_map/pallas_call | solution.py:25
  43.0 1.5 %collective-permute-start.13 = (bf16[64,1536]{1,0:T(8,128)(2,1)S(1)}, bf16[64,1536]{1,0:T(8,128)(2,1)S(1)}, u32[]{:S(2)}, u32[]{:S(2)}) collective-permute-start(bf16[64,1536]{1,0:T(8,128)(2,1)S(1)} %get-tuple-element.26), channel_id=1, source_target_pairs={{0,4},{4,0},{8,12},{12,8},{1,5},{5,1},{9,13},{13,9},{2,6},{6,2},{1... | collective-permute-start | bytes 589832 | tf_op jit(solution)/shard_map/ppermute | solution.py:17
  44.5 0.6 collective-permute-start.14
  45.1 1.5 %collective-permute-start.15 = (bf16[64,1536]{1,0:T(8,128)(2,1)S(1)}, bf16[64,1536]{1,0:T(8,128)(2,1)S(1)}, u32[]{:S(2)}, u32[]{:S(2)}) collective-permute-start(bf16[64,1536]{1,0:T(8,128)(2,1)S(1)} %get-tuple-element.28), channel_id=1, source_target_pairs={{0,12},{4,8},{8,4},{12,0},{1,13},{5,9},{9,5},{13,1},{2,14},{6,10},... | collective-permute-start | bytes 589832 | tf_op jit(solution)/shard_map/ppermute | solution.py:17
  46.6 2.1 %shard_map.61 = bf16[256,768]{1,0:T(8,128)(2,1)S(1)} custom-call(bf16[384,1536]{1,0:T(8,128)(2,1)S(1)} %get-tuple-element.21.hidden, bf16[256,384]{1,0:T(8,128)(2,1)S(1)} %get-tuple-element.22.pick_t, f32[384,1]{1,0:T(8,128)S(1)} %get-tuple-element.23.row_w, bf16[3072,1536]{1,0:T(8,128)(2,1)S(1)} %get-tuple-element.24.weights), custom_call_target="tpu_custom_call" | custom-call | flops 2415919104 | tf_op jit(solution)/shard_map/pallas_call | solution.py:25
  48.6 0.5 collective-permute-start.9
  49.1 5.4 %shard_map.60 = f32[256,768]{1,0:T(8,128)S(1)} custom-call(s32[2]{0:T(128)S(1)} %pad_add_fusion.place, bf16[384,1536]{1,0:T(8,128)(2,1)S(1)} %get-tuple-element.21.hidden, bf16[256,384]{1,0:T(8,128)(2,1)S(1)} %get-tuple-element.22.pick_t, f32[384,1]{1,0:T(8,128)S(1)} %get-tuple-element.23.row_w, bf16[4,1536,3072]{2,1,0:T(8,128)(2,1)} %w_down.1), custom_call_target="tpu_custom_call" | custom-call | flops 2415919104 | bytes 9437184 | tf_op jit(solution)/shard_map/pallas_call | solution.py:25
  54.5 0.0 collective-permute-done.13
  54.5 0.7 collective-permute-done.14
  55.2 0.0 collective-permute-done.15
  55.2 0.1 add_convert_fusion
  55.4 2.7 %collective-permute-start.16 = (bf16[64,768]{1,0:T(8,128)(2,1)S(1)}, bf16[64,768]{1,0:T(8,128)(2,1)S(1)}, u32[]{:S(2)}, u32[]{:S(2)}) collective-permute-start(bf16[64,768]{1,0:T(8,128)(2,1)S(1)} %get-tuple-element.34), channel_id=1, source_target_pairs={{0,2},{1,3},{2,0},{3,1},{4,6},{5,7},{6,4},{7,5},{8,10},{9,11},{10,... | collective-permute-start | bytes 294920 | tf_op jit(solution)/shard_map/ppermute | solution.py:17
  58.0 0.7 collective-permute-start.17
  58.7 1.0 %collective-permute-done.9 = bf16[256,768]{1,0:T(8,128)(2,1)S(1)} collective-permute-done((bf16[256,768]{1,0:T(8,128)(2,1)S(1)}, bf16[256,768]{1,0:T(8,128)(2,1)S(1)}, u32[]{:S(2)}, u32[]{:S(2)}) %collective-permute-start.9) | collective-permute-done | bytes 393248 | tf_op jit(solution)/shard_map/ppermute | solution.py:17
  59.7 0.1 fusion.5
  59.8 2.1 %collective-permute-start.10 = (bf16[64,768]{1,0:T(8,128)(2,1)S(1)}, bf16[64,768]{1,0:T(8,128)(2,1)S(1)}, u32[]{:S(2)}, u32[]{:S(2)}) collective-permute-start(bf16[64,768]{1,0:T(8,128)(2,1)S(1)} %get-tuple-element.31), channel_id=1, source_target_pairs={{0,4},{4,0},{8,12},{12,8},{1,5},{5,1},{9,13},{13,9},{2,6},{6,2},{1... | collective-permute-start | bytes 294920 | tf_op jit(solution)/shard_map/ppermute | solution.py:17
  61.9 1.5 %collective-permute-start.12 = (bf16[64,768]{1,0:T(8,128)(2,1)S(1)}, bf16[64,768]{1,0:T(8,128)(2,1)S(1)}, u32[]{:S(2)}, u32[]{:S(2)}) collective-permute-start(bf16[64,768]{1,0:T(8,128)(2,1)S(1)} %get-tuple-element.32), channel_id=1, source_target_pairs={{0,12},{4,8},{8,4},{12,0},{1,13},{5,9},{9,5},{13,1},{2,14},{6,10},... | collective-permute-start | bytes 294920 | tf_op jit(solution)/shard_map/ppermute | solution.py:17
  63.3 0.1 collective-permute-start.11
  63.4 1.9 %collective-permute-done.16 = bf16[64,768]{1,0:T(8,128)(2,1)S(1)} collective-permute-done((bf16[64,768]{1,0:T(8,128)(2,1)S(1)}, bf16[64,768]{1,0:T(8,128)(2,1)S(1)}, u32[]{:S(2)}, u32[]{:S(2)}) %collective-permute-start.16) | collective-permute-done | bytes 98336 | tf_op jit(solution)/shard_map/ppermute | solution.py:17
  65.3 0.0 collective-permute-done.17
  65.3 0.0 collective-permute-done.10
  65.3 2.2 %collective-permute-done.12 = bf16[64,768]{1,0:T(8,128)(2,1)S(1)} collective-permute-done((bf16[64,768]{1,0:T(8,128)(2,1)S(1)}, bf16[64,768]{1,0:T(8,128)(2,1)S(1)}, u32[]{:S(2)}, u32[]{:S(2)}) %collective-permute-start.12) | collective-permute-done | bytes 98336 | tf_op jit(solution)/shard_map/ppermute | solution.py:17
  67.4 1.0 %collective-permute-done.11 = bf16[64,768]{1,0:T(8,128)(2,1)S(1)} collective-permute-done((bf16[64,768]{1,0:T(8,128)(2,1)S(1)}, bf16[64,768]{1,0:T(8,128)(2,1)S(1)}, u32[]{:S(2)}, u32[]{:S(2)}) %collective-permute-start.11) | collective-permute-done | bytes 98336 | tf_op jit(solution)/shard_map/ppermute | solution.py:17
  68.4 0.7 %fusion.4 = bf16[64,768]{1,0:T(8,128)(2,1)} fusion(f32[256,768]{1,0:T(8,128)S(1)} %get-tuple-element.30, bf16[64,768]{1,0:T(8,128)(2,1)S(1)} %collective-permute-done.17, bf16[64,768]{1,0:T(8,128)(2,1)S(1)} %collective-permute-done.16, bf16[64,768]{1,0:T(8,128)(2,1)S(1)} %collective-permute-done.12, bf16[64,768]{1,0:T(8,128)(2,1)S(1)} %collective-permute-done.11, ...), kind=kLoop, calls=%fused_computation.7 | loop fusion | flops 540672 | bytes 786432 | tf_op jit(solution)/shard_map/convert_element_type | solution.py:363
  (5 shorter events, 0.1 us)
Async XLA Ops:
  0.0 9.3 %collective-permute-start.2 = (bf16[64,768]{1,0:T(8,128)(2,1)}, bf16[64,768]{1,0:T(8,128)(2,1)S(1)}, u32[]{:S(2)}, u32[]{:S(2)}) collective-permute-start(bf16[64,768]{1,0:T(8,128)(2,1)} %refs_0_.1), channel_id=1, source_target_pairs={{0,12},{4,8},{8,4},{12,0},{1,13},{5,9},{9,5},{13,1},{2,14},{6,10},... | collective-permute-start | bytes 294920 | tf_op jit(solution)/shard_map/ppermute | solution.py:17
  3.9 5.3 %collective-permute-start.1 = (bf16[64,768]{1,0:T(8,128)(2,1)}, bf16[64,768]{1,0:T(8,128)(2,1)S(1)}, u32[]{:S(2)}, u32[]{:S(2)}) collective-permute-start(bf16[64,768]{1,0:T(8,128)(2,1)} %refs_0_.1), channel_id=1, source_target_pairs={{0,8},{4,12},{8,0},{12,4},{1,9},{5,13},{9,1},{13,5},{2,10},{6,14},... | collective-permute-start | bytes 294920 | tf_op jit(solution)/shard_map/ppermute | solution.py:17
  4.4 4.9 %collective-permute-start = (bf16[64,768]{1,0:T(8,128)(2,1)}, bf16[64,768]{1,0:T(8,128)(2,1)S(1)}, u32[]{:S(2)}, u32[]{:S(2)}) collective-permute-start(bf16[64,768]{1,0:T(8,128)(2,1)} %refs_0_.1), channel_id=1, source_target_pairs={{0,4},{4,0},{8,12},{12,8},{1,5},{5,1},{9,13},{13,9},{2,6},{6,2},{1... | collective-permute-start | bytes 294920 | tf_op jit(solution)/shard_map/ppermute | solution.py:17
  4.5 12.4 %collective-permute-start.5 = (bf16[64,768]{1,0:T(8,128)(2,1)}, bf16[64,768]{1,0:T(8,128)(2,1)S(1)}, u32[]{:S(2)}, u32[]{:S(2)}) collective-permute-start(bf16[64,768]{1,0:T(8,128)(2,1)} %refs_0_.1), channel_id=1, source_target_pairs={{0,3},{1,2},{2,1},{3,0},{4,7},{5,6},{6,5},{7,4},{8,11},{9,10},{10,... | collective-permute-start | bytes 294920 | tf_op jit(solution)/shard_map/ppermute | solution.py:17
  8.6 8.4 %collective-permute-start.4 = (bf16[64,768]{1,0:T(8,128)(2,1)}, bf16[64,768]{1,0:T(8,128)(2,1)S(1)}, u32[]{:S(2)}, u32[]{:S(2)}) collective-permute-start(bf16[64,768]{1,0:T(8,128)(2,1)} %refs_0_.1), channel_id=1, source_target_pairs={{0,2},{1,3},{2,0},{3,1},{4,6},{5,7},{6,4},{7,5},{8,10},{9,11},{10,... | collective-permute-start | bytes 294920 | tf_op jit(solution)/shard_map/ppermute | solution.py:17
  9.4 0.9 %copy-start = (bf16[64,768]{1,0:T(8,128)(2,1)S(1)}, bf16[64,768]{1,0:T(8,128)(2,1)}, u32[]{:S(2)}) copy-start(bf16[64,768]{1,0:T(8,128)(2,1)} %refs_0_.1) | copy-start | bytes 294916
  10.3 19.0 %collective-permute-start.3 = (bf16[256,768]{1,0:T(8,128)(2,1)S(1)}, bf16[256,768]{1,0:T(8,128)(2,1)S(1)}, u32[]{:S(2)}, u32[]{:S(2)}) collective-permute-start(bf16[256,768]{1,0:T(8,128)(2,1)S(1)} %shard_map.55.refs_0_), channel_id=1, source_target_pairs={{0,1},{1,0},{2,3},{3,2},{4,5},{5,4},{6,7},{7,6},{8,9},{9,8},{10,11... | collective-permute-start | bytes 1179656 | tf_op jit(solution)/shard_map/ppermute | solution.py:17
  17.0 10.5 %collective-permute-start.8 = (bf16[64,1664]{1,0:T(8,128)(2,1)S(1)}, bf16[64,1664]{1,0:T(8,128)(2,1)S(1)}, u32[]{:S(2)}, u32[]{:S(2)}) collective-permute-start(bf16[64,1664]{1,0:T(8,128)(2,1)S(1)} %shard_map.57.after.refs_2_), channel_id=1, source_target_pairs={{0,12},{4,8},{8,4},{12,0},{1,13},{5,9},{9,5},{13,1},{2,14},{6,10},... | collective-permute-start | bytes 638984 | tf_op jit(solution)/shard_map/ppermute | solution.py:17
  18.8 10.1 %collective-permute-start.7 = (bf16[64,1664]{1,0:T(8,128)(2,1)S(1)}, bf16[64,1664]{1,0:T(8,128)(2,1)S(1)}, u32[]{:S(2)}, u32[]{:S(2)}) collective-permute-start(bf16[64,1664]{1,0:T(8,128)(2,1)S(1)} %shard_map.57.after.refs_2_), channel_id=1, source_target_pairs={{0,8},{4,12},{8,0},{12,4},{1,9},{5,13},{9,1},{13,5},{2,10},{6,14},... | collective-permute-start | bytes 638984 | tf_op jit(solution)/shard_map/ppermute | solution.py:17
  20.0 9.3 %collective-permute-start.6 = (bf16[64,1664]{1,0:T(8,128)(2,1)S(1)}, bf16[64,1664]{1,0:T(8,128)(2,1)S(1)}, u32[]{:S(2)}, u32[]{:S(2)}) collective-permute-start(bf16[64,1664]{1,0:T(8,128)(2,1)S(1)} %shard_map.57.after.refs_2_), channel_id=1, source_target_pairs={{0,4},{4,0},{8,12},{12,8},{1,5},{5,1},{9,13},{13,9},{2,6},{6,2},{1... | collective-permute-start | bytes 638984 | tf_op jit(solution)/shard_map/ppermute | solution.py:17
  43.0 11.5 %collective-permute-start.13 = (bf16[64,1536]{1,0:T(8,128)(2,1)S(1)}, bf16[64,1536]{1,0:T(8,128)(2,1)S(1)}, u32[]{:S(2)}, u32[]{:S(2)}) collective-permute-start(bf16[64,1536]{1,0:T(8,128)(2,1)S(1)} %get-tuple-element.26), channel_id=1, source_target_pairs={{0,4},{4,0},{8,12},{12,8},{1,5},{5,1},{9,13},{13,9},{2,6},{6,2},{1... | collective-permute-start | bytes 589832 | tf_op jit(solution)/shard_map/ppermute | solution.py:17
  44.5 10.8 %collective-permute-start.14 = (bf16[64,1536]{1,0:T(8,128)(2,1)S(1)}, bf16[64,1536]{1,0:T(8,128)(2,1)S(1)}, u32[]{:S(2)}, u32[]{:S(2)}) collective-permute-start(bf16[64,1536]{1,0:T(8,128)(2,1)S(1)} %get-tuple-element.27), channel_id=1, source_target_pairs={{0,8},{4,12},{8,0},{12,4},{1,9},{5,13},{9,1},{13,5},{2,10},{6,14},... | collective-permute-start | bytes 589832 | tf_op jit(solution)/shard_map/ppermute | solution.py:17
  45.1 10.2 %collective-permute-start.15 = (bf16[64,1536]{1,0:T(8,128)(2,1)S(1)}, bf16[64,1536]{1,0:T(8,128)(2,1)S(1)}, u32[]{:S(2)}, u32[]{:S(2)}) collective-permute-start(bf16[64,1536]{1,0:T(8,128)(2,1)S(1)} %get-tuple-element.28), channel_id=1, source_target_pairs={{0,12},{4,8},{8,4},{12,0},{1,13},{5,9},{9,5},{13,1},{2,14},{6,10},... | collective-permute-start | bytes 589832 | tf_op jit(solution)/shard_map/ppermute | solution.py:17
  48.6 11.0 %collective-permute-start.9 = (bf16[256,768]{1,0:T(8,128)(2,1)S(1)}, bf16[256,768]{1,0:T(8,128)(2,1)S(1)}, u32[]{:S(2)}, u32[]{:S(2)}) collective-permute-start(bf16[256,768]{1,0:T(8,128)(2,1)S(1)} %shard_map.61), channel_id=1, source_target_pairs={{0,1},{1,0},{2,3},{3,2},{4,5},{5,4},{6,7},{7,6},{8,9},{9,8},{10,11... | collective-permute-start | bytes 1179656 | tf_op jit(solution)/shard_map/ppermute | solution.py:17
  55.4 9.9 %collective-permute-start.16 = (bf16[64,768]{1,0:T(8,128)(2,1)S(1)}, bf16[64,768]{1,0:T(8,128)(2,1)S(1)}, u32[]{:S(2)}, u32[]{:S(2)}) collective-permute-start(bf16[64,768]{1,0:T(8,128)(2,1)S(1)} %get-tuple-element.34), channel_id=1, source_target_pairs={{0,2},{1,3},{2,0},{3,1},{4,6},{5,7},{6,4},{7,5},{8,10},{9,11},{10,... | collective-permute-start | bytes 294920 | tf_op jit(solution)/shard_map/ppermute | solution.py:17
  58.0 7.3 %collective-permute-start.17 = (bf16[64,768]{1,0:T(8,128)(2,1)S(1)}, bf16[64,768]{1,0:T(8,128)(2,1)S(1)}, u32[]{:S(2)}, u32[]{:S(2)}) collective-permute-start(bf16[64,768]{1,0:T(8,128)(2,1)S(1)} %get-tuple-element.35), channel_id=1, source_target_pairs={{0,3},{1,2},{2,1},{3,0},{4,7},{5,6},{6,5},{7,4},{8,11},{9,10},{10,... | collective-permute-start | bytes 294920 | tf_op jit(solution)/shard_map/ppermute | solution.py:17
  59.8 5.5 %collective-permute-start.10 = (bf16[64,768]{1,0:T(8,128)(2,1)S(1)}, bf16[64,768]{1,0:T(8,128)(2,1)S(1)}, u32[]{:S(2)}, u32[]{:S(2)}) collective-permute-start(bf16[64,768]{1,0:T(8,128)(2,1)S(1)} %get-tuple-element.31), channel_id=1, source_target_pairs={{0,4},{4,0},{8,12},{12,8},{1,5},{5,1},{9,13},{13,9},{2,6},{6,2},{1... | collective-permute-start | bytes 294920 | tf_op jit(solution)/shard_map/ppermute | solution.py:17
  61.9 5.6 %collective-permute-start.12 = (bf16[64,768]{1,0:T(8,128)(2,1)S(1)}, bf16[64,768]{1,0:T(8,128)(2,1)S(1)}, u32[]{:S(2)}, u32[]{:S(2)}) collective-permute-start(bf16[64,768]{1,0:T(8,128)(2,1)S(1)} %get-tuple-element.32), channel_id=1, source_target_pairs={{0,12},{4,8},{8,4},{12,0},{1,13},{5,9},{9,5},{13,1},{2,14},{6,10},... | collective-permute-start | bytes 294920 | tf_op jit(solution)/shard_map/ppermute | solution.py:17
  63.3 5.1 %collective-permute-start.11 = (bf16[64,768]{1,0:T(8,128)(2,1)S(1)}, bf16[64,768]{1,0:T(8,128)(2,1)S(1)}, u32[]{:S(2)}, u32[]{:S(2)}) collective-permute-start(bf16[64,768]{1,0:T(8,128)(2,1)S(1)} %get-tuple-element.33), channel_id=1, source_target_pairs={{0,8},{4,12},{8,0},{12,4},{1,9},{5,13},{9,1},{13,5},{2,10},{6,14},... | collective-permute-start | bytes 294920 | tf_op jit(solution)/shard_map/ppermute | solution.py:17

commit v6 on v5

--- a/solution.py
+++ b/solution.py
@@ -34,15 +34,23 @@
     )(*[value for value, _ in ins])
 
 
-def route_kernel(topk, place, routes, w_up, out, weights, sem):
+def route_kernel(topk, place, ids_hbm, route_hbm, w_up, out, weights, ids, route, sem, sems):
+    small = [
+        pltpu.make_async_copy(ids_hbm, ids, sems.at[0]),
+        pltpu.make_async_copy(route_hbm, route, sems.at[1]),
+    ]
+    for x in small:
+        x.start()
     copy = pltpu.make_async_copy(w_up.at[0], weights, sem)
     copy.start()
-    tok = routes.shape[1]
+    for x in small:
+        x.wait()
+    tok = ids.shape[1]
     rows = up_to(3 * topk, 16)
-    weight = routes[topk:, :]
+    weight = route[...]
     norm = weight / jnp.sum(weight, axis=0, keepdims=True)
     high = norm.astype(jnp.bfloat16).astype(jnp.float32)
-    info = jnp.concatenate([routes[:topk, :], high, norm - high], axis=0)
+    info = jnp.concatenate([ids[...].astype(jnp.float32), high, norm - high], axis=0)
     info = jnp.concatenate([info, jnp.zeros((rows - 3 * topk, tok), jnp.float32)], axis=0)
     info = jnp.concatenate([info, jnp.zeros((rows, out.shape[1] - tok), jnp.float32)], axis=1)
     out[...] = jnp.zeros(out.shape, out.dtype)
@@ -335,12 +343,14 @@
 
     a = [hop(tokens, "seg", k) for k in far]
     b = [tokens] + [hop(tokens, "expert", k) for k in peers]
-    routes = jnp.concatenate([expert_ids.T.astype(jnp.float32), route_weight.T], axis=0)
+    ids = pltpu.with_memory_space_constraint(expert_ids.T, pltpu.HBM)
+    weights = pltpu.with_memory_space_constraint(route_weight.T, pltpu.HBM)
     route, held_0 = call(
         functools.partial(route_kernel, topk),
-        [(place, pltpu.SMEM), (routes, pltpu.VMEM), (w_up, pltpu.HBM)],
+        [(place, pltpu.SMEM), (ids, pltpu.HBM), (weights, pltpu.HBM), (w_up, pltpu.HBM)],
         [jax.ShapeDtypeStruct((tok, LANES), tokens.dtype), pltpu.VMEM(w_up.shape[1:], w_up.dtype)],
-        [pltpu.SemaphoreType.DMA], 20,
+        [pltpu.VMEM((topk, tok), jnp.int32), pltpu.VMEM((topk, tok), jnp.float32),
+         pltpu.SemaphoreType.DMA, pltpu.SemaphoreType.DMA((2,))], 20,
     )
     near = join(b, 0)
     e = hop(near, "seg", 1)

time: 69.4 us -> 77.4 us (1.12)
  waiting for transfers between devices: 8.61 us -> 17.4 us
  other arithmetic: 2.36 us -> 0.99 us
  Pallas kernels: 32.3 us -> 33.3 us
  local copies, waits for them, and re-layouts: 0.93 us -> 0.04 us
    ppermute x18, waiting for transfers between devices: 8.61 us -> 17.4 us  [hop(): return lax.ppermute(value, axis, [(i, i ^ k) for i in range(n)])]
    pallas_call x7, Pallas kernels: 32.3 us -> 33.3 us  [call(): pl.pallas_call(body, in_specs=[pl.BlockSpec(memory_space=space) for _, sp...]
    unnamed x2 -> x0, local copies, waits for them, and re-layouts: 0.89 us -> none
  transfers between devices with their start and end apart: 18 -> 18, of which waited for: 8 -> 9; matrix products, arithmetic and copies ran while one was open for 2% -> 0% of each run, Pallas kernels for 27% -> 24%
where the time goes in v6:
time: 77.4 us; the launch traced here: 77.2 us
  Pallas kernels  33.3 us (43%)
  starting transfers between devices  25.4 us (33%)
  waiting for transfers between devices  17.4 us (22%)
  other arithmetic  0.99 us (1%)
    pallas_call x7, Pallas kernels, call(): pl.pallas_call(body, in_specs=[pl.BlockSpec(memory_space=space) for _, sp...  33.3 us
    ppermute x18, starting transfers between devices, hop(): return lax.ppermute(value, axis, [(i, i ^ k) for i in range(n)])  25.4 us
    ppermute x18, waiting for transfers between devices, hop(): return lax.ppermute(value, axis, [(i, i ^ k) for i in range(n)])  17.4 us
  transfers between devices with their start and end apart: 18, of which 9 were waited for; matrix products, arithmetic and copies ran while one was open for 0% of the time, Pallas kernels for 24%

profile of v6, /device:TPU:0, one launch (start us, length us, event | category | flops | bytes accessed | tf_op | source)
XLA Modules:
  0.0 77.2 jit_solution(9045778360706777668)
XLA Ops:
  0.0 3.9 %collective-permute-start.2 = (bf16[64,768]{1,0:T(8,128)(2,1)}, bf16[64,768]{1,0:T(8,128)(2,1)S(1)}, u32[]{:S(2)}, u32[]{:S(2)}) collective-permute-start(bf16[64,768]{1,0:T(8,128)(2,1)} %refs_0_.1), channel_id=1, source_target_pairs={{0,12},{4,8},{8,4},{12,0},{1,13},{5,9},{9,5},{13,1},{2,14},{6,10},... | collective-permute-start | bytes 294920 | tf_op jit(solution)/shard_map/ppermute | solution.py:17
  3.9 0.5 collective-permute-start.1
  4.4 0.1 collective-permute-start
  4.5 2.9 %collective-permute-done.2.refs_3_ = bf16[64,768]{1,0:T(8,128)(2,1)S(1)} collective-permute-done((bf16[64,768]{1,0:T(8,128)(2,1)}, bf16[64,768]{1,0:T(8,128)(2,1)S(1)}, u32[]{:S(2)}, u32[]{:S(2)}) %collective-permute-start.2) | collective-permute-done | bytes 98336 | tf_op jit(solution)/shard_map/ppermute | solution.py:17
  7.4 1.6 %collective-permute-done.1.refs_2_ = bf16[64,768]{1,0:T(8,128)(2,1)S(1)} collective-permute-done((bf16[64,768]{1,0:T(8,128)(2,1)}, bf16[64,768]{1,0:T(8,128)(2,1)S(1)}, u32[]{:S(2)}, u32[]{:S(2)}) %collective-permute-start.1) | collective-permute-done | bytes 98336 | tf_op jit(solution)/shard_map/ppermute | solution.py:17
  9.0 0.3 collective-permute-done.refs_1_
  9.4 0.9 %shard_map.55.refs_0_ = bf16[256,768]{1,0:T(8,128)(2,1)S(1)} custom-call(bf16[64,768]{1,0:T(8,128)(2,1)} %refs_0_.1, bf16[64,768]{1,0:T(8,128)(2,1)S(1)} %collective-permute-done.refs_1_, bf16[64,768]{1,0:T(8,128)(2,1)S(1)} %collective-permute-done.1.refs_2_, bf16[64,768]{1,0:T(8,128)(2,1)S(1)} %collective-permute-done.2.refs_3_), custom_call_target="tpu_custom_call" | custom-call | tf_op jit(solution)/shard_map/pallas_call | solution.py:25
  10.3 1.6 %collective-permute-start.3 = (bf16[256,768]{1,0:T(8,128)(2,1)S(1)}, bf16[256,768]{1,0:T(8,128)(2,1)S(1)}, u32[]{:S(2)}, u32[]{:S(2)}) collective-permute-start(bf16[256,768]{1,0:T(8,128)(2,1)S(1)} %shard_map.55.refs_0_), channel_id=1, source_target_pairs={{0,1},{1,0},{2,3},{3,2},{4,5},{5,4},{6,7},{7,6},{8,9},{9,8},{10,11... | collective-permute-start | bytes 1179656 | tf_op jit(solution)/shard_map/ppermute | solution.py:17
  11.9 2.5 %collective-permute-start.5 = (bf16[64,768]{1,0:T(8,128)(2,1)}, bf16[64,768]{1,0:T(8,128)(2,1)S(1)}, u32[]{:S(2)}, u32[]{:S(2)}) collective-permute-start(bf16[64,768]{1,0:T(8,128)(2,1)} %refs_0_.1), channel_id=1, source_target_pairs={{0,3},{1,2},{2,1},{3,0},{4,7},{5,6},{6,5},{7,4},{8,11},{9,10},{10,... | collective-permute-start | bytes 294920 | tf_op jit(solution)/shard_map/ppermute | solution.py:17
  14.4 0.1 collective-permute-start.4
  14.5 0.1 pad_add_fusion.place
  14.6 4.3 %shard_map.56 = (bf16[64,128]{1,0:T(8,128)(2,1)S(1)}, bf16[3072,1536]{1,0:T(8,128)(2,1)S(1)}) custom-call(s32[2]{0:T(128)S(1)} %pad_add_fusion.place, s32[4,64]{1,0:T(4,128)} %bitcast.4, f32[4,64]{1,0:T(4,128)} %bitcast.5, bf16[4,3072,1536]{2,1,0:T(8,128)(2,1)} %refs_9_.1), custom_call_target="tpu_custom_call" | custom-call | tf_op jit(solution)/shard_map/pallas_call | solution.py:25
  18.9 7.2 %collective-permute-done.5.refs_1_ = bf16[64,768]{1,0:T(8,128)(2,1)S(1)} collective-permute-done((bf16[64,768]{1,0:T(8,128)(2,1)}, bf16[64,768]{1,0:T(8,128)(2,1)S(1)}, u32[]{:S(2)}, u32[]{:S(2)}) %collective-permute-start.5) | collective-permute-done | bytes 98336 | tf_op jit(solution)/shard_map/ppermute | solution.py:17
  26.1 0.0 collective-permute-done.4.refs_0_
  26.1 1.0 %collective-permute-start.8 = (bf16[64,1664]{1,0:T(8,128)(2,1)S(1)}, bf16[64,1664]{1,0:T(8,128)(2,1)S(1)}, u32[]{:S(2)}, u32[]{:S(2)}) collective-permute-start(bf16[64,1664]{1,0:T(8,128)(2,1)S(1)} %shard_map.57.after.refs_2_), channel_id=1, source_target_pairs={{0,12},{4,8},{8,4},{12,0},{1,13},{5,9},{9,5},{13,1},{2,14},{6,10},... | collective-permute-start | bytes 638984 | tf_op jit(solution)/shard_map/ppermute | solution.py:17
  27.2 2.2 %collective-permute-start.7 = (bf16[64,1664]{1,0:T(8,128)(2,1)S(1)}, bf16[64,1664]{1,0:T(8,128)(2,1)S(1)}, u32[]{:S(2)}, u32[]{:S(2)}) collective-permute-start(bf16[64,1664]{1,0:T(8,128)(2,1)S(1)} %shard_map.57.after.refs_2_), channel_id=1, source_target_pairs={{0,8},{4,12},{8,0},{12,4},{1,9},{5,13},{9,1},{13,5},{2,10},{6,14},... | collective-permute-start | bytes 638984 | tf_op jit(solution)/shard_map/ppermute | solution.py:17
  29.4 0.3 collective-permute-start.6
  29.7 6.9 %shard_map.58 = (bf16[3072,1536]{1,0:T(8,128)(2,1)S(1)}, bf16[3072,1536]{1,0:T(8,128)(2,1)S(1)}) custom-call(bf16[4,3072,1536]{2,1,0:T(8,128)(2,1)} %refs_9_.1, bf16[64,1664]{1,0:T(8,128)(2,1)S(1)} %shard_map.57.after.refs_2_, s32[2]{0:T(128)S(1)} %pad_add_fusion.place), custom_call_target="tpu_custom_call" | custom-call | bytes 18874368 | tf_op jit(solution)/shard_map/pallas_call | solution.py:25
  36.6 0.0 collective-permute-done.8.refs_5_
  36.6 0.0 collective-permute-done.7.refs_4_
  36.7 0.2 collective-permute-done.6.refs_3_
  36.8 0.0 collective-permute-done.3.refs_1_
  36.8 13.7 %shard_map.59 = (bf16[64,1536]{1,0:T(8,128)(2,1)S(1)}, bf16[64,1536]{1,0:T(8,128)(2,1)S(1)}, bf16[64,1536]{1,0:T(8,128)(2,1)S(1)}, bf16[64,1536]{1,0:T(8,128)(2,...) custom-call(s32[2]{0:T(128)S(1)} %pad_add_fusion.place, ...), custom_call_target="tpu_custom_call", output_to_operand_aliasing={{7}: (7, {}), {8}: (8, {}), {9}: (9, {})} | custom-call | flops 9663676416 | bytes 37748736 | tf_op jit(solution)/shard_map/pallas_call | solution.py:25
  50.6 1.6 %collective-permute-start.13 = (bf16[64,1536]{1,0:T(8,128)(2,1)S(1)}, bf16[64,1536]{1,0:T(8,128)(2,1)S(1)}, u32[]{:S(2)}, u32[]{:S(2)}) collective-permute-start(bf16[64,1536]{1,0:T(8,128)(2,1)S(1)} %get-tuple-element.26), channel_id=1, source_target_pairs={{0,4},{4,0},{8,12},{12,8},{1,5},{5,1},{9,13},{13,9},{2,6},{6,2},{1... | collective-permute-start | bytes 589832 | tf_op jit(solution)/shard_map/ppermute | solution.py:17
  52.2 0.4 collective-permute-start.14
  52.6 1.5 %collective-permute-start.15 = (bf16[64,1536]{1,0:T(8,128)(2,1)S(1)}, bf16[64,1536]{1,0:T(8,128)(2,1)S(1)}, u32[]{:S(2)}, u32[]{:S(2)}) collective-permute-start(bf16[64,1536]{1,0:T(8,128)(2,1)S(1)} %get-tuple-element.28), channel_id=1, source_target_pairs={{0,12},{4,8},{8,4},{12,0},{1,13},{5,9},{9,5},{13,1},{2,14},{6,10},... | collective-permute-start | bytes 589832 | tf_op jit(solution)/shard_map/ppermute | solution.py:17
  54.1 2.1 %shard_map.61 = bf16[256,768]{1,0:T(8,128)(2,1)S(1)} custom-call(bf16[384,1536]{1,0:T(8,128)(2,1)S(1)} %get-tuple-element.21.hidden, bf16[256,384]{1,0:T(8,128)(2,1)S(1)} %get-tuple-element.22.pick_t, f32[384,1]{1,0:T(8,128)S(1)} %get-tuple-element.23.row_w, bf16[3072,1536]{1,0:T(8,128)(2,1)S(1)} %get-tuple-element.24.weights), custom_call_target="tpu_custom_call" | custom-call | flops 2415919104 | tf_op jit(solution)/shard_map/pallas_call | solution.py:25
  56.2 2.7 %collective-permute-start.9 = (bf16[256,768]{1,0:T(8,128)(2,1)S(1)}, bf16[256,768]{1,0:T(8,128)(2,1)S(1)}, u32[]{:S(2)}, u32[]{:S(2)}) collective-permute-start(bf16[256,768]{1,0:T(8,128)(2,1)S(1)} %shard_map.61), channel_id=1, source_target_pairs={{0,1},{1,0},{2,3},{3,2},{4,5},{5,4},{6,7},{7,6},{8,9},{9,8},{10,11... | collective-permute-start | bytes 1179656 | tf_op jit(solution)/shard_map/ppermute | solution.py:17
  58.9 5.4 %shard_map.60 = f32[256,768]{1,0:T(8,128)S(1)} custom-call(s32[2]{0:T(128)S(1)} %pad_add_fusion.place, bf16[384,1536]{1,0:T(8,128)(2,1)S(1)} %get-tuple-element.21.hidden, bf16[256,384]{1,0:T(8,128)(2,1)S(1)} %get-tuple-element.22.pick_t, f32[384,1]{1,0:T(8,128)S(1)} %get-tuple-element.23.row_w, bf16[4,1536,3072]{2,1,0:T(8,128)(2,1)} %w_down.1), custom_call_target="tpu_custom_call" | custom-call | flops 2415919104 | bytes 9437184 | tf_op jit(solution)/shard_map/pallas_call | solution.py:25
  64.3 0.0 collective-permute-done.13
  64.3 0.0 collective-permute-done.14
  64.3 0.0 collective-permute-done.15
  64.3 0.1 add_convert_fusion
  64.5 0.8 %collective-permute-start.16 = (bf16[64,768]{1,0:T(8,128)(2,1)S(1)}, bf16[64,768]{1,0:T(8,128)(2,1)S(1)}, u32[]{:S(2)}, u32[]{:S(2)}) collective-permute-start(bf16[64,768]{1,0:T(8,128)(2,1)S(1)} %get-tuple-element.34), channel_id=1, source_target_pairs={{0,2},{1,3},{2,0},{3,1},{4,6},{5,7},{6,4},{7,5},{8,10},{9,11},{10,... | collective-permute-start | bytes 294920 | tf_op jit(solution)/shard_map/ppermute | solution.py:17
  65.3 2.4 %collective-permute-start.17 = (bf16[64,768]{1,0:T(8,128)(2,1)S(1)}, bf16[64,768]{1,0:T(8,128)(2,1)S(1)}, u32[]{:S(2)}, u32[]{:S(2)}) collective-permute-start(bf16[64,768]{1,0:T(8,128)(2,1)S(1)} %get-tuple-element.35), channel_id=1, source_target_pairs={{0,3},{1,2},{2,1},{3,0},{4,7},{5,6},{6,5},{7,4},{8,11},{9,10},{10,... | collective-permute-start | bytes 294920 | tf_op jit(solution)/shard_map/ppermute | solution.py:17
  67.7 0.3 collective-permute-done.9
  68.0 0.1 fusion.5
  68.1 1.8 %collective-permute-start.10 = (bf16[64,768]{1,0:T(8,128)(2,1)S(1)}, bf16[64,768]{1,0:T(8,128)(2,1)S(1)}, u32[]{:S(2)}, u32[]{:S(2)}) collective-permute-start(bf16[64,768]{1,0:T(8,128)(2,1)S(1)} %get-tuple-element.31), channel_id=1, source_target_pairs={{0,4},{4,0},{8,12},{12,8},{1,5},{5,1},{9,13},{13,9},{2,6},{6,2},{1... | collective-permute-start | bytes 294920 | tf_op jit(solution)/shard_map/ppermute | solution.py:17
  69.9 1.6 %collective-permute-start.12 = (bf16[64,768]{1,0:T(8,128)(2,1)S(1)}, bf16[64,768]{1,0:T(8,128)(2,1)S(1)}, u32[]{:S(2)}, u32[]{:S(2)}) collective-permute-start(bf16[64,768]{1,0:T(8,128)(2,1)S(1)} %get-tuple-element.32), channel_id=1, source_target_pairs={{0,12},{4,8},{8,4},{12,0},{1,13},{5,9},{9,5},{13,1},{2,14},{6,10},... | collective-permute-start | bytes 294920 | tf_op jit(solution)/shard_map/ppermute | solution.py:17
  71.5 0.2 collective-permute-start.11
  71.7 2.2 %collective-permute-done.16 = bf16[64,768]{1,0:T(8,128)(2,1)S(1)} collective-permute-done((bf16[64,768]{1,0:T(8,128)(2,1)S(1)}, bf16[64,768]{1,0:T(8,128)(2,1)S(1)}, u32[]{:S(2)}, u32[]{:S(2)}) %collective-permute-start.16) | collective-permute-done | bytes 98336 | tf_op jit(solution)/shard_map/ppermute | solution.py:17
  73.9 0.0 collective-permute-done.17
  73.9 0.0 collective-permute-done.10
  73.9 1.6 %collective-permute-done.12 = bf16[64,768]{1,0:T(8,128)(2,1)S(1)} collective-permute-done((bf16[64,768]{1,0:T(8,128)(2,1)S(1)}, bf16[64,768]{1,0:T(8,128)(2,1)S(1)}, u32[]{:S(2)}, u32[]{:S(2)}) %collective-permute-start.12) | collective-permute-done | bytes 98336 | tf_op jit(solution)/shard_map/ppermute | solution.py:17
  75.5 1.0 %collective-permute-done.11 = bf16[64,768]{1,0:T(8,128)(2,1)S(1)} collective-permute-done((bf16[64,768]{1,0:T(8,128)(2,1)S(1)}, bf16[64,768]{1,0:T(8,128)(2,1)S(1)}, u32[]{:S(2)}, u32[]{:S(2)}) %collective-permute-start.11) | collective-permute-done | bytes 98336 | tf_op jit(solution)/shard_map/ppermute | solution.py:17
  76.5 0.7 fusion.4
  (3 shorter events, 0.1 us)
Async XLA Ops:
  0.0 7.4 %collective-permute-start.2 = (bf16[64,768]{1,0:T(8,128)(2,1)}, bf16[64,768]{1,0:T(8,128)(2,1)S(1)}, u32[]{:S(2)}, u32[]{:S(2)}) collective-permute-start(bf16[64,768]{1,0:T(8,128)(2,1)} %refs_0_.1), channel_id=1, source_target_pairs={{0,12},{4,8},{8,4},{12,0},{1,13},{5,9},{9,5},{13,1},{2,14},{6,10},... | collective-permute-start | bytes 294920 | tf_op jit(solution)/shard_map/ppermute | solution.py:17
  3.9 5.1 %collective-permute-start.1 = (bf16[64,768]{1,0:T(8,128)(2,1)}, bf16[64,768]{1,0:T(8,128)(2,1)S(1)}, u32[]{:S(2)}, u32[]{:S(2)}) collective-permute-start(bf16[64,768]{1,0:T(8,128)(2,1)} %refs_0_.1), channel_id=1, source_target_pairs={{0,8},{4,12},{8,0},{12,4},{1,9},{5,13},{9,1},{13,5},{2,10},{6,14},... | collective-permute-start | bytes 294920 | tf_op jit(solution)/shard_map/ppermute | solution.py:17
  4.4 4.9 %collective-permute-start = (bf16[64,768]{1,0:T(8,128)(2,1)}, bf16[64,768]{1,0:T(8,128)(2,1)S(1)}, u32[]{:S(2)}, u32[]{:S(2)}) collective-permute-start(bf16[64,768]{1,0:T(8,128)(2,1)} %refs_0_.1), channel_id=1, source_target_pairs={{0,4},{4,0},{8,12},{12,8},{1,5},{5,1},{9,13},{13,9},{2,6},{6,2},{1... | collective-permute-start | bytes 294920 | tf_op jit(solution)/shard_map/ppermute | solution.py:17
  10.3 26.6 %collective-permute-start.3 = (bf16[256,768]{1,0:T(8,128)(2,1)S(1)}, bf16[256,768]{1,0:T(8,128)(2,1)S(1)}, u32[]{:S(2)}, u32[]{:S(2)}) collective-permute-start(bf16[256,768]{1,0:T(8,128)(2,1)S(1)} %shard_map.55.refs_0_), channel_id=1, source_target_pairs={{0,1},{1,0},{2,3},{3,2},{4,5},{5,4},{6,7},{7,6},{8,9},{9,8},{10,11... | collective-permute-start | bytes 1179656 | tf_op jit(solution)/shard_map/ppermute | solution.py:17
  11.9 14.2 %collective-permute-start.5 = (bf16[64,768]{1,0:T(8,128)(2,1)}, bf16[64,768]{1,0:T(8,128)(2,1)S(1)}, u32[]{:S(2)}, u32[]{:S(2)}) collective-permute-start(bf16[64,768]{1,0:T(8,128)(2,1)} %refs_0_.1), channel_id=1, source_target_pairs={{0,3},{1,2},{2,1},{3,0},{4,7},{5,6},{6,5},{7,4},{8,11},{9,10},{10,... | collective-permute-start | bytes 294920 | tf_op jit(solution)/shard_map/ppermute | solution.py:17
  14.4 11.7 %collective-permute-start.4 = (bf16[64,768]{1,0:T(8,128)(2,1)}, bf16[64,768]{1,0:T(8,128)(2,1)S(1)}, u32[]{:S(2)}, u32[]{:S(2)}) collective-permute-start(bf16[64,768]{1,0:T(8,128)(2,1)} %refs_0_.1), channel_id=1, source_target_pairs={{0,2},{1,3},{2,0},{3,1},{4,6},{5,7},{6,4},{7,5},{8,10},{9,11},{10,... | collective-permute-start | bytes 294920 | tf_op jit(solution)/shard_map/ppermute | solution.py:17
  26.1 10.5 %collective-permute-start.8 = (bf16[64,1664]{1,0:T(8,128)(2,1)S(1)}, bf16[64,1664]{1,0:T(8,128)(2,1)S(1)}, u32[]{:S(2)}, u32[]{:S(2)}) collective-permute-start(bf16[64,1664]{1,0:T(8,128)(2,1)S(1)} %shard_map.57.after.refs_2_), channel_id=1, source_target_pairs={{0,12},{4,8},{8,4},{12,0},{1,13},{5,9},{9,5},{13,1},{2,14},{6,10},... | collective-permute-start | bytes 638984 | tf_op jit(solution)/shard_map/ppermute | solution.py:17
  27.2 9.5 %collective-permute-start.7 = (bf16[64,1664]{1,0:T(8,128)(2,1)S(1)}, bf16[64,1664]{1,0:T(8,128)(2,1)S(1)}, u32[]{:S(2)}, u32[]{:S(2)}) collective-permute-start(bf16[64,1664]{1,0:T(8,128)(2,1)S(1)} %shard_map.57.after.refs_2_), channel_id=1, source_target_pairs={{0,8},{4,12},{8,0},{12,4},{1,9},{5,13},{9,1},{13,5},{2,10},{6,14},... | collective-permute-start | bytes 638984 | tf_op jit(solution)/shard_map/ppermute | solution.py:17
  29.4 7.5 %collective-permute-start.6 = (bf16[64,1664]{1,0:T(8,128)(2,1)S(1)}, bf16[64,1664]{1,0:T(8,128)(2,1)S(1)}, u32[]{:S(2)}, u32[]{:S(2)}) collective-permute-start(bf16[64,1664]{1,0:T(8,128)(2,1)S(1)} %shard_map.57.after.refs_2_), channel_id=1, source_target_pairs={{0,4},{4,0},{8,12},{12,8},{1,5},{5,1},{9,13},{13,9},{2,6},{6,2},{1... | collective-permute-start | bytes 638984 | tf_op jit(solution)/shard_map/ppermute | solution.py:17
  50.6 13.7 %collective-permute-start.13 = (bf16[64,1536]{1,0:T(8,128)(2,1)S(1)}, bf16[64,1536]{1,0:T(8,128)(2,1)S(1)}, u32[]{:S(2)}, u32[]{:S(2)}) collective-permute-start(bf16[64,1536]{1,0:T(8,128)(2,1)S(1)} %get-tuple-element.26), channel_id=1, source_target_pairs={{0,4},{4,0},{8,12},{12,8},{1,5},{5,1},{9,13},{13,9},{2,6},{6,2},{1... | collective-permute-start | bytes 589832 | tf_op jit(solution)/shard_map/ppermute | solution.py:17
  52.2 12.1 %collective-permute-start.14 = (bf16[64,1536]{1,0:T(8,128)(2,1)S(1)}, bf16[64,1536]{1,0:T(8,128)(2,1)S(1)}, u32[]{:S(2)}, u32[]{:S(2)}) collective-permute-start(bf16[64,1536]{1,0:T(8,128)(2,1)S(1)} %get-tuple-element.27), channel_id=1, source_target_pairs={{0,8},{4,12},{8,0},{12,4},{1,9},{5,13},{9,1},{13,5},{2,10},{6,14},... | collective-permute-start | bytes 589832 | tf_op jit(solution)/shard_map/ppermute | solution.py:17
  52.6 11.7 %collective-permute-start.15 = (bf16[64,1536]{1,0:T(8,128)(2,1)S(1)}, bf16[64,1536]{1,0:T(8,128)(2,1)S(1)}, u32[]{:S(2)}, u32[]{:S(2)}) collective-permute-start(bf16[64,1536]{1,0:T(8,128)(2,1)S(1)} %get-tuple-element.28), channel_id=1, source_target_pairs={{0,12},{4,8},{8,4},{12,0},{1,13},{5,9},{9,5},{13,1},{2,14},{6,10},... | collective-permute-start | bytes 589832 | tf_op jit(solution)/shard_map/ppermute | solution.py:17
  56.2 11.8 %collective-permute-start.9 = (bf16[256,768]{1,0:T(8,128)(2,1)S(1)}, bf16[256,768]{1,0:T(8,128)(2,1)S(1)}, u32[]{:S(2)}, u32[]{:S(2)}) collective-permute-start(bf16[256,768]{1,0:T(8,128)(2,1)S(1)} %shard_map.61), channel_id=1, source_target_pairs={{0,1},{1,0},{2,3},{3,2},{4,5},{5,4},{6,7},{7,6},{8,9},{9,8},{10,11... | collective-permute-start | bytes 1179656 | tf_op jit(solution)/shard_map/ppermute | solution.py:17
  64.5 9.4 %collective-permute-start.16 = (bf16[64,768]{1,0:T(8,128)(2,1)S(1)}, bf16[64,768]{1,0:T(8,128)(2,1)S(1)}, u32[]{:S(2)}, u32[]{:S(2)}) collective-permute-start(bf16[64,768]{1,0:T(8,128)(2,1)S(1)} %get-tuple-element.34), channel_id=1, source_target_pairs={{0,2},{1,3},{2,0},{3,1},{4,6},{5,7},{6,4},{7,5},{8,10},{9,11},{10,... | collective-permute-start | bytes 294920 | tf_op jit(solution)/shard_map/ppermute | solution.py:17
  65.3 8.6 %collective-permute-start.17 = (bf16[64,768]{1,0:T(8,128)(2,1)S(1)}, bf16[64,768]{1,0:T(8,128)(2,1)S(1)}, u32[]{:S(2)}, u32[]{:S(2)}) collective-permute-start(bf16[64,768]{1,0:T(8,128)(2,1)S(1)} %get-tuple-element.35), channel_id=1, source_target_pairs={{0,3},{1,2},{2,1},{3,0},{4,7},{5,6},{6,5},{7,4},{8,11},{9,10},{10,... | collective-permute-start | bytes 294920 | tf_op jit(solution)/shard_map/ppermute | solution.py:17
  68.1 5.8 %collective-permute-start.10 = (bf16[64,768]{1,0:T(8,128)(2,1)S(1)}, bf16[64,768]{1,0:T(8,128)(2,1)S(1)}, u32[]{:S(2)}, u32[]{:S(2)}) collective-permute-start(bf16[64,768]{1,0:T(8,128)(2,1)S(1)} %get-tuple-element.31), channel_id=1, source_target_pairs={{0,4},{4,0},{8,12},{12,8},{1,5},{5,1},{9,13},{13,9},{2,6},{6,2},{1... | collective-permute-start | bytes 294920 | tf_op jit(solution)/shard_map/ppermute | solution.py:17
  69.9 5.6 %collective-permute-start.12 = (bf16[64,768]{1,0:T(8,128)(2,1)S(1)}, bf16[64,768]{1,0:T(8,128)(2,1)S(1)}, u32[]{:S(2)}, u32[]{:S(2)}) collective-permute-start(bf16[64,768]{1,0:T(8,128)(2,1)S(1)} %get-tuple-element.32), channel_id=1, source_target_pairs={{0,12},{4,8},{8,4},{12,0},{1,13},{5,9},{9,5},{13,1},{2,14},{6,10},... | collective-permute-start | bytes 294920 | tf_op jit(solution)/shard_map/ppermute | solution.py:17
  71.5 5.0 %collective-permute-start.11 = (bf16[64,768]{1,0:T(8,128)(2,1)S(1)}, bf16[64,768]{1,0:T(8,128)(2,1)S(1)}, u32[]{:S(2)}, u32[]{:S(2)}) collective-permute-start(bf16[64,768]{1,0:T(8,128)(2,1)S(1)} %get-tuple-element.33), channel_id=1, source_target_pairs={{0,8},{4,12},{8,0},{12,4},{1,9},{5,13},{9,1},{13,5},{2,10},{6,14},... | collective-permute-start | bytes 294920 | tf_op jit(solution)/shard_map/ppermute | solution.py:17

commit v7 on v6

--- a/solution.py
+++ b/solution.py
@@ -204,12 +204,12 @@
     for e, held in enumerate(w_held):
         half = held.shape[1] // 2
 
-        def from_held(f, carry, e=e, held=held):
-            cols = pl.ds(pl.multiple_of(f * half, LANES), half)
-            up(slice(e * rows, (e + 1) * rows), cols, held[:, cols])
-            return carry
-
-        lax.fori_loop(0, 2, from_held, 0)
+        @pl.when(place[0] >= 0)
+        def _(e=e, held=held, half=half):
+            for f in range(2):
+                cols = slice(f * half, (f + 1) * half)
+                up(slice(e * rows, (e + 1) * rows), cols, held[:, cols])
+
         for copy in copies[e]:
             copy.start()
 

time: 77.4 us -> 77.3 us (level)
  no operation moved by 1% of the time
where the time goes in v7:
time: 77.3 us; the launch traced here: 77.1 us
  Pallas kernels  33.2 us (43%)
  starting transfers between devices  25.4 us (33%)
  waiting for transfers between devices  17.4 us (23%)
  other arithmetic  0.99 us (1%)
    pallas_call x7, Pallas kernels, call(): pl.pallas_call(body, in_specs=[pl.BlockSpec(memory_space=space) for _, sp...  33.2 us
    ppermute x18, starting transfers between devices, hop(): return lax.ppermute(value, axis, [(i, i ^ k) for i in range(n)])  25.4 us
    ppermute x18, waiting for transfers between devices, hop(): return lax.ppermute(value, axis, [(i, i ^ k) for i in range(n)])  17.4 us
  transfers between devices with their start and end apart: 18, of which 9 were waited for; matrix products, arithmetic and copies ran while one was open for 0% of the time, Pallas kernels for 24%

profile of v7, /device:TPU:0, one launch (start us, length us, event | category | flops | bytes accessed | tf_op | source)
XLA Modules:
  0.0 77.1 jit_solution(668008705327770693)
XLA Ops:
  0.0 3.9 %collective-permute-start.2 = (bf16[64,768]{1,0:T(8,128)(2,1)}, bf16[64,768]{1,0:T(8,128)(2,1)S(1)}, u32[]{:S(2)}, u32[]{:S(2)}) collective-permute-start(bf16[64,768]{1,0:T(8,128)(2,1)} %refs_0_.1), channel_id=1, source_target_pairs={{0,12},{4,8},{8,4},{12,0},{1,13},{5,9},{9,5},{13,1},{2,14},{6,10},... | collective-permute-start | bytes 294920 | tf_op jit(solution)/shard_map/ppermute | solution.py:17
  3.9 0.5 collective-permute-start.1
  4.4 0.1 collective-permute-start
  4.5 2.9 %collective-permute-done.2.refs_3_ = bf16[64,768]{1,0:T(8,128)(2,1)S(1)} collective-permute-done((bf16[64,768]{1,0:T(8,128)(2,1)}, bf16[64,768]{1,0:T(8,128)(2,1)S(1)}, u32[]{:S(2)}, u32[]{:S(2)}) %collective-permute-start.2) | collective-permute-done | bytes 98336 | tf_op jit(solution)/shard_map/ppermute | solution.py:17
  7.4 1.6 %collective-permute-done.1.refs_2_ = bf16[64,768]{1,0:T(8,128)(2,1)S(1)} collective-permute-done((bf16[64,768]{1,0:T(8,128)(2,1)}, bf16[64,768]{1,0:T(8,128)(2,1)S(1)}, u32[]{:S(2)}, u32[]{:S(2)}) %collective-permute-start.1) | collective-permute-done | bytes 98336 | tf_op jit(solution)/shard_map/ppermute | solution.py:17
  9.0 0.3 collective-permute-done.refs_1_
  9.4 0.9 %shard_map.55.refs_0_ = bf16[256,768]{1,0:T(8,128)(2,1)S(1)} custom-call(bf16[64,768]{1,0:T(8,128)(2,1)} %refs_0_.1, bf16[64,768]{1,0:T(8,128)(2,1)S(1)} %collective-permute-done.refs_1_, bf16[64,768]{1,0:T(8,128)(2,1)S(1)} %collective-permute-done.1.refs_2_, bf16[64,768]{1,0:T(8,128)(2,1)S(1)} %collective-permute-done.2.refs_3_), custom_call_target="tpu_custom_call" | custom-call | tf_op jit(solution)/shard_map/pallas_call | solution.py:25
  10.3 1.6 %collective-permute-start.3 = (bf16[256,768]{1,0:T(8,128)(2,1)S(1)}, bf16[256,768]{1,0:T(8,128)(2,1)S(1)}, u32[]{:S(2)}, u32[]{:S(2)}) collective-permute-start(bf16[256,768]{1,0:T(8,128)(2,1)S(1)} %shard_map.55.refs_0_), channel_id=1, source_target_pairs={{0,1},{1,0},{2,3},{3,2},{4,5},{5,4},{6,7},{7,6},{8,9},{9,8},{10,11... | collective-permute-start | bytes 1179656 | tf_op jit(solution)/shard_map/ppermute | solution.py:17
  11.9 2.5 %collective-permute-start.5 = (bf16[64,768]{1,0:T(8,128)(2,1)}, bf16[64,768]{1,0:T(8,128)(2,1)S(1)}, u32[]{:S(2)}, u32[]{:S(2)}) collective-permute-start(bf16[64,768]{1,0:T(8,128)(2,1)} %refs_0_.1), channel_id=1, source_target_pairs={{0,3},{1,2},{2,1},{3,0},{4,7},{5,6},{6,5},{7,4},{8,11},{9,10},{10,... | collective-permute-start | bytes 294920 | tf_op jit(solution)/shard_map/ppermute | solution.py:17
  14.4 0.1 collective-permute-start.4
  14.5 0.1 pad_add_fusion.place
  14.6 4.3 %shard_map.56 = (bf16[64,128]{1,0:T(8,128)(2,1)S(1)}, bf16[3072,1536]{1,0:T(8,128)(2,1)S(1)}) custom-call(s32[2]{0:T(128)S(1)} %pad_add_fusion.place, s32[4,64]{1,0:T(4,128)} %bitcast.4, f32[4,64]{1,0:T(4,128)} %bitcast.5, bf16[4,3072,1536]{2,1,0:T(8,128)(2,1)} %refs_9_.1), custom_call_target="tpu_custom_call" | custom-call | tf_op jit(solution)/shard_map/pallas_call | solution.py:25
  18.9 7.2 %collective-permute-done.5.refs_1_ = bf16[64,768]{1,0:T(8,128)(2,1)S(1)} collective-permute-done((bf16[64,768]{1,0:T(8,128)(2,1)}, bf16[64,768]{1,0:T(8,128)(2,1)S(1)}, u32[]{:S(2)}, u32[]{:S(2)}) %collective-permute-start.5) | collective-permute-done | bytes 98336 | tf_op jit(solution)/shard_map/ppermute | solution.py:17
  26.1 0.0 collective-permute-done.4.refs_0_
  26.1 1.0 %collective-permute-start.8 = (bf16[64,1664]{1,0:T(8,128)(2,1)S(1)}, bf16[64,1664]{1,0:T(8,128)(2,1)S(1)}, u32[]{:S(2)}, u32[]{:S(2)}) collective-permute-start(bf16[64,1664]{1,0:T(8,128)(2,1)S(1)} %shard_map.57.after.refs_2_), channel_id=1, source_target_pairs={{0,12},{4,8},{8,4},{12,0},{1,13},{5,9},{9,5},{13,1},{2,14},{6,10},... | collective-permute-start | bytes 638984 | tf_op jit(solution)/shard_map/ppermute | solution.py:17
  27.2 2.2 %collective-permute-start.7 = (bf16[64,1664]{1,0:T(8,128)(2,1)S(1)}, bf16[64,1664]{1,0:T(8,128)(2,1)S(1)}, u32[]{:S(2)}, u32[]{:S(2)}) collective-permute-start(bf16[64,1664]{1,0:T(8,128)(2,1)S(1)} %shard_map.57.after.refs_2_), channel_id=1, source_target_pairs={{0,8},{4,12},{8,0},{12,4},{1,9},{5,13},{9,1},{13,5},{2,10},{6,14},... | collective-permute-start | bytes 638984 | tf_op jit(solution)/shard_map/ppermute | solution.py:17
  29.4 0.3 collective-permute-start.6
  29.7 6.9 %shard_map.58 = (bf16[3072,1536]{1,0:T(8,128)(2,1)S(1)}, bf16[3072,1536]{1,0:T(8,128)(2,1)S(1)}) custom-call(bf16[4,3072,1536]{2,1,0:T(8,128)(2,1)} %refs_9_.1, bf16[64,1664]{1,0:T(8,128)(2,1)S(1)} %shard_map.57.after.refs_2_, s32[2]{0:T(128)S(1)} %pad_add_fusion.place), custom_call_target="tpu_custom_call" | custom-call | bytes 18874368 | tf_op jit(solution)/shard_map/pallas_call | solution.py:25
  36.6 0.0 collective-permute-done.8.refs_5_
  36.6 0.0 collective-permute-done.7.refs_4_
  36.7 0.2 collective-permute-done.6.refs_3_
  36.8 0.0 collective-permute-done.3.refs_1_
  36.8 13.6 %shard_map.59 = (bf16[64,1536]{1,0:T(8,128)(2,1)S(1)}, bf16[64,1536]{1,0:T(8,128)(2,1)S(1)}, bf16[64,1536]{1,0:T(8,128)(2,1)S(1)}, bf16[64,1536]{1,0:T(8,128)(2,...) custom-call(s32[2]{0:T(128)S(1)} %pad_add_fusion.place, ...), custom_call_target="tpu_custom_call", output_to_operand_aliasing={{7}: (7, {}), {8}: (8, {}), {9}: (9, {})} | custom-call | flops 9663676416 | bytes 37748736 | tf_op jit(solution)/shard_map/pallas_call | solution.py:25
  50.5 1.6 %collective-permute-start.13 = (bf16[64,1536]{1,0:T(8,128)(2,1)S(1)}, bf16[64,1536]{1,0:T(8,128)(2,1)S(1)}, u32[]{:S(2)}, u32[]{:S(2)}) collective-permute-start(bf16[64,1536]{1,0:T(8,128)(2,1)S(1)} %get-tuple-element.26), channel_id=1, source_target_pairs={{0,4},{4,0},{8,12},{12,8},{1,5},{5,1},{9,13},{13,9},{2,6},{6,2},{1... | collective-permute-start | bytes 589832 | tf_op jit(solution)/shard_map/ppermute | solution.py:17
  52.1 0.4 collective-permute-start.14
  52.5 1.5 %collective-permute-start.15 = (bf16[64,1536]{1,0:T(8,128)(2,1)S(1)}, bf16[64,1536]{1,0:T(8,128)(2,1)S(1)}, u32[]{:S(2)}, u32[]{:S(2)}) collective-permute-start(bf16[64,1536]{1,0:T(8,128)(2,1)S(1)} %get-tuple-element.28), channel_id=1, source_target_pairs={{0,12},{4,8},{8,4},{12,0},{1,13},{5,9},{9,5},{13,1},{2,14},{6,10},... | collective-permute-start | bytes 589832 | tf_op jit(solution)/shard_map/ppermute | solution.py:17
  54.0 2.1 %shard_map.61 = bf16[256,768]{1,0:T(8,128)(2,1)S(1)} custom-call(bf16[384,1536]{1,0:T(8,128)(2,1)S(1)} %get-tuple-element.21.hidden, bf16[256,384]{1,0:T(8,128)(2,1)S(1)} %get-tuple-element.22.pick_t, f32[384,1]{1,0:T(8,128)S(1)} %get-tuple-element.23.row_w, bf16[3072,1536]{1,0:T(8,128)(2,1)S(1)} %get-tuple-element.24.weights), custom_call_target="tpu_custom_call" | custom-call | flops 2415919104 | tf_op jit(solution)/shard_map/pallas_call | solution.py:25
  56.1 2.7 %collective-permute-start.9 = (bf16[256,768]{1,0:T(8,128)(2,1)S(1)}, bf16[256,768]{1,0:T(8,128)(2,1)S(1)}, u32[]{:S(2)}, u32[]{:S(2)}) collective-permute-start(bf16[256,768]{1,0:T(8,128)(2,1)S(1)} %shard_map.61), channel_id=1, source_target_pairs={{0,1},{1,0},{2,3},{3,2},{4,5},{5,4},{6,7},{7,6},{8,9},{9,8},{10,11... | collective-permute-start | bytes 1179656 | tf_op jit(solution)/shard_map/ppermute | solution.py:17
  58.8 5.4 %shard_map.60 = f32[256,768]{1,0:T(8,128)S(1)} custom-call(s32[2]{0:T(128)S(1)} %pad_add_fusion.place, bf16[384,1536]{1,0:T(8,128)(2,1)S(1)} %get-tuple-element.21.hidden, bf16[256,384]{1,0:T(8,128)(2,1)S(1)} %get-tuple-element.22.pick_t, f32[384,1]{1,0:T(8,128)S(1)} %get-tuple-element.23.row_w, bf16[4,1536,3072]{2,1,0:T(8,128)(2,1)} %w_down.1), custom_call_target="tpu_custom_call" | custom-call | flops 2415919104 | bytes 9437184 | tf_op jit(solution)/shard_map/pallas_call | solution.py:25
  64.2 0.0 collective-permute-done.13
  64.2 0.0 collective-permute-done.14
  64.2 0.0 collective-permute-done.15
  64.3 0.1 add_convert_fusion
  64.4 0.8 %collective-permute-start.16 = (bf16[64,768]{1,0:T(8,128)(2,1)S(1)}, bf16[64,768]{1,0:T(8,128)(2,1)S(1)}, u32[]{:S(2)}, u32[]{:S(2)}) collective-permute-start(bf16[64,768]{1,0:T(8,128)(2,1)S(1)} %get-tuple-element.34), channel_id=1, source_target_pairs={{0,2},{1,3},{2,0},{3,1},{4,6},{5,7},{6,4},{7,5},{8,10},{9,11},{10,... | collective-permute-start | bytes 294920 | tf_op jit(solution)/shard_map/ppermute | solution.py:17
  65.2 2.5 %collective-permute-start.17 = (bf16[64,768]{1,0:T(8,128)(2,1)S(1)}, bf16[64,768]{1,0:T(8,128)(2,1)S(1)}, u32[]{:S(2)}, u32[]{:S(2)}) collective-permute-start(bf16[64,768]{1,0:T(8,128)(2,1)S(1)} %get-tuple-element.35), channel_id=1, source_target_pairs={{0,3},{1,2},{2,1},{3,0},{4,7},{5,6},{6,5},{7,4},{8,11},{9,10},{10,... | collective-permute-start | bytes 294920 | tf_op jit(solution)/shard_map/ppermute | solution.py:17
  67.6 0.3 collective-permute-done.9
  67.9 0.1 fusion.5
  68.0 1.8 %collective-permute-start.10 = (bf16[64,768]{1,0:T(8,128)(2,1)S(1)}, bf16[64,768]{1,0:T(8,128)(2,1)S(1)}, u32[]{:S(2)}, u32[]{:S(2)}) collective-permute-start(bf16[64,768]{1,0:T(8,128)(2,1)S(1)} %get-tuple-element.31), channel_id=1, source_target_pairs={{0,4},{4,0},{8,12},{12,8},{1,5},{5,1},{9,13},{13,9},{2,6},{6,2},{1... | collective-permute-start | bytes 294920 | tf_op jit(solution)/shard_map/ppermute | solution.py:17
  69.8 1.6 %collective-permute-start.12 = (bf16[64,768]{1,0:T(8,128)(2,1)S(1)}, bf16[64,768]{1,0:T(8,128)(2,1)S(1)}, u32[]{:S(2)}, u32[]{:S(2)}) collective-permute-start(bf16[64,768]{1,0:T(8,128)(2,1)S(1)} %get-tuple-element.32), channel_id=1, source_target_pairs={{0,12},{4,8},{8,4},{12,0},{1,13},{5,9},{9,5},{13,1},{2,14},{6,10},... | collective-permute-start | bytes 294920 | tf_op jit(solution)/shard_map/ppermute | solution.py:17
  71.4 0.2 collective-permute-start.11
  71.6 2.2 %collective-permute-done.16 = bf16[64,768]{1,0:T(8,128)(2,1)S(1)} collective-permute-done((bf16[64,768]{1,0:T(8,128)(2,1)S(1)}, bf16[64,768]{1,0:T(8,128)(2,1)S(1)}, u32[]{:S(2)}, u32[]{:S(2)}) %collective-permute-start.16) | collective-permute-done | bytes 98336 | tf_op jit(solution)/shard_map/ppermute | solution.py:17
  73.8 0.0 collective-permute-done.17
  73.8 0.0 collective-permute-done.10
  73.8 1.6 %collective-permute-done.12 = bf16[64,768]{1,0:T(8,128)(2,1)S(1)} collective-permute-done((bf16[64,768]{1,0:T(8,128)(2,1)S(1)}, bf16[64,768]{1,0:T(8,128)(2,1)S(1)}, u32[]{:S(2)}, u32[]{:S(2)}) %collective-permute-start.12) | collective-permute-done | bytes 98336 | tf_op jit(solution)/shard_map/ppermute | solution.py:17
  75.4 1.0 %collective-permute-done.11 = bf16[64,768]{1,0:T(8,128)(2,1)S(1)} collective-permute-done((bf16[64,768]{1,0:T(8,128)(2,1)S(1)}, bf16[64,768]{1,0:T(8,128)(2,1)S(1)}, u32[]{:S(2)}, u32[]{:S(2)}) %collective-permute-start.11) | collective-permute-done | bytes 98336 | tf_op jit(solution)/shard_map/ppermute | solution.py:17
  76.4 0.7 fusion.4
  (3 shorter events, 0.1 us)
Async XLA Ops:
  0.0 7.4 %collective-permute-start.2 = (bf16[64,768]{1,0:T(8,128)(2,1)}, bf16[64,768]{1,0:T(8,128)(2,1)S(1)}, u32[]{:S(2)}, u32[]{:S(2)}) collective-permute-start(bf16[64,768]{1,0:T(8,128)(2,1)} %refs_0_.1), channel_id=1, source_target_pairs={{0,12},{4,8},{8,4},{12,0},{1,13},{5,9},{9,5},{13,1},{2,14},{6,10},... | collective-permute-start | bytes 294920 | tf_op jit(solution)/shard_map/ppermute | solution.py:17
  3.9 5.1 %collective-permute-start.1 = (bf16[64,768]{1,0:T(8,128)(2,1)}, bf16[64,768]{1,0:T(8,128)(2,1)S(1)}, u32[]{:S(2)}, u32[]{:S(2)}) collective-permute-start(bf16[64,768]{1,0:T(8,128)(2,1)} %refs_0_.1), channel_id=1, source_target_pairs={{0,8},{4,12},{8,0},{12,4},{1,9},{5,13},{9,1},{13,5},{2,10},{6,14},... | collective-permute-start | bytes 294920 | tf_op jit(solution)/shard_map/ppermute | solution.py:17
  4.4 4.9 %collective-permute-start = (bf16[64,768]{1,0:T(8,128)(2,1)}, bf16[64,768]{1,0:T(8,128)(2,1)S(1)}, u32[]{:S(2)}, u32[]{:S(2)}) collective-permute-start(bf16[64,768]{1,0:T(8,128)(2,1)} %refs_0_.1), channel_id=1, source_target_pairs={{0,4},{4,0},{8,12},{12,8},{1,5},{5,1},{9,13},{13,9},{2,6},{6,2},{1... | collective-permute-start | bytes 294920 | tf_op jit(solution)/shard_map/ppermute | solution.py:17
  10.3 26.6 %collective-permute-start.3 = (bf16[256,768]{1,0:T(8,128)(2,1)S(1)}, bf16[256,768]{1,0:T(8,128)(2,1)S(1)}, u32[]{:S(2)}, u32[]{:S(2)}) collective-permute-start(bf16[256,768]{1,0:T(8,128)(2,1)S(1)} %shard_map.55.refs_0_), channel_id=1, source_target_pairs={{0,1},{1,0},{2,3},{3,2},{4,5},{5,4},{6,7},{7,6},{8,9},{9,8},{10,11... | collective-permute-start | bytes 1179656 | tf_op jit(solution)/shard_map/ppermute | solution.py:17
  11.9 14.2 %collective-permute-start.5 = (bf16[64,768]{1,0:T(8,128)(2,1)}, bf16[64,768]{1,0:T(8,128)(2,1)S(1)}, u32[]{:S(2)}, u32[]{:S(2)}) collective-permute-start(bf16[64,768]{1,0:T(8,128)(2,1)} %refs_0_.1), channel_id=1, source_target_pairs={{0,3},{1,2},{2,1},{3,0},{4,7},{5,6},{6,5},{7,4},{8,11},{9,10},{10,... | collective-permute-start | bytes 294920 | tf_op jit(solution)/shard_map/ppermute | solution.py:17
  14.4 11.7 %collective-permute-start.4 = (bf16[64,768]{1,0:T(8,128)(2,1)}, bf16[64,768]{1,0:T(8,128)(2,1)S(1)}, u32[]{:S(2)}, u32[]{:S(2)}) collective-permute-start(bf16[64,768]{1,0:T(8,128)(2,1)} %refs_0_.1), channel_id=1, source_target_pairs={{0,2},{1,3},{2,0},{3,1},{4,6},{5,7},{6,4},{7,5},{8,10},{9,11},{10,... | collective-permute-start | bytes 294920 | tf_op jit(solution)/shard_map/ppermute | solution.py:17
  26.1 10.5 %collective-permute-start.8 = (bf16[64,1664]{1,0:T(8,128)(2,1)S(1)}, bf16[64,1664]{1,0:T(8,128)(2,1)S(1)}, u32[]{:S(2)}, u32[]{:S(2)}) collective-permute-start(bf16[64,1664]{1,0:T(8,128)(2,1)S(1)} %shard_map.57.after.refs_2_), channel_id=1, source_target_pairs={{0,12},{4,8},{8,4},{12,0},{1,13},{5,9},{9,5},{13,1},{2,14},{6,10},... | collective-permute-start | bytes 638984 | tf_op jit(solution)/shard_map/ppermute | solution.py:17
  27.2 9.5 %collective-permute-start.7 = (bf16[64,1664]{1,0:T(8,128)(2,1)S(1)}, bf16[64,1664]{1,0:T(8,128)(2,1)S(1)}, u32[]{:S(2)}, u32[]{:S(2)}) collective-permute-start(bf16[64,1664]{1,0:T(8,128)(2,1)S(1)} %shard_map.57.after.refs_2_), channel_id=1, source_target_pairs={{0,8},{4,12},{8,0},{12,4},{1,9},{5,13},{9,1},{13,5},{2,10},{6,14},... | collective-permute-start | bytes 638984 | tf_op jit(solution)/shard_map/ppermute | solution.py:17
  29.4 7.5 %collective-permute-start.6 = (bf16[64,1664]{1,0:T(8,128)(2,1)S(1)}, bf16[64,1664]{1,0:T(8,128)(2,1)S(1)}, u32[]{:S(2)}, u32[]{:S(2)}) collective-permute-start(bf16[64,1664]{1,0:T(8,128)(2,1)S(1)} %shard_map.57.after.refs_2_), channel_id=1, source_target_pairs={{0,4},{4,0},{8,12},{12,8},{1,5},{5,1},{9,13},{13,9},{2,6},{6,2},{1... | collective-permute-start | bytes 638984 | tf_op jit(solution)/shard_map/ppermute | solution.py:17
  50.5 13.7 %collective-permute-start.13 = (bf16[64,1536]{1,0:T(8,128)(2,1)S(1)}, bf16[64,1536]{1,0:T(8,128)(2,1)S(1)}, u32[]{:S(2)}, u32[]{:S(2)}) collective-permute-start(bf16[64,1536]{1,0:T(8,128)(2,1)S(1)} %get-tuple-element.26), channel_id=1, source_target_pairs={{0,4},{4,0},{8,12},{12,8},{1,5},{5,1},{9,13},{13,9},{2,6},{6,2},{1... | collective-permute-start | bytes 589832 | tf_op jit(solution)/shard_map/ppermute | solution.py:17
  52.1 12.1 %collective-permute-start.14 = (bf16[64,1536]{1,0:T(8,128)(2,1)S(1)}, bf16[64,1536]{1,0:T(8,128)(2,1)S(1)}, u32[]{:S(2)}, u32[]{:S(2)}) collective-permute-start(bf16[64,1536]{1,0:T(8,128)(2,1)S(1)} %get-tuple-element.27), channel_id=1, source_target_pairs={{0,8},{4,12},{8,0},{12,4},{1,9},{5,13},{9,1},{13,5},{2,10},{6,14},... | collective-permute-start | bytes 589832 | tf_op jit(solution)/shard_map/ppermute | solution.py:17
  52.5 11.7 %collective-permute-start.15 = (bf16[64,1536]{1,0:T(8,128)(2,1)S(1)}, bf16[64,1536]{1,0:T(8,128)(2,1)S(1)}, u32[]{:S(2)}, u32[]{:S(2)}) collective-permute-start(bf16[64,1536]{1,0:T(8,128)(2,1)S(1)} %get-tuple-element.28), channel_id=1, source_target_pairs={{0,12},{4,8},{8,4},{12,0},{1,13},{5,9},{9,5},{13,1},{2,14},{6,10},... | collective-permute-start | bytes 589832 | tf_op jit(solution)/shard_map/ppermute | solution.py:17
  56.1 11.8 %collective-permute-start.9 = (bf16[256,768]{1,0:T(8,128)(2,1)S(1)}, bf16[256,768]{1,0:T(8,128)(2,1)S(1)}, u32[]{:S(2)}, u32[]{:S(2)}) collective-permute-start(bf16[256,768]{1,0:T(8,128)(2,1)S(1)} %shard_map.61), channel_id=1, source_target_pairs={{0,1},{1,0},{2,3},{3,2},{4,5},{5,4},{6,7},{7,6},{8,9},{9,8},{10,11... | collective-permute-start | bytes 1179656 | tf_op jit(solution)/shard_map/ppermute | solution.py:17
  64.4 9.4 %collective-permute-start.16 = (bf16[64,768]{1,0:T(8,128)(2,1)S(1)}, bf16[64,768]{1,0:T(8,128)(2,1)S(1)}, u32[]{:S(2)}, u32[]{:S(2)}) collective-permute-start(bf16[64,768]{1,0:T(8,128)(2,1)S(1)} %get-tuple-element.34), channel_id=1, source_target_pairs={{0,2},{1,3},{2,0},{3,1},{4,6},{5,7},{6,4},{7,5},{8,10},{9,11},{10,... | collective-permute-start | bytes 294920 | tf_op jit(solution)/shard_map/ppermute | solution.py:17
  65.2 8.6 %collective-permute-start.17 = (bf16[64,768]{1,0:T(8,128)(2,1)S(1)}, bf16[64,768]{1,0:T(8,128)(2,1)S(1)}, u32[]{:S(2)}, u32[]{:S(2)}) collective-permute-start(bf16[64,768]{1,0:T(8,128)(2,1)S(1)} %get-tuple-element.35), channel_id=1, source_target_pairs={{0,3},{1,2},{2,1},{3,0},{4,7},{5,6},{6,5},{7,4},{8,11},{9,10},{10,... | collective-permute-start | bytes 294920 | tf_op jit(solution)/shard_map/ppermute | solution.py:17
  68.0 5.8 %collective-permute-start.10 = (bf16[64,768]{1,0:T(8,128)(2,1)S(1)}, bf16[64,768]{1,0:T(8,128)(2,1)S(1)}, u32[]{:S(2)}, u32[]{:S(2)}) collective-permute-start(bf16[64,768]{1,0:T(8,128)(2,1)S(1)} %get-tuple-element.31), channel_id=1, source_target_pairs={{0,4},{4,0},{8,12},{12,8},{1,5},{5,1},{9,13},{13,9},{2,6},{6,2},{1... | collective-permute-start | bytes 294920 | tf_op jit(solution)/shard_map/ppermute | solution.py:17
  69.8 5.6 %collective-permute-start.12 = (bf16[64,768]{1,0:T(8,128)(2,1)S(1)}, bf16[64,768]{1,0:T(8,128)(2,1)S(1)}, u32[]{:S(2)}, u32[]{:S(2)}) collective-permute-start(bf16[64,768]{1,0:T(8,128)(2,1)S(1)} %get-tuple-element.32), channel_id=1, source_target_pairs={{0,12},{4,8},{8,4},{12,0},{1,13},{5,9},{9,5},{13,1},{2,14},{6,10},... | collective-permute-start | bytes 294920 | tf_op jit(solution)/shard_map/ppermute | solution.py:17
  71.4 5.0 %collective-permute-start.11 = (bf16[64,768]{1,0:T(8,128)(2,1)S(1)}, bf16[64,768]{1,0:T(8,128)(2,1)S(1)}, u32[]{:S(2)}, u32[]{:S(2)}) collective-permute-start(bf16[64,768]{1,0:T(8,128)(2,1)S(1)} %get-tuple-element.33), channel_id=1, source_target_pairs={{0,8},{4,12},{8,0},{12,4},{1,9},{5,13},{9,1},{13,5},{2,10},{6,14},... | collective-permute-start | bytes 294920 | tf_op jit(solution)/shard_map/ppermute | solution.py:17

commit v8 on v7

--- a/solution.py
+++ b/solution.py
@@ -137,25 +137,21 @@
     ]
 
 
-def down_rows(hidden, weight, row_w, at, high, low):
+def down_rows(hidden, weight, row_w, at, high):
     result = jnp.dot(hidden[at, :], weight, preferred_element_type=jnp.float32)
-    result = result * row_w[at, :]
-    upper = result.astype(jnp.bfloat16)
-    high[at, :] = upper
-    low[at, :] = (result - upper.astype(jnp.float32)).astype(jnp.bfloat16)
-
-
-def combine(pick_t, high, low):
-    total = jnp.dot(pick_t[...], high[...], preferred_element_type=jnp.float32)
-    return total + jnp.dot(pick_t[...], low[...], preferred_element_type=jnp.float32)
-
-
-def down_slice(weights, hidden, pick_t, row_w, rows, n_loc, slice_d, high, low):
+    high[at, :] = (result * row_w[at, :]).astype(jnp.bfloat16)
+
+
+def combine(pick_t, high):
+    return jnp.dot(pick_t[...], high[...], preferred_element_type=jnp.float32)
+
+
+def down_slice(weights, hidden, pick_t, row_w, rows, n_loc, slice_d, high):
     for e in range(n_loc):
         at = slice(e * rows, (e + 1) * rows)
         weight = weights[piece(e, hidden.shape[1], slice_d)]
-        down_rows(hidden, weight, row_w, at, high, low)
-    return combine(pick_t, high, low)
+        down_rows(hidden, weight, row_w, at, high)
+    return combine(pick_t, high)
 
 
 def up_kernel(sizes, place, *refs):
@@ -167,7 +163,7 @@
     (w_up, w_down), refs = refs[:2], refs[2:]
     outs, refs = refs[:n_exp], refs[n_exp:]
     (hidden, pick_t, row_w), room, refs = refs[:3], refs[3:3 + n_held], refs[3 + n_held:]
-    pick, joined, packed, buf_u, sem_u, sem_a, high, low = refs
+    pick, joined, packed, buf_u, sem_u, sem_a, high = refs
     per = w_up.shape[2] // tile_f
     tiles = (n_loc - n_held) * per
     deep_u = buf_u.shape[0]
@@ -229,7 +225,7 @@
     for i in range(far):
         for copy in copies[i]:
             copy.wait()
-        total = down_slice(room[i], hidden, pick_t, row_w, rows, n_loc, slice_d, high, low)
+        total = down_slice(room[i], hidden, pick_t, row_w, rows, n_loc, slice_d, high)
         total = total.astype(jnp.bfloat16)
         for k, out in enumerate(outs):
             out[:, i * slice_d:(i + 1) * slice_d] = total[k * tok:(k + 1) * tok]
@@ -237,12 +233,12 @@
         copy.wait()
 
 
-def down_kernel(rows, n_loc, hidden, pick_t, row_w, weights, out, high, low):
-    total = down_slice(weights, hidden, pick_t, row_w, rows, n_loc, out.shape[1], high, low)
+def down_kernel(rows, n_loc, hidden, pick_t, row_w, weights, out, high):
+    total = down_slice(weights, hidden, pick_t, row_w, rows, n_loc, out.shape[1], high)
     out[...] = total.astype(out.dtype)
 
 
-def own_kernel(rows, place, hidden, pick_t, row_w, w_down, out, buf, sem, high, low):
+def own_kernel(rows, place, hidden, pick_t, row_w, w_down, out, buf, sem, high):
     n_loc = w_down.shape[0]
     at = pl.multiple_of(place[0] * out.shape[1], LANES)
     copies = [
@@ -253,15 +249,15 @@
         copy.start()
     for e, copy in enumerate(copies):
         copy.wait()
-        down_rows(hidden, buf[e], row_w, slice(e * rows, (e + 1) * rows), high, low)
-    out[...] = combine(pick_t, high, low).astype(out.dtype)
+        down_rows(hidden, buf[e], row_w, slice(e * rows, (e + 1) * rows), high)
+    out[...] = combine(pick_t, high).astype(out.dtype)
 
 
 def down_scratch(n_loc, rows, ff, slice_d, deep):
     bf16 = jnp.bfloat16
     return [
         pltpu.VMEM((deep, ff, slice_d), bf16), pltpu.SemaphoreType.DMA((deep,)),
-        pltpu.VMEM((n_loc * rows, slice_d), bf16), pltpu.VMEM((n_loc * rows, slice_d), bf16),
+        pltpu.VMEM((n_loc * rows, slice_d), bf16),
     ]
 
 
@@ -291,7 +287,7 @@
          pltpu.VMEM((3, width, tile_f), bf16),
          pltpu.SemaphoreType.DMA((3,)),
          pltpu.SemaphoreType.DMA((len(w_held), n_loc)),
-         pltpu.VMEM((n_loc * rows, slice_d), bf16), pltpu.VMEM((n_loc * rows, slice_d), bf16)],
+         pltpu.VMEM((n_loc * rows, slice_d), bf16)],
         15, flops=2 * n_loc * 256 * width * ff, moved=n_loc * ff * width * 2,
         aliases=[(3 + n_exp + i, n_exp + 3 + i) for i in range(len(w_held))],
     )
@@ -306,7 +302,7 @@
         functools.partial(down_kernel, rows, n_loc),
         [(x, pltpu.VMEM) for x in (hidden, pick_t, row_w, weights)],
         [jax.ShapeDtypeStruct((pick_t.shape[0], slice_d), dtype)],
-        [pltpu.VMEM((n_loc * rows, slice_d), bf16), pltpu.VMEM((n_loc * rows, slice_d), bf16)],
+        [pltpu.VMEM((n_loc * rows, slice_d), bf16)],
         16, flops=2 * n_loc * 256 * slice_d * ff,
     )[0]
 

time: 77.3 us -> 77.1 us (level)
  transfers between devices with their start and end apart: 18 -> 18, of which waited for: 9 -> 8; matrix products, arithmetic and copies ran while one was open for 0% -> 0% of each run, Pallas kernels for 24% -> 24%
where the time goes in v8:
time: 77.1 us; the launch traced here: 76.9 us
  Pallas kernels  32.8 us (43%)
  starting transfers between devices  25.8 us (33%)
  waiting for transfers between devices  17.2 us (22%)
  other arithmetic  0.99 us (1%)
    pallas_call x7, Pallas kernels, call(): pl.pallas_call(body, in_specs=[pl.BlockSpec(memory_space=space) for _, sp...  32.8 us
    ppermute x18, starting transfers between devices, hop(): return lax.ppermute(value, axis, [(i, i ^ k) for i in range(n)])  25.8 us
    ppermute x18, waiting for transfers between devices, hop(): return lax.ppermute(value, axis, [(i, i ^ k) for i in range(n)])  17.2 us
  transfers between devices with their start and end apart: 18, of which 8 were waited for; matrix products, arithmetic and copies ran while one was open for 0% of the time, Pallas kernels for 24%

profile of v8, /device:TPU:0, one launch (start us, length us, event | category | flops | bytes accessed | tf_op | source)
XLA Modules:
  0.0 76.9 jit_solution(2754913474187521146)
XLA Ops:
  0.0 3.9 %collective-permute-start.2 = (bf16[64,768]{1,0:T(8,128)(2,1)}, bf16[64,768]{1,0:T(8,128)(2,1)S(1)}, u32[]{:S(2)}, u32[]{:S(2)}) collective-permute-start(bf16[64,768]{1,0:T(8,128)(2,1)} %refs_0_.1), channel_id=1, source_target_pairs={{0,12},{4,8},{8,4},{12,0},{1,13},{5,9},{9,5},{13,1},{2,14},{6,10},... | collective-permute-start | bytes 294920 | tf_op jit(solution)/shard_map/ppermute | solution.py:17
  3.9 0.5 collective-permute-start.1
  4.4 0.1 collective-permute-start
  4.5 2.9 %collective-permute-done.2.refs_3_ = bf16[64,768]{1,0:T(8,128)(2,1)S(1)} collective-permute-done((bf16[64,768]{1,0:T(8,128)(2,1)}, bf16[64,768]{1,0:T(8,128)(2,1)S(1)}, u32[]{:S(2)}, u32[]{:S(2)}) %collective-permute-start.2) | collective-permute-done | bytes 98336 | tf_op jit(solution)/shard_map/ppermute | solution.py:17
  7.4 1.6 %collective-permute-done.1.refs_2_ = bf16[64,768]{1,0:T(8,128)(2,1)S(1)} collective-permute-done((bf16[64,768]{1,0:T(8,128)(2,1)}, bf16[64,768]{1,0:T(8,128)(2,1)S(1)}, u32[]{:S(2)}, u32[]{:S(2)}) %collective-permute-start.1) | collective-permute-done | bytes 98336 | tf_op jit(solution)/shard_map/ppermute | solution.py:17
  9.0 0.3 collective-permute-done.refs_1_
  9.4 0.9 %shard_map.55.refs_0_ = bf16[256,768]{1,0:T(8,128)(2,1)S(1)} custom-call(bf16[64,768]{1,0:T(8,128)(2,1)} %refs_0_.1, bf16[64,768]{1,0:T(8,128)(2,1)S(1)} %collective-permute-done.refs_1_, bf16[64,768]{1,0:T(8,128)(2,1)S(1)} %collective-permute-done.1.refs_2_, bf16[64,768]{1,0:T(8,128)(2,1)S(1)} %collective-permute-done.2.refs_3_), custom_call_target="tpu_custom_call" | custom-call | tf_op jit(solution)/shard_map/pallas_call | solution.py:25
  10.3 1.6 %collective-permute-start.3 = (bf16[256,768]{1,0:T(8,128)(2,1)S(1)}, bf16[256,768]{1,0:T(8,128)(2,1)S(1)}, u32[]{:S(2)}, u32[]{:S(2)}) collective-permute-start(bf16[256,768]{1,0:T(8,128)(2,1)S(1)} %shard_map.55.refs_0_), channel_id=1, source_target_pairs={{0,1},{1,0},{2,3},{3,2},{4,5},{5,4},{6,7},{7,6},{8,9},{9,8},{10,11... | collective-permute-start | bytes 1179656 | tf_op jit(solution)/shard_map/ppermute | solution.py:17
  11.9 2.5 %collective-permute-start.5 = (bf16[64,768]{1,0:T(8,128)(2,1)}, bf16[64,768]{1,0:T(8,128)(2,1)S(1)}, u32[]{:S(2)}, u32[]{:S(2)}) collective-permute-start(bf16[64,768]{1,0:T(8,128)(2,1)} %refs_0_.1), channel_id=1, source_target_pairs={{0,3},{1,2},{2,1},{3,0},{4,7},{5,6},{6,5},{7,4},{8,11},{9,10},{10,... | collective-permute-start | bytes 294920 | tf_op jit(solution)/shard_map/ppermute | solution.py:17
  14.4 0.1 collective-permute-start.4
  14.5 0.1 pad_add_fusion.place
  14.6 4.3 %shard_map.56 = (bf16[64,128]{1,0:T(8,128)(2,1)S(1)}, bf16[3072,1536]{1,0:T(8,128)(2,1)S(1)}) custom-call(s32[2]{0:T(128)S(1)} %pad_add_fusion.place, s32[4,64]{1,0:T(4,128)} %bitcast.4, f32[4,64]{1,0:T(4,128)} %bitcast.5, bf16[4,3072,1536]{2,1,0:T(8,128)(2,1)} %refs_9_.1), custom_call_target="tpu_custom_call" | custom-call | tf_op jit(solution)/shard_map/pallas_call | solution.py:25
  18.9 7.2 %collective-permute-done.5.refs_1_ = bf16[64,768]{1,0:T(8,128)(2,1)S(1)} collective-permute-done((bf16[64,768]{1,0:T(8,128)(2,1)}, bf16[64,768]{1,0:T(8,128)(2,1)S(1)}, u32[]{:S(2)}, u32[]{:S(2)}) %collective-permute-start.5) | collective-permute-done | bytes 98336 | tf_op jit(solution)/shard_map/ppermute | solution.py:17
  26.1 0.0 collective-permute-done.4.refs_0_
  26.1 1.0 %collective-permute-start.8 = (bf16[64,1664]{1,0:T(8,128)(2,1)S(1)}, bf16[64,1664]{1,0:T(8,128)(2,1)S(1)}, u32[]{:S(2)}, u32[]{:S(2)}) collective-permute-start(bf16[64,1664]{1,0:T(8,128)(2,1)S(1)} %shard_map.57.after.refs_2_), channel_id=1, source_target_pairs={{0,12},{4,8},{8,4},{12,0},{1,13},{5,9},{9,5},{13,1},{2,14},{6,10},... | collective-permute-start | bytes 638984 | tf_op jit(solution)/shard_map/ppermute | solution.py:17
  27.2 2.2 %collective-permute-start.7 = (bf16[64,1664]{1,0:T(8,128)(2,1)S(1)}, bf16[64,1664]{1,0:T(8,128)(2,1)S(1)}, u32[]{:S(2)}, u32[]{:S(2)}) collective-permute-start(bf16[64,1664]{1,0:T(8,128)(2,1)S(1)} %shard_map.57.after.refs_2_), channel_id=1, source_target_pairs={{0,8},{4,12},{8,0},{12,4},{1,9},{5,13},{9,1},{13,5},{2,10},{6,14},... | collective-permute-start | bytes 638984 | tf_op jit(solution)/shard_map/ppermute | solution.py:17
  29.4 0.3 collective-permute-start.6
  29.7 6.9 %shard_map.58 = (bf16[3072,1536]{1,0:T(8,128)(2,1)S(1)}, bf16[3072,1536]{1,0:T(8,128)(2,1)S(1)}) custom-call(bf16[4,3072,1536]{2,1,0:T(8,128)(2,1)} %refs_9_.1, bf16[64,1664]{1,0:T(8,128)(2,1)S(1)} %shard_map.57.after.refs_2_, s32[2]{0:T(128)S(1)} %pad_add_fusion.place), custom_call_target="tpu_custom_call" | custom-call | bytes 18874368 | tf_op jit(solution)/shard_map/pallas_call | solution.py:25
  36.6 0.0 collective-permute-done.8.refs_5_
  36.6 0.0 collective-permute-done.7.refs_4_
  36.7 0.2 collective-permute-done.6.refs_3_
  36.8 0.0 collective-permute-done.3.refs_1_
  36.8 13.6 %shard_map.59 = (bf16[64,1536]{1,0:T(8,128)(2,1)S(1)}, bf16[64,1536]{1,0:T(8,128)(2,1)S(1)}, bf16[64,1536]{1,0:T(8,128)(2,1)S(1)}, bf16[64,1536]{1,0:T(8,128)(2,...) custom-call(s32[2]{0:T(128)S(1)} %pad_add_fusion.place, ...), custom_call_target="tpu_custom_call", output_to_operand_aliasing={{7}: (7, {}), {8}: (8, {}), {9}: (9, {})} | custom-call | flops 9663676416 | bytes 37748736 | tf_op jit(solution)/shard_map/pallas_call | solution.py:25
  50.5 1.6 %collective-permute-start.13 = (bf16[64,1536]{1,0:T(8,128)(2,1)S(1)}, bf16[64,1536]{1,0:T(8,128)(2,1)S(1)}, u32[]{:S(2)}, u32[]{:S(2)}) collective-permute-start(bf16[64,1536]{1,0:T(8,128)(2,1)S(1)} %get-tuple-element.26), channel_id=1, source_target_pairs={{0,4},{4,0},{8,12},{12,8},{1,5},{5,1},{9,13},{13,9},{2,6},{6,2},{1... | collective-permute-start | bytes 589832 | tf_op jit(solution)/shard_map/ppermute | solution.py:17
  52.1 0.4 collective-permute-start.14
  52.5 1.5 %collective-permute-start.15 = (bf16[64,1536]{1,0:T(8,128)(2,1)S(1)}, bf16[64,1536]{1,0:T(8,128)(2,1)S(1)}, u32[]{:S(2)}, u32[]{:S(2)}) collective-permute-start(bf16[64,1536]{1,0:T(8,128)(2,1)S(1)} %get-tuple-element.28), channel_id=1, source_target_pairs={{0,12},{4,8},{8,4},{12,0},{1,13},{5,9},{9,5},{13,1},{2,14},{6,10},... | collective-permute-start | bytes 589832 | tf_op jit(solution)/shard_map/ppermute | solution.py:17
  54.0 1.8 %shard_map.61 = bf16[256,768]{1,0:T(8,128)(2,1)S(1)} custom-call(bf16[384,1536]{1,0:T(8,128)(2,1)S(1)} %get-tuple-element.21.hidden, bf16[256,384]{1,0:T(8,128)(2,1)S(1)} %get-tuple-element.22.pick_t, f32[384,1]{1,0:T(8,128)S(1)} %get-tuple-element.23.row_w, bf16[3072,1536]{1,0:T(8,128)(2,1)S(1)} %get-tuple-element.24.weights), custom_call_target="tpu_custom_call" | custom-call | flops 2415919104 | tf_op jit(solution)/shard_map/pallas_call | solution.py:25
  55.9 2.7 %collective-permute-start.9 = (bf16[256,768]{1,0:T(8,128)(2,1)S(1)}, bf16[256,768]{1,0:T(8,128)(2,1)S(1)}, u32[]{:S(2)}, u32[]{:S(2)}) collective-permute-start(bf16[256,768]{1,0:T(8,128)(2,1)S(1)} %shard_map.61), channel_id=1, source_target_pairs={{0,1},{1,0},{2,3},{3,2},{4,5},{5,4},{6,7},{7,6},{8,9},{9,8},{10,11... | collective-permute-start | bytes 1179656 | tf_op jit(solution)/shard_map/ppermute | solution.py:17
  58.6 5.2 %shard_map.60 = f32[256,768]{1,0:T(8,128)S(1)} custom-call(s32[2]{0:T(128)S(1)} %pad_add_fusion.place, bf16[384,1536]{1,0:T(8,128)(2,1)S(1)} %get-tuple-element.21.hidden, bf16[256,384]{1,0:T(8,128)(2,1)S(1)} %get-tuple-element.22.pick_t, f32[384,1]{1,0:T(8,128)S(1)} %get-tuple-element.23.row_w, bf16[4,1536,3072]{2,1,0:T(8,128)(2,1)} %w_down.1), custom_call_target="tpu_custom_call" | custom-call | flops 2415919104 | bytes 9437184 | tf_op jit(solution)/shard_map/pallas_call | solution.py:25
  63.8 0.0 collective-permute-done.13
  63.8 0.0 collective-permute-done.14
  63.8 0.0 collective-permute-done.15
  63.9 0.1 add_convert_fusion
  64.0 1.2 %collective-permute-start.16 = (bf16[64,768]{1,0:T(8,128)(2,1)S(1)}, bf16[64,768]{1,0:T(8,128)(2,1)S(1)}, u32[]{:S(2)}, u32[]{:S(2)}) collective-permute-start(bf16[64,768]{1,0:T(8,128)(2,1)S(1)} %get-tuple-element.34), channel_id=1, source_target_pairs={{0,2},{1,3},{2,0},{3,1},{4,6},{5,7},{6,4},{7,5},{8,10},{9,11},{10,... | collective-permute-start | bytes 294920 | tf_op jit(solution)/shard_map/ppermute | solution.py:17
  65.2 2.5 %collective-permute-start.17 = (bf16[64,768]{1,0:T(8,128)(2,1)S(1)}, bf16[64,768]{1,0:T(8,128)(2,1)S(1)}, u32[]{:S(2)}, u32[]{:S(2)}) collective-permute-start(bf16[64,768]{1,0:T(8,128)(2,1)S(1)} %get-tuple-element.35), channel_id=1, source_target_pairs={{0,3},{1,2},{2,1},{3,0},{4,7},{5,6},{6,5},{7,4},{8,11},{9,10},{10,... | collective-permute-start | bytes 294920 | tf_op jit(solution)/shard_map/ppermute | solution.py:17
  67.6 0.0 collective-permute-done.9
  67.7 0.1 fusion.5
  67.8 1.8 %collective-permute-start.10 = (bf16[64,768]{1,0:T(8,128)(2,1)S(1)}, bf16[64,768]{1,0:T(8,128)(2,1)S(1)}, u32[]{:S(2)}, u32[]{:S(2)}) collective-permute-start(bf16[64,768]{1,0:T(8,128)(2,1)S(1)} %get-tuple-element.31), channel_id=1, source_target_pairs={{0,4},{4,0},{8,12},{12,8},{1,5},{5,1},{9,13},{13,9},{2,6},{6,2},{1... | collective-permute-start | bytes 294920 | tf_op jit(solution)/shard_map/ppermute | solution.py:17
  69.6 1.6 %collective-permute-start.12 = (bf16[64,768]{1,0:T(8,128)(2,1)S(1)}, bf16[64,768]{1,0:T(8,128)(2,1)S(1)}, u32[]{:S(2)}, u32[]{:S(2)}) collective-permute-start(bf16[64,768]{1,0:T(8,128)(2,1)S(1)} %get-tuple-element.32), channel_id=1, source_target_pairs={{0,12},{4,8},{8,4},{12,0},{1,13},{5,9},{9,5},{13,1},{2,14},{6,10},... | collective-permute-start | bytes 294920 | tf_op jit(solution)/shard_map/ppermute | solution.py:17
  71.2 0.2 collective-permute-start.11
  71.4 2.0 %collective-permute-done.16 = bf16[64,768]{1,0:T(8,128)(2,1)S(1)} collective-permute-done((bf16[64,768]{1,0:T(8,128)(2,1)S(1)}, bf16[64,768]{1,0:T(8,128)(2,1)S(1)}, u32[]{:S(2)}, u32[]{:S(2)}) %collective-permute-start.16) | collective-permute-done | bytes 98336 | tf_op jit(solution)/shard_map/ppermute | solution.py:17
  73.4 0.0 collective-permute-done.17
  73.4 0.0 collective-permute-done.10
  73.4 1.8 %collective-permute-done.12 = bf16[64,768]{1,0:T(8,128)(2,1)S(1)} collective-permute-done((bf16[64,768]{1,0:T(8,128)(2,1)S(1)}, bf16[64,768]{1,0:T(8,128)(2,1)S(1)}, u32[]{:S(2)}, u32[]{:S(2)}) %collective-permute-start.12) | collective-permute-done | bytes 98336 | tf_op jit(solution)/shard_map/ppermute | solution.py:17
  75.2 1.0 %collective-permute-done.11 = bf16[64,768]{1,0:T(8,128)(2,1)S(1)} collective-permute-done((bf16[64,768]{1,0:T(8,128)(2,1)S(1)}, bf16[64,768]{1,0:T(8,128)(2,1)S(1)}, u32[]{:S(2)}, u32[]{:S(2)}) %collective-permute-start.11) | collective-permute-done | bytes 98336 | tf_op jit(solution)/shard_map/ppermute | solution.py:17
  76.2 0.7 fusion.4
  (3 shorter events, 0.1 us)
Async XLA Ops:
  0.0 7.4 %collective-permute-start.2 = (bf16[64,768]{1,0:T(8,128)(2,1)}, bf16[64,768]{1,0:T(8,128)(2,1)S(1)}, u32[]{:S(2)}, u32[]{:S(2)}) collective-permute-start(bf16[64,768]{1,0:T(8,128)(2,1)} %refs_0_.1), channel_id=1, source_target_pairs={{0,12},{4,8},{8,4},{12,0},{1,13},{5,9},{9,5},{13,1},{2,14},{6,10},... | collective-permute-start | bytes 294920 | tf_op jit(solution)/shard_map/ppermute | solution.py:17
  3.9 5.1 %collective-permute-start.1 = (bf16[64,768]{1,0:T(8,128)(2,1)}, bf16[64,768]{1,0:T(8,128)(2,1)S(1)}, u32[]{:S(2)}, u32[]{:S(2)}) collective-permute-start(bf16[64,768]{1,0:T(8,128)(2,1)} %refs_0_.1), channel_id=1, source_target_pairs={{0,8},{4,12},{8,0},{12,4},{1,9},{5,13},{9,1},{13,5},{2,10},{6,14},... | collective-permute-start | bytes 294920 | tf_op jit(solution)/shard_map/ppermute | solution.py:17
  4.4 4.9 %collective-permute-start = (bf16[64,768]{1,0:T(8,128)(2,1)}, bf16[64,768]{1,0:T(8,128)(2,1)S(1)}, u32[]{:S(2)}, u32[]{:S(2)}) collective-permute-start(bf16[64,768]{1,0:T(8,128)(2,1)} %refs_0_.1), channel_id=1, source_target_pairs={{0,4},{4,0},{8,12},{12,8},{1,5},{5,1},{9,13},{13,9},{2,6},{6,2},{1... | collective-permute-start | bytes 294920 | tf_op jit(solution)/shard_map/ppermute | solution.py:17
  10.3 26.6 %collective-permute-start.3 = (bf16[256,768]{1,0:T(8,128)(2,1)S(1)}, bf16[256,768]{1,0:T(8,128)(2,1)S(1)}, u32[]{:S(2)}, u32[]{:S(2)}) collective-permute-start(bf16[256,768]{1,0:T(8,128)(2,1)S(1)} %shard_map.55.refs_0_), channel_id=1, source_target_pairs={{0,1},{1,0},{2,3},{3,2},{4,5},{5,4},{6,7},{7,6},{8,9},{9,8},{10,11... | collective-permute-start | bytes 1179656 | tf_op jit(solution)/shard_map/ppermute | solution.py:17
  11.9 14.2 %collective-permute-start.5 = (bf16[64,768]{1,0:T(8,128)(2,1)}, bf16[64,768]{1,0:T(8,128)(2,1)S(1)}, u32[]{:S(2)}, u32[]{:S(2)}) collective-permute-start(bf16[64,768]{1,0:T(8,128)(2,1)} %refs_0_.1), channel_id=1, source_target_pairs={{0,3},{1,2},{2,1},{3,0},{4,7},{5,6},{6,5},{7,4},{8,11},{9,10},{10,... | collective-permute-start | bytes 294920 | tf_op jit(solution)/shard_map/ppermute | solution.py:17
  14.4 11.7 %collective-permute-start.4 = (bf16[64,768]{1,0:T(8,128)(2,1)}, bf16[64,768]{1,0:T(8,128)(2,1)S(1)}, u32[]{:S(2)}, u32[]{:S(2)}) collective-permute-start(bf16[64,768]{1,0:T(8,128)(2,1)} %refs_0_.1), channel_id=1, source_target_pairs={{0,2},{1,3},{2,0},{3,1},{4,6},{5,7},{6,4},{7,5},{8,10},{9,11},{10,... | collective-permute-start | bytes 294920 | tf_op jit(solution)/shard_map/ppermute | solution.py:17
  26.1 10.5 %collective-permute-start.8 = (bf16[64,1664]{1,0:T(8,128)(2,1)S(1)}, bf16[64,1664]{1,0:T(8,128)(2,1)S(1)}, u32[]{:S(2)}, u32[]{:S(2)}) collective-permute-start(bf16[64,1664]{1,0:T(8,128)(2,1)S(1)} %shard_map.57.after.refs_2_), channel_id=1, source_target_pairs={{0,12},{4,8},{8,4},{12,0},{1,13},{5,9},{9,5},{13,1},{2,14},{6,10},... | collective-permute-start | bytes 638984 | tf_op jit(solution)/shard_map/ppermute | solution.py:17
  27.2 9.5 %collective-permute-start.7 = (bf16[64,1664]{1,0:T(8,128)(2,1)S(1)}, bf16[64,1664]{1,0:T(8,128)(2,1)S(1)}, u32[]{:S(2)}, u32[]{:S(2)}) collective-permute-start(bf16[64,1664]{1,0:T(8,128)(2,1)S(1)} %shard_map.57.after.refs_2_), channel_id=1, source_target_pairs={{0,8},{4,12},{8,0},{12,4},{1,9},{5,13},{9,1},{13,5},{2,10},{6,14},... | collective-permute-start | bytes 638984 | tf_op jit(solution)/shard_map/ppermute | solution.py:17
  29.4 7.5 %collective-permute-start.6 = (bf16[64,1664]{1,0:T(8,128)(2,1)S(1)}, bf16[64,1664]{1,0:T(8,128)(2,1)S(1)}, u32[]{:S(2)}, u32[]{:S(2)}) collective-permute-start(bf16[64,1664]{1,0:T(8,128)(2,1)S(1)} %shard_map.57.after.refs_2_), channel_id=1, source_target_pairs={{0,4},{4,0},{8,12},{12,8},{1,5},{5,1},{9,13},{13,9},{2,6},{6,2},{1... | collective-permute-start | bytes 638984 | tf_op jit(solution)/shard_map/ppermute | solution.py:17
  50.5 13.3 %collective-permute-start.13 = (bf16[64,1536]{1,0:T(8,128)(2,1)S(1)}, bf16[64,1536]{1,0:T(8,128)(2,1)S(1)}, u32[]{:S(2)}, u32[]{:S(2)}) collective-permute-start(bf16[64,1536]{1,0:T(8,128)(2,1)S(1)} %get-tuple-element.26), channel_id=1, source_target_pairs={{0,4},{4,0},{8,12},{12,8},{1,5},{5,1},{9,13},{13,9},{2,6},{6,2},{1... | collective-permute-start | bytes 589832 | tf_op jit(solution)/shard_map/ppermute | solution.py:17
  52.1 11.7 %collective-permute-start.14 = (bf16[64,1536]{1,0:T(8,128)(2,1)S(1)}, bf16[64,1536]{1,0:T(8,128)(2,1)S(1)}, u32[]{:S(2)}, u32[]{:S(2)}) collective-permute-start(bf16[64,1536]{1,0:T(8,128)(2,1)S(1)} %get-tuple-element.27), channel_id=1, source_target_pairs={{0,8},{4,12},{8,0},{12,4},{1,9},{5,13},{9,1},{13,5},{2,10},{6,14},... | collective-permute-start | bytes 589832 | tf_op jit(solution)/shard_map/ppermute | solution.py:17
  52.5 11.3 %collective-permute-start.15 = (bf16[64,1536]{1,0:T(8,128)(2,1)S(1)}, bf16[64,1536]{1,0:T(8,128)(2,1)S(1)}, u32[]{:S(2)}, u32[]{:S(2)}) collective-permute-start(bf16[64,1536]{1,0:T(8,128)(2,1)S(1)} %get-tuple-element.28), channel_id=1, source_target_pairs={{0,12},{4,8},{8,4},{12,0},{1,13},{5,9},{9,5},{13,1},{2,14},{6,10},... | collective-permute-start | bytes 589832 | tf_op jit(solution)/shard_map/ppermute | solution.py:17
  55.9 11.8 %collective-permute-start.9 = (bf16[256,768]{1,0:T(8,128)(2,1)S(1)}, bf16[256,768]{1,0:T(8,128)(2,1)S(1)}, u32[]{:S(2)}, u32[]{:S(2)}) collective-permute-start(bf16[256,768]{1,0:T(8,128)(2,1)S(1)} %shard_map.61), channel_id=1, source_target_pairs={{0,1},{1,0},{2,3},{3,2},{4,5},{5,4},{6,7},{7,6},{8,9},{9,8},{10,11... | collective-permute-start | bytes 1179656 | tf_op jit(solution)/shard_map/ppermute | solution.py:17
  64.0 9.4 %collective-permute-start.16 = (bf16[64,768]{1,0:T(8,128)(2,1)S(1)}, bf16[64,768]{1,0:T(8,128)(2,1)S(1)}, u32[]{:S(2)}, u32[]{:S(2)}) collective-permute-start(bf16[64,768]{1,0:T(8,128)(2,1)S(1)} %get-tuple-element.34), channel_id=1, source_target_pairs={{0,2},{1,3},{2,0},{3,1},{4,6},{5,7},{6,4},{7,5},{8,10},{9,11},{10,... | collective-permute-start | bytes 294920 | tf_op jit(solution)/shard_map/ppermute | solution.py:17
  65.2 8.3 %collective-permute-start.17 = (bf16[64,768]{1,0:T(8,128)(2,1)S(1)}, bf16[64,768]{1,0:T(8,128)(2,1)S(1)}, u32[]{:S(2)}, u32[]{:S(2)}) collective-permute-start(bf16[64,768]{1,0:T(8,128)(2,1)S(1)} %get-tuple-element.35), channel_id=1, source_target_pairs={{0,3},{1,2},{2,1},{3,0},{4,7},{5,6},{6,5},{7,4},{8,11},{9,10},{10,... | collective-permute-start | bytes 294920 | tf_op jit(solution)/shard_map/ppermute | solution.py:17
  67.8 5.6 %collective-permute-start.10 = (bf16[64,768]{1,0:T(8,128)(2,1)S(1)}, bf16[64,768]{1,0:T(8,128)(2,1)S(1)}, u32[]{:S(2)}, u32[]{:S(2)}) collective-permute-start(bf16[64,768]{1,0:T(8,128)(2,1)S(1)} %get-tuple-element.31), channel_id=1, source_target_pairs={{0,4},{4,0},{8,12},{12,8},{1,5},{5,1},{9,13},{13,9},{2,6},{6,2},{1... | collective-permute-start | bytes 294920 | tf_op jit(solution)/shard_map/ppermute | solution.py:17
  69.6 5.6 %collective-permute-start.12 = (bf16[64,768]{1,0:T(8,128)(2,1)S(1)}, bf16[64,768]{1,0:T(8,128)(2,1)S(1)}, u32[]{:S(2)}, u32[]{:S(2)}) collective-permute-start(bf16[64,768]{1,0:T(8,128)(2,1)S(1)} %get-tuple-element.32), channel_id=1, source_target_pairs={{0,12},{4,8},{8,4},{12,0},{1,13},{5,9},{9,5},{13,1},{2,14},{6,10},... | collective-permute-start | bytes 294920 | tf_op jit(solution)/shard_map/ppermute | solution.py:17
  71.2 5.0 %collective-permute-start.11 = (bf16[64,768]{1,0:T(8,128)(2,1)S(1)}, bf16[64,768]{1,0:T(8,128)(2,1)S(1)}, u32[]{:S(2)}, u32[]{:S(2)}) collective-permute-start(bf16[64,768]{1,0:T(8,128)(2,1)S(1)} %get-tuple-element.33), channel_id=1, source_target_pairs={{0,8},{4,12},{8,0},{12,4},{1,9},{5,13},{9,1},{13,5},{2,10},{6,14},... | collective-permute-start | bytes 294920 | tf_op jit(solution)/shard_map/ppermute | solution.py:17

commit v9 on v8

--- a/solution.py
+++ b/solution.py
@@ -247,10 +247,13 @@
     ]
     for copy in copies:
         copy.start()
+    half = n_loc // 2 * rows
     for e, copy in enumerate(copies):
         copy.wait()
         down_rows(hidden, buf[e], row_w, slice(e * rows, (e + 1) * rows), high)
-    out[...] = combine(pick_t, high).astype(out.dtype)
+        if e + 1 == n_loc // 2:
+            out[...] = combine(pick_t.at[:, :half], high.at[:half])
+    out[...] += combine(pick_t.at[:, half:], high.at[half:])
 
 
 def down_scratch(n_loc, rows, ff, slice_d, deep):

time: 77.1 us -> 77.1 us (level)
  no operation moved by 1% of the time
where the time goes in v9:
time: 77.1 us; the launch traced here: 76.9 us
  Pallas kernels  32.7 us (42%)
  starting transfers between devices  25.8 us (33%)
  waiting for transfers between devices  17.2 us (22%)
  other arithmetic  0.99 us (1%)
    pallas_call x7, Pallas kernels, call(): pl.pallas_call(body, in_specs=[pl.BlockSpec(memory_space=space) for _, sp...  32.7 us
    ppermute x18, starting transfers between devices, hop(): return lax.ppermute(value, axis, [(i, i ^ k) for i in range(n)])  25.8 us
    ppermute x18, waiting for transfers between devices, hop(): return lax.ppermute(value, axis, [(i, i ^ k) for i in range(n)])  17.2 us
  transfers between devices with their start and end apart: 18, of which 8 were waited for; matrix products, arithmetic and copies ran while one was open for 0% of the time, Pallas kernels for 24%

profile of v9, /device:TPU:0, one launch (start us, length us, event | category | flops | bytes accessed | tf_op | source)
XLA Modules:
  0.0 76.9 jit_solution(2348665814129593483)
XLA Ops:
  0.0 3.9 %collective-permute-start.2 = (bf16[64,768]{1,0:T(8,128)(2,1)}, bf16[64,768]{1,0:T(8,128)(2,1)S(1)}, u32[]{:S(2)}, u32[]{:S(2)}) collective-permute-start(bf16[64,768]{1,0:T(8,128)(2,1)} %refs_0_.1), channel_id=1, source_target_pairs={{0,12},{4,8},{8,4},{12,0},{1,13},{5,9},{9,5},{13,1},{2,14},{6,10},... | collective-permute-start | bytes 294920 | tf_op jit(solution)/shard_map/ppermute | solution.py:17
  3.9 0.5 collective-permute-start.1
  4.4 0.1 collective-permute-start
  4.5 2.9 %collective-permute-done.2.refs_3_ = bf16[64,768]{1,0:T(8,128)(2,1)S(1)} collective-permute-done((bf16[64,768]{1,0:T(8,128)(2,1)}, bf16[64,768]{1,0:T(8,128)(2,1)S(1)}, u32[]{:S(2)}, u32[]{:S(2)}) %collective-permute-start.2) | collective-permute-done | bytes 98336 | tf_op jit(solution)/shard_map/ppermute | solution.py:17
  7.4 1.6 %collective-permute-done.1.refs_2_ = bf16[64,768]{1,0:T(8,128)(2,1)S(1)} collective-permute-done((bf16[64,768]{1,0:T(8,128)(2,1)}, bf16[64,768]{1,0:T(8,128)(2,1)S(1)}, u32[]{:S(2)}, u32[]{:S(2)}) %collective-permute-start.1) | collective-permute-done | bytes 98336 | tf_op jit(solution)/shard_map/ppermute | solution.py:17
  9.0 0.3 collective-permute-done.refs_1_
  9.4 0.9 %shard_map.55.refs_0_ = bf16[256,768]{1,0:T(8,128)(2,1)S(1)} custom-call(bf16[64,768]{1,0:T(8,128)(2,1)} %refs_0_.1, bf16[64,768]{1,0:T(8,128)(2,1)S(1)} %collective-permute-done.refs_1_, bf16[64,768]{1,0:T(8,128)(2,1)S(1)} %collective-permute-done.1.refs_2_, bf16[64,768]{1,0:T(8,128)(2,1)S(1)} %collective-permute-done.2.refs_3_), custom_call_target="tpu_custom_call" | custom-call | tf_op jit(solution)/shard_map/pallas_call | solution.py:25
  10.3 1.6 %collective-permute-start.3 = (bf16[256,768]{1,0:T(8,128)(2,1)S(1)}, bf16[256,768]{1,0:T(8,128)(2,1)S(1)}, u32[]{:S(2)}, u32[]{:S(2)}) collective-permute-start(bf16[256,768]{1,0:T(8,128)(2,1)S(1)} %shard_map.55.refs_0_), channel_id=1, source_target_pairs={{0,1},{1,0},{2,3},{3,2},{4,5},{5,4},{6,7},{7,6},{8,9},{9,8},{10,11... | collective-permute-start | bytes 1179656 | tf_op jit(solution)/shard_map/ppermute | solution.py:17
  11.9 2.5 %collective-permute-start.5 = (bf16[64,768]{1,0:T(8,128)(2,1)}, bf16[64,768]{1,0:T(8,128)(2,1)S(1)}, u32[]{:S(2)}, u32[]{:S(2)}) collective-permute-start(bf16[64,768]{1,0:T(8,128)(2,1)} %refs_0_.1), channel_id=1, source_target_pairs={{0,3},{1,2},{2,1},{3,0},{4,7},{5,6},{6,5},{7,4},{8,11},{9,10},{10,... | collective-permute-start | bytes 294920 | tf_op jit(solution)/shard_map/ppermute | solution.py:17
  14.4 0.1 collective-permute-start.4
  14.5 0.1 pad_add_fusion.place
  14.6 4.3 %shard_map.56 = (bf16[64,128]{1,0:T(8,128)(2,1)S(1)}, bf16[3072,1536]{1,0:T(8,128)(2,1)S(1)}) custom-call(s32[2]{0:T(128)S(1)} %pad_add_fusion.place, s32[4,64]{1,0:T(4,128)} %bitcast.4, f32[4,64]{1,0:T(4,128)} %bitcast.5, bf16[4,3072,1536]{2,1,0:T(8,128)(2,1)} %refs_9_.1), custom_call_target="tpu_custom_call" | custom-call | tf_op jit(solution)/shard_map/pallas_call | solution.py:25
  18.9 7.2 %collective-permute-done.5.refs_1_ = bf16[64,768]{1,0:T(8,128)(2,1)S(1)} collective-permute-done((bf16[64,768]{1,0:T(8,128)(2,1)}, bf16[64,768]{1,0:T(8,128)(2,1)S(1)}, u32[]{:S(2)}, u32[]{:S(2)}) %collective-permute-start.5) | collective-permute-done | bytes 98336 | tf_op jit(solution)/shard_map/ppermute | solution.py:17
  26.1 0.0 collective-permute-done.4.refs_0_
  26.1 1.0 %collective-permute-start.8 = (bf16[64,1664]{1,0:T(8,128)(2,1)S(1)}, bf16[64,1664]{1,0:T(8,128)(2,1)S(1)}, u32[]{:S(2)}, u32[]{:S(2)}) collective-permute-start(bf16[64,1664]{1,0:T(8,128)(2,1)S(1)} %shard_map.57.after.refs_2_), channel_id=1, source_target_pairs={{0,12},{4,8},{8,4},{12,0},{1,13},{5,9},{9,5},{13,1},{2,14},{6,10},... | collective-permute-start | bytes 638984 | tf_op jit(solution)/shard_map/ppermute | solution.py:17
  27.2 2.2 %collective-permute-start.7 = (bf16[64,1664]{1,0:T(8,128)(2,1)S(1)}, bf16[64,1664]{1,0:T(8,128)(2,1)S(1)}, u32[]{:S(2)}, u32[]{:S(2)}) collective-permute-start(bf16[64,1664]{1,0:T(8,128)(2,1)S(1)} %shard_map.57.after.refs_2_), channel_id=1, source_target_pairs={{0,8},{4,12},{8,0},{12,4},{1,9},{5,13},{9,1},{13,5},{2,10},{6,14},... | collective-permute-start | bytes 638984 | tf_op jit(solution)/shard_map/ppermute | solution.py:17
  29.4 0.3 collective-permute-start.6
  29.7 6.9 %shard_map.58 = (bf16[3072,1536]{1,0:T(8,128)(2,1)S(1)}, bf16[3072,1536]{1,0:T(8,128)(2,1)S(1)}) custom-call(bf16[4,3072,1536]{2,1,0:T(8,128)(2,1)} %refs_9_.1, bf16[64,1664]{1,0:T(8,128)(2,1)S(1)} %shard_map.57.after.refs_2_, s32[2]{0:T(128)S(1)} %pad_add_fusion.place), custom_call_target="tpu_custom_call" | custom-call | bytes 18874368 | tf_op jit(solution)/shard_map/pallas_call | solution.py:25
  36.6 0.0 collective-permute-done.8.refs_5_
  36.6 0.0 collective-permute-done.7.refs_4_
  36.7 0.2 collective-permute-done.6.refs_3_
  36.8 0.0 collective-permute-done.3.refs_1_
  36.8 13.6 %shard_map.59 = (bf16[64,1536]{1,0:T(8,128)(2,1)S(1)}, bf16[64,1536]{1,0:T(8,128)(2,1)S(1)}, bf16[64,1536]{1,0:T(8,128)(2,1)S(1)}, bf16[64,1536]{1,0:T(8,128)(2,...) custom-call(s32[2]{0:T(128)S(1)} %pad_add_fusion.place, ...), custom_call_target="tpu_custom_call", output_to_operand_aliasing={{7}: (7, {}), {8}: (8, {}), {9}: (9, {})} | custom-call | flops 9663676416 | bytes 37748736 | tf_op jit(solution)/shard_map/pallas_call | solution.py:25
  50.5 1.6 %collective-permute-start.13 = (bf16[64,1536]{1,0:T(8,128)(2,1)S(1)}, bf16[64,1536]{1,0:T(8,128)(2,1)S(1)}, u32[]{:S(2)}, u32[]{:S(2)}) collective-permute-start(bf16[64,1536]{1,0:T(8,128)(2,1)S(1)} %get-tuple-element.26), channel_id=1, source_target_pairs={{0,4},{4,0},{8,12},{12,8},{1,5},{5,1},{9,13},{13,9},{2,6},{6,2},{1... | collective-permute-start | bytes 589832 | tf_op jit(solution)/shard_map/ppermute | solution.py:17
  52.1 0.4 collective-permute-start.14
  52.5 1.5 %collective-permute-start.15 = (bf16[64,1536]{1,0:T(8,128)(2,1)S(1)}, bf16[64,1536]{1,0:T(8,128)(2,1)S(1)}, u32[]{:S(2)}, u32[]{:S(2)}) collective-permute-start(bf16[64,1536]{1,0:T(8,128)(2,1)S(1)} %get-tuple-element.28), channel_id=1, source_target_pairs={{0,12},{4,8},{8,4},{12,0},{1,13},{5,9},{9,5},{13,1},{2,14},{6,10},... | collective-permute-start | bytes 589832 | tf_op jit(solution)/shard_map/ppermute | solution.py:17
  54.0 1.8 %shard_map.61 = bf16[256,768]{1,0:T(8,128)(2,1)S(1)} custom-call(bf16[384,1536]{1,0:T(8,128)(2,1)S(1)} %get-tuple-element.21.hidden, bf16[256,384]{1,0:T(8,128)(2,1)S(1)} %get-tuple-element.22.pick_t, f32[384,1]{1,0:T(8,128)S(1)} %get-tuple-element.23.row_w, bf16[3072,1536]{1,0:T(8,128)(2,1)S(1)} %get-tuple-element.24.weights), custom_call_target="tpu_custom_call" | custom-call | flops 2415919104 | tf_op jit(solution)/shard_map/pallas_call | solution.py:25
  55.9 2.7 %collective-permute-start.9 = (bf16[256,768]{1,0:T(8,128)(2,1)S(1)}, bf16[256,768]{1,0:T(8,128)(2,1)S(1)}, u32[]{:S(2)}, u32[]{:S(2)}) collective-permute-start(bf16[256,768]{1,0:T(8,128)(2,1)S(1)} %shard_map.61), channel_id=1, source_target_pairs={{0,1},{1,0},{2,3},{3,2},{4,5},{5,4},{6,7},{7,6},{8,9},{9,8},{10,11... | collective-permute-start | bytes 1179656 | tf_op jit(solution)/shard_map/ppermute | solution.py:17
  58.6 5.1 %shard_map.60 = f32[256,768]{1,0:T(8,128)S(1)} custom-call(s32[2]{0:T(128)S(1)} %pad_add_fusion.place, bf16[384,1536]{1,0:T(8,128)(2,1)S(1)} %get-tuple-element.21.hidden, bf16[256,384]{1,0:T(8,128)(2,1)S(1)} %get-tuple-element.22.pick_t, f32[384,1]{1,0:T(8,128)S(1)} %get-tuple-element.23.row_w, bf16[4,1536,3072]{2,1,0:T(8,128)(2,1)} %w_down.1), custom_call_target="tpu_custom_call" | custom-call | flops 2415919104 | bytes 9437184 | tf_op jit(solution)/shard_map/pallas_call | solution.py:25
  63.8 0.0 collective-permute-done.13
  63.8 0.0 collective-permute-done.14
  63.8 0.0 collective-permute-done.15
  63.8 0.1 add_convert_fusion
  63.9 1.2 %collective-permute-start.16 = (bf16[64,768]{1,0:T(8,128)(2,1)S(1)}, bf16[64,768]{1,0:T(8,128)(2,1)S(1)}, u32[]{:S(2)}, u32[]{:S(2)}) collective-permute-start(bf16[64,768]{1,0:T(8,128)(2,1)S(1)} %get-tuple-element.34), channel_id=1, source_target_pairs={{0,2},{1,3},{2,0},{3,1},{4,6},{5,7},{6,4},{7,5},{8,10},{9,11},{10,... | collective-permute-start | bytes 294920 | tf_op jit(solution)/shard_map/ppermute | solution.py:17
  65.2 2.5 %collective-permute-start.17 = (bf16[64,768]{1,0:T(8,128)(2,1)S(1)}, bf16[64,768]{1,0:T(8,128)(2,1)S(1)}, u32[]{:S(2)}, u32[]{:S(2)}) collective-permute-start(bf16[64,768]{1,0:T(8,128)(2,1)S(1)} %get-tuple-element.35), channel_id=1, source_target_pairs={{0,3},{1,2},{2,1},{3,0},{4,7},{5,6},{6,5},{7,4},{8,11},{9,10},{10,... | collective-permute-start | bytes 294920 | tf_op jit(solution)/shard_map/ppermute | solution.py:17
  67.6 0.0 collective-permute-done.9
  67.7 0.1 fusion.5
  67.8 1.8 %collective-permute-start.10 = (bf16[64,768]{1,0:T(8,128)(2,1)S(1)}, bf16[64,768]{1,0:T(8,128)(2,1)S(1)}, u32[]{:S(2)}, u32[]{:S(2)}) collective-permute-start(bf16[64,768]{1,0:T(8,128)(2,1)S(1)} %get-tuple-element.31), channel_id=1, source_target_pairs={{0,4},{4,0},{8,12},{12,8},{1,5},{5,1},{9,13},{13,9},{2,6},{6,2},{1... | collective-permute-start | bytes 294920 | tf_op jit(solution)/shard_map/ppermute | solution.py:17
  69.6 1.6 %collective-permute-start.12 = (bf16[64,768]{1,0:T(8,128)(2,1)S(1)}, bf16[64,768]{1,0:T(8,128)(2,1)S(1)}, u32[]{:S(2)}, u32[]{:S(2)}) collective-permute-start(bf16[64,768]{1,0:T(8,128)(2,1)S(1)} %get-tuple-element.32), channel_id=1, source_target_pairs={{0,12},{4,8},{8,4},{12,0},{1,13},{5,9},{9,5},{13,1},{2,14},{6,10},... | collective-permute-start | bytes 294920 | tf_op jit(solution)/shard_map/ppermute | solution.py:17
  71.2 0.2 collective-permute-start.11
  71.4 2.0 %collective-permute-done.16 = bf16[64,768]{1,0:T(8,128)(2,1)S(1)} collective-permute-done((bf16[64,768]{1,0:T(8,128)(2,1)S(1)}, bf16[64,768]{1,0:T(8,128)(2,1)S(1)}, u32[]{:S(2)}, u32[]{:S(2)}) %collective-permute-start.16) | collective-permute-done | bytes 98336 | tf_op jit(solution)/shard_map/ppermute | solution.py:17
  73.3 0.0 collective-permute-done.17
  73.3 0.0 collective-permute-done.10
  73.4 1.8 %collective-permute-done.12 = bf16[64,768]{1,0:T(8,128)(2,1)S(1)} collective-permute-done((bf16[64,768]{1,0:T(8,128)(2,1)S(1)}, bf16[64,768]{1,0:T(8,128)(2,1)S(1)}, u32[]{:S(2)}, u32[]{:S(2)}) %collective-permute-start.12) | collective-permute-done | bytes 98336 | tf_op jit(solution)/shard_map/ppermute | solution.py:17
  75.2 1.0 %collective-permute-done.11 = bf16[64,768]{1,0:T(8,128)(2,1)S(1)} collective-permute-done((bf16[64,768]{1,0:T(8,128)(2,1)S(1)}, bf16[64,768]{1,0:T(8,128)(2,1)S(1)}, u32[]{:S(2)}, u32[]{:S(2)}) %collective-permute-start.11) | collective-permute-done | bytes 98336 | tf_op jit(solution)/shard_map/ppermute | solution.py:17
  76.2 0.7 fusion.4
  (3 shorter events, 0.1 us)
Async XLA Ops:
  0.0 7.4 %collective-permute-start.2 = (bf16[64,768]{1,0:T(8,128)(2,1)}, bf16[64,768]{1,0:T(8,128)(2,1)S(1)}, u32[]{:S(2)}, u32[]{:S(2)}) collective-permute-start(bf16[64,768]{1,0:T(8,128)(2,1)} %refs_0_.1), channel_id=1, source_target_pairs={{0,12},{4,8},{8,4},{12,0},{1,13},{5,9},{9,5},{13,1},{2,14},{6,10},... | collective-permute-start | bytes 294920 | tf_op jit(solution)/shard_map/ppermute | solution.py:17
  3.9 5.1 %collective-permute-start.1 = (bf16[64,768]{1,0:T(8,128)(2,1)}, bf16[64,768]{1,0:T(8,128)(2,1)S(1)}, u32[]{:S(2)}, u32[]{:S(2)}) collective-permute-start(bf16[64,768]{1,0:T(8,128)(2,1)} %refs_0_.1), channel_id=1, source_target_pairs={{0,8},{4,12},{8,0},{12,4},{1,9},{5,13},{9,1},{13,5},{2,10},{6,14},... | collective-permute-start | bytes 294920 | tf_op jit(solution)/shard_map/ppermute | solution.py:17
  4.4 4.9 %collective-permute-start = (bf16[64,768]{1,0:T(8,128)(2,1)}, bf16[64,768]{1,0:T(8,128)(2,1)S(1)}, u32[]{:S(2)}, u32[]{:S(2)}) collective-permute-start(bf16[64,768]{1,0:T(8,128)(2,1)} %refs_0_.1), channel_id=1, source_target_pairs={{0,4},{4,0},{8,12},{12,8},{1,5},{5,1},{9,13},{13,9},{2,6},{6,2},{1... | collective-permute-start | bytes 294920 | tf_op jit(solution)/shard_map/ppermute | solution.py:17
  10.3 26.6 %collective-permute-start.3 = (bf16[256,768]{1,0:T(8,128)(2,1)S(1)}, bf16[256,768]{1,0:T(8,128)(2,1)S(1)}, u32[]{:S(2)}, u32[]{:S(2)}) collective-permute-start(bf16[256,768]{1,0:T(8,128)(2,1)S(1)} %shard_map.55.refs_0_), channel_id=1, source_target_pairs={{0,1},{1,0},{2,3},{3,2},{4,5},{5,4},{6,7},{7,6},{8,9},{9,8},{10,11... | collective-permute-start | bytes 1179656 | tf_op jit(solution)/shard_map/ppermute | solution.py:17
  11.9 14.2 %collective-permute-start.5 = (bf16[64,768]{1,0:T(8,128)(2,1)}, bf16[64,768]{1,0:T(8,128)(2,1)S(1)}, u32[]{:S(2)}, u32[]{:S(2)}) collective-permute-start(bf16[64,768]{1,0:T(8,128)(2,1)} %refs_0_.1), channel_id=1, source_target_pairs={{0,3},{1,2},{2,1},{3,0},{4,7},{5,6},{6,5},{7,4},{8,11},{9,10},{10,... | collective-permute-start | bytes 294920 | tf_op jit(solution)/shard_map/ppermute | solution.py:17
  14.4 11.7 %collective-permute-start.4 = (bf16[64,768]{1,0:T(8,128)(2,1)}, bf16[64,768]{1,0:T(8,128)(2,1)S(1)}, u32[]{:S(2)}, u32[]{:S(2)}) collective-permute-start(bf16[64,768]{1,0:T(8,128)(2,1)} %refs_0_.1), channel_id=1, source_target_pairs={{0,2},{1,3},{2,0},{3,1},{4,6},{5,7},{6,4},{7,5},{8,10},{9,11},{10,... | collective-permute-start | bytes 294920 | tf_op jit(solution)/shard_map/ppermute | solution.py:17
  26.1 10.5 %collective-permute-start.8 = (bf16[64,1664]{1,0:T(8,128)(2,1)S(1)}, bf16[64,1664]{1,0:T(8,128)(2,1)S(1)}, u32[]{:S(2)}, u32[]{:S(2)}) collective-permute-start(bf16[64,1664]{1,0:T(8,128)(2,1)S(1)} %shard_map.57.after.refs_2_), channel_id=1, source_target_pairs={{0,12},{4,8},{8,4},{12,0},{1,13},{5,9},{9,5},{13,1},{2,14},{6,10},... | collective-permute-start | bytes 638984 | tf_op jit(solution)/shard_map/ppermute | solution.py:17
  27.2 9.5 %collective-permute-start.7 = (bf16[64,1664]{1,0:T(8,128)(2,1)S(1)}, bf16[64,1664]{1,0:T(8,128)(2,1)S(1)}, u32[]{:S(2)}, u32[]{:S(2)}) collective-permute-start(bf16[64,1664]{1,0:T(8,128)(2,1)S(1)} %shard_map.57.after.refs_2_), channel_id=1, source_target_pairs={{0,8},{4,12},{8,0},{12,4},{1,9},{5,13},{9,1},{13,5},{2,10},{6,14},... | collective-permute-start | bytes 638984 | tf_op jit(solution)/shard_map/ppermute | solution.py:17
  29.4 7.5 %collective-permute-start.6 = (bf16[64,1664]{1,0:T(8,128)(2,1)S(1)}, bf16[64,1664]{1,0:T(8,128)(2,1)S(1)}, u32[]{:S(2)}, u32[]{:S(2)}) collective-permute-start(bf16[64,1664]{1,0:T(8,128)(2,1)S(1)} %shard_map.57.after.refs_2_), channel_id=1, source_target_pairs={{0,4},{4,0},{8,12},{12,8},{1,5},{5,1},{9,13},{13,9},{2,6},{6,2},{1... | collective-permute-start | bytes 638984 | tf_op jit(solution)/shard_map/ppermute | solution.py:17
  50.5 13.3 %collective-permute-start.13 = (bf16[64,1536]{1,0:T(8,128)(2,1)S(1)}, bf16[64,1536]{1,0:T(8,128)(2,1)S(1)}, u32[]{:S(2)}, u32[]{:S(2)}) collective-permute-start(bf16[64,1536]{1,0:T(8,128)(2,1)S(1)} %get-tuple-element.26), channel_id=1, source_target_pairs={{0,4},{4,0},{8,12},{12,8},{1,5},{5,1},{9,13},{13,9},{2,6},{6,2},{1... | collective-permute-start | bytes 589832 | tf_op jit(solution)/shard_map/ppermute | solution.py:17
  52.1 11.7 %collective-permute-start.14 = (bf16[64,1536]{1,0:T(8,128)(2,1)S(1)}, bf16[64,1536]{1,0:T(8,128)(2,1)S(1)}, u32[]{:S(2)}, u32[]{:S(2)}) collective-permute-start(bf16[64,1536]{1,0:T(8,128)(2,1)S(1)} %get-tuple-element.27), channel_id=1, source_target_pairs={{0,8},{4,12},{8,0},{12,4},{1,9},{5,13},{9,1},{13,5},{2,10},{6,14},... | collective-permute-start | bytes 589832 | tf_op jit(solution)/shard_map/ppermute | solution.py:17
  52.5 11.3 %collective-permute-start.15 = (bf16[64,1536]{1,0:T(8,128)(2,1)S(1)}, bf16[64,1536]{1,0:T(8,128)(2,1)S(1)}, u32[]{:S(2)}, u32[]{:S(2)}) collective-permute-start(bf16[64,1536]{1,0:T(8,128)(2,1)S(1)} %get-tuple-element.28), channel_id=1, source_target_pairs={{0,12},{4,8},{8,4},{12,0},{1,13},{5,9},{9,5},{13,1},{2,14},{6,10},... | collective-permute-start | bytes 589832 | tf_op jit(solution)/shard_map/ppermute | solution.py:17
  55.9 11.8 %collective-permute-start.9 = (bf16[256,768]{1,0:T(8,128)(2,1)S(1)}, bf16[256,768]{1,0:T(8,128)(2,1)S(1)}, u32[]{:S(2)}, u32[]{:S(2)}) collective-permute-start(bf16[256,768]{1,0:T(8,128)(2,1)S(1)} %shard_map.61), channel_id=1, source_target_pairs={{0,1},{1,0},{2,3},{3,2},{4,5},{5,4},{6,7},{7,6},{8,9},{9,8},{10,11... | collective-permute-start | bytes 1179656 | tf_op jit(solution)/shard_map/ppermute | solution.py:17
  63.9 9.4 %collective-permute-start.16 = (bf16[64,768]{1,0:T(8,128)(2,1)S(1)}, bf16[64,768]{1,0:T(8,128)(2,1)S(1)}, u32[]{:S(2)}, u32[]{:S(2)}) collective-permute-start(bf16[64,768]{1,0:T(8,128)(2,1)S(1)} %get-tuple-element.34), channel_id=1, source_target_pairs={{0,2},{1,3},{2,0},{3,1},{4,6},{5,7},{6,4},{7,5},{8,10},{9,11},{10,... | collective-permute-start | bytes 294920 | tf_op jit(solution)/shard_map/ppermute | solution.py:17
  65.2 8.2 %collective-permute-start.17 = (bf16[64,768]{1,0:T(8,128)(2,1)S(1)}, bf16[64,768]{1,0:T(8,128)(2,1)S(1)}, u32[]{:S(2)}, u32[]{:S(2)}) collective-permute-start(bf16[64,768]{1,0:T(8,128)(2,1)S(1)} %get-tuple-element.35), channel_id=1, source_target_pairs={{0,3},{1,2},{2,1},{3,0},{4,7},{5,6},{6,5},{7,4},{8,11},{9,10},{10,... | collective-permute-start | bytes 294920 | tf_op jit(solution)/shard_map/ppermute | solution.py:17
  67.8 5.5 %collective-permute-start.10 = (bf16[64,768]{1,0:T(8,128)(2,1)S(1)}, bf16[64,768]{1,0:T(8,128)(2,1)S(1)}, u32[]{:S(2)}, u32[]{:S(2)}) collective-permute-start(bf16[64,768]{1,0:T(8,128)(2,1)S(1)} %get-tuple-element.31), channel_id=1, source_target_pairs={{0,4},{4,0},{8,12},{12,8},{1,5},{5,1},{9,13},{13,9},{2,6},{6,2},{1... | collective-permute-start | bytes 294920 | tf_op jit(solution)/shard_map/ppermute | solution.py:17
  69.6 5.6 %collective-permute-start.12 = (bf16[64,768]{1,0:T(8,128)(2,1)S(1)}, bf16[64,768]{1,0:T(8,128)(2,1)S(1)}, u32[]{:S(2)}, u32[]{:S(2)}) collective-permute-start(bf16[64,768]{1,0:T(8,128)(2,1)S(1)} %get-tuple-element.32), channel_id=1, source_target_pairs={{0,12},{4,8},{8,4},{12,0},{1,13},{5,9},{9,5},{13,1},{2,14},{6,10},... | collective-permute-start | bytes 294920 | tf_op jit(solution)/shard_map/ppermute | solution.py:17
  71.2 5.0 %collective-permute-start.11 = (bf16[64,768]{1,0:T(8,128)(2,1)S(1)}, bf16[64,768]{1,0:T(8,128)(2,1)S(1)}, u32[]{:S(2)}, u32[]{:S(2)}) collective-permute-start(bf16[64,768]{1,0:T(8,128)(2,1)S(1)} %get-tuple-element.33), channel_id=1, source_target_pairs={{0,8},{4,12},{8,0},{12,4},{1,9},{5,13},{9,1},{13,5},{2,10},{6,14},... | collective-permute-start | bytes 294920 | tf_op jit(solution)/shard_map/ppermute | solution.py:17
